TPU v7x, 256 devices: a whole 4x4x8 slice. The times are simulated.
256 devices in a mesh: grp: 4 (over y), seq: 64 (over z, x, core).
Axes of the slice: x: 4, y: 4, z: 8, core: 2. Of those that a mesh axis runs over, the one named last changes fastest.
Arguments:
- queries: bfloat16 [8192, 64, 192], P('seq', 'grp'), may hold values from -6 to 6
- key_cache: bfloat16 [4, 65536, 192], P('grp', 'seq'), may hold values from -6 to 6
- group_value_cache: bfloat16 [4, 65536, 128], P('grp', 'seq'), may hold values from -6 to 6
- coarse_keys: bfloat16 [4, 4096, 192], P('grp', 'seq'), may hold values from -6 to 6
- coarse_values: bfloat16 [4, 4096, 128], P('grp', 'seq'), may hold values from -6 to 6
- hidden: bfloat16 [8192, 2560], P('seq'), may hold values from -6 to 6
- gate_weight: bfloat16 [4, 2560, 32], P('grp'), may hold values from -0.125 to 0.125
- out_weight: bfloat16 [8192, 2560], P('grp'), may hold values from -0.09375 to 0.09375
- selected: int32 [4, 64, 16], P('grp', 'seq'), may hold values from 0 to 1023, as said below
Outputs:
- layer_out: bfloat16 [8192, 2560], P('seq', 'grp')
Inputs may be any that keep to these rules, and one draw needn't show every extreme that they name: selected[g, t] lists 16 distinct blocks of 64 positions for tile t of group g; the first is block 0; none starts after the tile's last query position; at most 1 of them lie within one index of seq's 1024 positions.
All inputs are finite; a program needn't handle non-finite values.
Results may differ from a plain program's by a relative error of at most 0.013.
Values may be sent and summed in bfloat16 or wider, within the bound.
No kernel may reach another device: no remote copies, remote signals or barrier semaphores. Data moves between devices by JAX's collectives and lax.ppermute only.
A program may use at most 128 MiB of HBM per device.

v0:
```python
import math

import jax
import jax.numpy as jnp
from jax import lax
from jax.sharding import PartitionSpec as P

BLK = 64
SEL = 16
TILE = 128
CSTRIDE = 16
CLEN = 32


NEGATIVE = -1e30


def copy_for_each(x, axis):
    peers = lax.axis_size(axis)
    return lax.all_to_all(jnp.broadcast_to(x[None], (peers, *x.shape)), axis, 0, 0, tiled=True)


def in_order(tiles, dim):
    tiles = jnp.moveaxis(tiles, 0, dim)
    lengths = tiles.shape
    return tiles.reshape(*lengths[:dim], lengths[dim] * lengths[dim + 1], *lengths[dim + 2 :])


def collect(x, axis, dim):
    tiles = copy_for_each(x, axis)
    return in_order(tiles, dim)


def sent_together(arrays, axis, dim, along):
    ends, at = ([], 0)
    for a in arrays[:-1]:
        at += a.shape[along]
        ends.append(at)
    both = jnp.concatenate(arrays, axis=along)
    return tuple(jnp.split(lax.all_gather(both, axis, axis=dim, tiled=True), ends, axis=along))


def cut_along(x, dim, peers):
    before, after = (x.shape[:dim], x.shape[dim + 1 :])
    return jnp.moveaxis(x.reshape(*before, peers, -1, *after), dim, 0)


def sent_and_summed(x, axis, dim):
    peers = lax.axis_size(axis)
    tiles = lax.all_to_all(cut_along(x, dim, peers), axis, 0, 0, tiled=True)
    return jnp.sum(tiles.astype(jnp.float32), axis=0)


def online_block(folded, part_keys, part_values, query_rows, row_pos, key_pos, score_scale):
    running, row_total, summed_out = folded
    logit_scores = (
        lax.dot_general(
            query_rows, part_keys, (((1,), (1,)), ((), ())), preferred_element_type=jnp.float32
        )
        * score_scale
    )
    logit_scores = jnp.where(key_pos[None, :] <= row_pos[:, None], logit_scores, -jnp.inf)
    new_max = jnp.maximum(running, jnp.max(logit_scores, axis=1))
    factor = jnp.exp(running - new_max)
    weights = jnp.exp(logit_scores - new_max[:, None])
    row_total = row_total * factor + jnp.sum(weights, axis=1)
    summed_out = summed_out * factor[:, None] + jnp.dot(
        weights.astype(jnp.bfloat16), part_values, preferred_element_type=jnp.float32
    )
    return (new_max, row_total, summed_out)


def shards(
    queries,
    key_cache,
    group_value_cache,
    coarse_keys,
    coarse_values,
    hidden,
    gate_weight,
    out_weight,
    selected,
):
    seq_count = lax.axis_size("seq")
    seq_index = lax.axis_index("seq")
    ctx_dev = key_cache.shape[1]
    context = ctx_dev * seq_count
    heads_here = queries.shape[1]
    key_width = queries.shape[2]
    value_width = group_value_cache.shape[2]
    score_scale = key_width ** (-0.5)
    query_rows = queries.reshape(TILE * heads_here, key_width)
    query_pos = context - TILE * seq_count + seq_index * TILE + jnp.arange(TILE, dtype=jnp.int32)
    row_pos = jnp.repeat(query_pos, heads_here)
    row_count = TILE * heads_here
    fold_start = (
        jnp.full((row_count,), NEGATIVE, jnp.float32),
        jnp.zeros((row_count,), jnp.float32),
        jnp.zeros((row_count, value_width), jnp.float32),
    )
    requests = collect(selected[0], "seq", 0)
    blocks_dev = ctx_dev // BLK
    slot_cap = max(1, 2 * SEL // seq_count)
    owners = requests // blocks_dev
    earlier = jnp.tril(jnp.ones((SEL, SEL), jnp.int32), -1)
    same_owner = (owners[:, :, None] == owners[:, None, :]).astype(jnp.int32)
    order_rank = jnp.sum(same_owner * earlier[None], axis=2)
    served = owners == seq_index
    slot_ids = jnp.arange(slot_cap, dtype=jnp.int32)
    matches = (served[:, :, None] & (order_rank[:, :, None] == slot_ids[None, None, :])).astype(
        jnp.int32
    )
    local_block = jnp.sum(matches * (requests - seq_index * blocks_dev)[:, :, None], axis=1)
    filled = jnp.sum(matches, axis=1) > 0
    block_keys_grouped = key_cache[0].reshape(blocks_dev, BLK, key_width)
    value_blocks = group_value_cache[0].reshape(blocks_dev, BLK, value_width)
    outgoing = jnp.concatenate(
        [
            jnp.take(block_keys_grouped, local_block, axis=0),
            jnp.take(value_blocks, local_block, axis=0),
        ],
        axis=3,
    )
    outgoing = jnp.where(filled[:, :, None, None], outgoing, jnp.zeros_like(outgoing))
    incoming = lax.all_to_all(outgoing, "seq", split_axis=0, concat_axis=0, tiled=True)
    gathered = sent_together((coarse_keys[0], coarse_values[0]), "seq", 0, 1)
    piece_keys, piece_values = gathered
    length = piece_keys.shape[0]
    span_rows = math.gcd(length, 512)

    def advance(loop_index, state_now):
        offset = loop_index * span_rows
        part_keys = lax.dynamic_slice_in_dim(piece_keys, offset, span_rows, 0)
        part_values = lax.dynamic_slice_in_dim(piece_values, offset, span_rows, 0)
        key_pos = (offset + jnp.arange(span_rows, dtype=jnp.int32)) * CSTRIDE + CLEN - 1
        return online_block(
            state_now, part_keys, part_values, query_rows, row_pos, key_pos, score_scale
        )

    coarse_state = lax.fori_loop(0, length // span_rows, advance, fold_start)
    coarse_out = coarse_state[2] / coarse_state[1][:, None]
    own_list = selected[0, 0]
    own_owner = own_list // blocks_dev
    own_rank = jnp.sum(
        (own_owner[:, None] == own_owner[None, :]).astype(jnp.int32) * earlier, axis=1
    )
    picked_rows = incoming[own_owner, own_rank].reshape(SEL * BLK, key_width + value_width)
    picked_keys = picked_rows[:, :key_width]
    picked_values = picked_rows[:, key_width:]
    picked_pos = (own_list[:, None] * BLK + jnp.arange(BLK, dtype=jnp.int32)[None, :]).reshape(-1)
    picked_state = online_block(
        fold_start, picked_keys, picked_values, query_rows, row_pos, picked_pos, score_scale
    )
    picked_out = picked_state[2] / picked_state[1][:, None]
    gate_logits = jnp.dot(hidden, gate_weight[0], preferred_element_type=jnp.float32)
    gate_coarse = jax.nn.sigmoid(gate_logits[:, :heads_here])
    gate_picked = jax.nn.sigmoid(gate_logits[:, heads_here:])
    mixed_heads = gate_coarse[:, :, None] * coarse_out.reshape(
        TILE, heads_here, value_width
    ) + gate_picked[:, :, None] * picked_out.reshape(TILE, heads_here, value_width)
    attended = mixed_heads.astype(jnp.bfloat16).reshape(TILE, heads_here * value_width)
    partial_value = jnp.dot(attended, out_weight, preferred_element_type=jnp.float32)
    result = sent_and_summed(partial_value.astype(jnp.bfloat16), "grp", 1)
    return result.astype(jnp.bfloat16)


def solution(mesh):
    return jax.shard_map(
        shards,
        mesh=mesh,
        in_specs=(
            P("seq", "grp", None),
            P("grp", "seq", None),
            P("grp", "seq", None),
            P("grp", "seq", None),
            P("grp", "seq", None),
            P("seq", None),
            P("grp", None, None),
            P("grp", None),
            P("grp", "seq", None),
        ),
        out_specs=P("seq", "grp"),
        check_vma=False,
    )
```

profile of v0, /device:TPU:1, one launch (start us, length us, event | category | flops | bytes accessed | tf_op | source)
XLA Modules:
  0.0 221.0 jit_solution(5985491464048930562)
XLA Ops:
  9.4 13.0 %all-to-all-start = ((s32[64,1,16]{2,1,0:T(1,128)}), s32[64,1,16]{2,1,0:T(1,128)S(1)}, u32[]{:S(2)}, u32[]{:S(2)}) async-start(s32[64,1,16]{2,1,0:T(1,128)} %broadcast_in_dim.104), calls=%async_computation | async-start | bytes 65536 | tf_op jit(solution)/shard_map/all_to_all | solution.py:20
  26.7 2.7 %copy.32 = bf16[128,16,192]{2,1,0:T(8,128)(2,1)} copy(bf16[128,16,192]{0,2,1:T(8,128)(2,1)} %param.11) | data formatting | bytes 1572864 | tf_op args[0]
  29.6 2.1 all-to-all-done
  32.2 2.1 gather_fusion
  37.1 3.3 %fusion.17 = bf16[64,1,64,320]{3,2,1,0:T(8,128)(2,1)} fusion(bf16[64,1,64,128]{3,2,0,1:T(8,128)(2,1)S(1)} %select_bitcast_fusion.1, bf16[64,1,64,192]{3,2,0,1:T(8,128)(2,1)S(1)} %select_bitcast_fusion, pred[64]{0:T(512)(128)(4,1)S(1)} %get-tuple-element.328), kind=kLoop, calls=%fused_computation.29 | loop fusion | flops 6553600 | bytes 5242944 | tf_op jit(solution)/shard_map/jit(_where)/select_n | solution.py:124
  40.4 8.4 %all-to-all-start.1 = ((bf16[64,1,64,320]{3,2,1,0:T(8,128)(2,1)}), bf16[64,1,64,320]{3,2,1,0:T(8,128)(2,1)}, u32[]{:S(2)}, u32[]{:S(2)}) async-start(bf16[64,1,64,320]{3,2,1,0:T(8,128)(2,1)} %fusion.17), calls=%async_computation.1 | async-start | bytes 6291456 | tf_op jit(solution)/shard_map/all_to_all | solution.py:125
  48.8 53.7 %all-gather.2.cloned.1.call-done = bf16[4096,320]{1,0:T(8,128)(2,1)} async-done(((bf16[64,320]{1,0:T(8,128)(2,1)}), bf16[4096,320]{1,0:T(8,128)(2,1)}) %all-gather.2.cloned.1.call-update) | async-done | bytes 2621456 | tf_op jit(solution)/shard_map/all_gather | solution.py:40
  102.5 3.0 %split.8 = bf16[4096,192]{1,0:T(8,128)(2,1)} slice(bf16[4096,320]{1,0:T(8,128)(2,1)} %all-gather.2.cloned.1.call-done), slice={[0:4096], [0:192]} | slice | bytes 3145728 | tf_op jit(solution)/shard_map/split | solution.py:40
  105.5 2.0 split.9
  107.5 71.0 %while.22 = (s32[]{:T(128)}, f32[2048]{0:T(1024)S(1)}, f32[2048]{0:T(1024)S(1)}, f32[2048,128]{1,0:T(8,128)S(1)}, bf16[4096,192]{1,0:T(8,128)(2,1)}, /*index=5*/...) while((s32[]{:T(128)}, f32[2048]{0:T(1024)S(1)}, ...), condition=%wide.region_3.4_spmd.clone, body=%wide.region_0.3_spmd.clone.sunk | while | flops 680275456 | bytes 33067732 | solution.py:140
  107.7 4.0 %fusion.72 = (f32[2048]{0:T(1024)S(1)}, f32[2048,512]{0,1:T(8,128)}) fusion(bf16[2048,192]{1,0:T(8,128)(2,1)} %get-tuple-element.415, bf16[4096,192]{1,0:T(8,128)(2,1)} %get-tuple-element.414, s32[]{:T(128)S(6)} %select_n.248, s32[2048]{0:T(1024)S(1)} %le.142, s32[512]{0:T(512)S(1)} %multiply_add_fusion.2), kind=kOutput, calls=%fused_computation.118.clone.1 | convolution fusion | flops 406845440 | bytes 5523460 | tf_op jit(solution)/shard_map/while/body/eval_jaxpr/dot_general | solution.py:57
  111.7 2.9 %fusion.73 = f32[2048]{0:T(1024)S(1)} fusion(f32[2048,512]{0,1:T(8,128)} %get-tuple-element.383, f32[2048]{0:T(1024)S(1)} %select_maximum_fusion.2), kind=kLoop, calls=%fused_computation.7.clone.1 | loop fusion | flops 2095104 | bytes 4210688 | tf_op jit(solution)/shard_map/while/body/eval_jaxpr/reduce_sum | solution.py:66
  116.5 4.0 %fusion.72 = (f32[2048]{0:T(1024)S(1)}, f32[2048,512]{0,1:T(8,128)}) fusion(bf16[2048,192]{1,0:T(8,128)(2,1)} %get-tuple-element.415, bf16[4096,192]{1,0:T(8,128)(2,1)} %get-tuple-element.414, s32[]{:T(128)S(6)} %select_n.248, s32[2048]{0:T(1024)S(1)} %le.142, s32[512]{0:T(512)S(1)} %multiply_add_fusion.2), kind=kOutput, calls=%fused_computation.118.clone.1 | convolution fusion | flops 406845440 | bytes 5523460 | tf_op jit(solution)/shard_map/while/body/eval_jaxpr/dot_general | solution.py:57
  120.6 2.9 %fusion.73 = f32[2048]{0:T(1024)S(1)} fusion(f32[2048,512]{0,1:T(8,128)} %get-tuple-element.383, f32[2048]{0:T(1024)S(1)} %select_maximum_fusion.2), kind=kLoop, calls=%fused_computation.7.clone.1 | loop fusion | flops 2095104 | bytes 4210688 | tf_op jit(solution)/shard_map/while/body/eval_jaxpr/reduce_sum | solution.py:66
  125.4 4.0 %fusion.72 = (f32[2048]{0:T(1024)S(1)}, f32[2048,512]{0,1:T(8,128)}) fusion(bf16[2048,192]{1,0:T(8,128)(2,1)} %get-tuple-element.415, bf16[4096,192]{1,0:T(8,128)(2,1)} %get-tuple-element.414, s32[]{:T(128)S(6)} %select_n.248, s32[2048]{0:T(1024)S(1)} %le.142, s32[512]{0:T(512)S(1)} %multiply_add_fusion.2), kind=kOutput, calls=%fused_computation.118.clone.1 | convolution fusion | flops 406845440 | bytes 5523460 | tf_op jit(solution)/shard_map/while/body/eval_jaxpr/dot_general | solution.py:57
  129.5 2.9 %fusion.73 = f32[2048]{0:T(1024)S(1)} fusion(f32[2048,512]{0,1:T(8,128)} %get-tuple-element.383, f32[2048]{0:T(1024)S(1)} %select_maximum_fusion.2), kind=kLoop, calls=%fused_computation.7.clone.1 | loop fusion | flops 2095104 | bytes 4210688 | tf_op jit(solution)/shard_map/while/body/eval_jaxpr/reduce_sum | solution.py:66
  134.3 4.0 %fusion.72 = (f32[2048]{0:T(1024)S(1)}, f32[2048,512]{0,1:T(8,128)}) fusion(bf16[2048,192]{1,0:T(8,128)(2,1)} %get-tuple-element.415, bf16[4096,192]{1,0:T(8,128)(2,1)} %get-tuple-element.414, s32[]{:T(128)S(6)} %select_n.248, s32[2048]{0:T(1024)S(1)} %le.142, s32[512]{0:T(512)S(1)} %multiply_add_fusion.2), kind=kOutput, calls=%fused_computation.118.clone.1 | convolution fusion | flops 406845440 | bytes 5523460 | tf_op jit(solution)/shard_map/while/body/eval_jaxpr/dot_general | solution.py:57
  138.3 2.9 %fusion.73 = f32[2048]{0:T(1024)S(1)} fusion(f32[2048,512]{0,1:T(8,128)} %get-tuple-element.383, f32[2048]{0:T(1024)S(1)} %select_maximum_fusion.2), kind=kLoop, calls=%fused_computation.7.clone.1 | loop fusion | flops 2095104 | bytes 4210688 | tf_op jit(solution)/shard_map/while/body/eval_jaxpr/reduce_sum | solution.py:66
  143.2 4.0 %fusion.72 = (f32[2048]{0:T(1024)S(1)}, f32[2048,512]{0,1:T(8,128)}) fusion(bf16[2048,192]{1,0:T(8,128)(2,1)} %get-tuple-element.415, bf16[4096,192]{1,0:T(8,128)(2,1)} %get-tuple-element.414, s32[]{:T(128)S(6)} %select_n.248, s32[2048]{0:T(1024)S(1)} %le.142, s32[512]{0:T(512)S(1)} %multiply_add_fusion.2), kind=kOutput, calls=%fused_computation.118.clone.1 | convolution fusion | flops 406845440 | bytes 5523460 | tf_op jit(solution)/shard_map/while/body/eval_jaxpr/dot_general | solution.py:57
  147.2 2.9 %fusion.73 = f32[2048]{0:T(1024)S(1)} fusion(f32[2048,512]{0,1:T(8,128)} %get-tuple-element.383, f32[2048]{0:T(1024)S(1)} %select_maximum_fusion.2), kind=kLoop, calls=%fused_computation.7.clone.1 | loop fusion | flops 2095104 | bytes 4210688 | tf_op jit(solution)/shard_map/while/body/eval_jaxpr/reduce_sum | solution.py:66
  152.1 4.0 %fusion.72 = (f32[2048]{0:T(1024)S(1)}, f32[2048,512]{0,1:T(8,128)}) fusion(bf16[2048,192]{1,0:T(8,128)(2,1)} %get-tuple-element.415, bf16[4096,192]{1,0:T(8,128)(2,1)} %get-tuple-element.414, s32[]{:T(128)S(6)} %select_n.248, s32[2048]{0:T(1024)S(1)} %le.142, s32[512]{0:T(512)S(1)} %multiply_add_fusion.2), kind=kOutput, calls=%fused_computation.118.clone.1 | convolution fusion | flops 406845440 | bytes 5523460 | tf_op jit(solution)/shard_map/while/body/eval_jaxpr/dot_general | solution.py:57
  156.1 2.9 %fusion.73 = f32[2048]{0:T(1024)S(1)} fusion(f32[2048,512]{0,1:T(8,128)} %get-tuple-element.383, f32[2048]{0:T(1024)S(1)} %select_maximum_fusion.2), kind=kLoop, calls=%fused_computation.7.clone.1 | loop fusion | flops 2095104 | bytes 4210688 | tf_op jit(solution)/shard_map/while/body/eval_jaxpr/reduce_sum | solution.py:66
  160.9 4.0 %fusion.72 = (f32[2048]{0:T(1024)S(1)}, f32[2048,512]{0,1:T(8,128)}) fusion(bf16[2048,192]{1,0:T(8,128)(2,1)} %get-tuple-element.415, bf16[4096,192]{1,0:T(8,128)(2,1)} %get-tuple-element.414, s32[]{:T(128)S(6)} %select_n.248, s32[2048]{0:T(1024)S(1)} %le.142, s32[512]{0:T(512)S(1)} %multiply_add_fusion.2), kind=kOutput, calls=%fused_computation.118.clone.1 | convolution fusion | flops 406845440 | bytes 5523460 | tf_op jit(solution)/shard_map/while/body/eval_jaxpr/dot_general | solution.py:57
  165.0 2.9 %fusion.73 = f32[2048]{0:T(1024)S(1)} fusion(f32[2048,512]{0,1:T(8,128)} %get-tuple-element.383, f32[2048]{0:T(1024)S(1)} %select_maximum_fusion.2), kind=kLoop, calls=%fused_computation.7.clone.1 | loop fusion | flops 2095104 | bytes 4210688 | tf_op jit(solution)/shard_map/while/body/eval_jaxpr/reduce_sum | solution.py:66
  169.8 4.0 %fusion.72 = (f32[2048]{0:T(1024)S(1)}, f32[2048,512]{0,1:T(8,128)}) fusion(bf16[2048,192]{1,0:T(8,128)(2,1)} %get-tuple-element.415, bf16[4096,192]{1,0:T(8,128)(2,1)} %get-tuple-element.414, s32[]{:T(128)S(6)} %select_n.248, s32[2048]{0:T(1024)S(1)} %le.142, s32[512]{0:T(512)S(1)} %multiply_add_fusion.2), kind=kOutput, calls=%fused_computation.118.clone.1 | convolution fusion | flops 406845440 | bytes 5523460 | tf_op jit(solution)/shard_map/while/body/eval_jaxpr/dot_general | solution.py:57
  173.9 2.9 %fusion.73 = f32[2048]{0:T(1024)S(1)} fusion(f32[2048,512]{0,1:T(8,128)} %get-tuple-element.383, f32[2048]{0:T(1024)S(1)} %select_maximum_fusion.2), kind=kLoop, calls=%fused_computation.7.clone.1 | loop fusion | flops 2095104 | bytes 4210688 | tf_op jit(solution)/shard_map/while/body/eval_jaxpr/reduce_sum | solution.py:66
  179.0 2.6 %gather_fusion.2 = bf16[16,64,320]{2,1,0:T(8,128)(2,1)S(1)} fusion(bf16[64,1,64,320]{3,2,1,0:T(8,128)(2,1)} %all-to-all-done.1, s32[16]{0:T(128)S(1)} %fusion.54), kind=kCustom, calls=%fused_computation.2 | custom fusion | bytes 1310848 | tf_op jit(solution)/shard_map/gather | solution.py:147
  181.7 2.6 %fusion.13 = (f32[2048]{0:T(1024)S(1)}, f32[1024,2048]{1,0:T(8,128)S(1)}) fusion(s32[2048]{0:T(1024)S(1)} %le.97, s32[1024]{0:T(1024)S(1)} %add.264, bf16[2048,192]{1,0:T(8,128)(2,1)} %get-tuple-element.426, bf16[1024,320]{1,0:T(8,128)(2,1)S(1)} %bitcast.131), kind=kOutput, calls=%fused_computation.24 | convolution fusion | flops 813692928 | bytes 9719808 | tf_op jit(solution)/shard_map/dot_general | solution.py:57
  184.3 2.6 %fusion.11 = f32[2048]{0:T(1024)S(1)} fusion(f32[1024,2048]{1,0:T(8,128)S(1)} %get-tuple-element.326, f32[2048]{0:T(1024)S(1)} %broadcast_maximum_fusion, s32[2048]{0:T(1024)S(1)} %le.97, s32[1024]{0:T(1024)S(1)} %add.264), kind=kLoop, calls=%fused_computation.22 | loop fusion | flops 10483712 | bytes 8417280 | tf_op jit(solution)/shard_map/reduce_sum | solution.py:66
  186.9 3.6 %fusion.21 = f32[2048,128]{1,0:T(8,128)} fusion(f32[1024,2048]{1,0:T(8,128)S(1)} %get-tuple-element.326, f32[2048]{0:T(1024)S(1)} %broadcast_maximum_fusion, s32[2048]{0:T(1024)S(1)} %le.97, s32[1024]{0:T(1024)S(1)} %add.264, f32[2048]{0:T(1024)S(1)} %get-tuple-element.320, f32[2048]{0:T(1024)S(1)} %get-tuple-element.319, bf16[1024,320]{1,0:T(8,128)(2,1)S(1)} %bitcast.132), kind=kOutput, calls=%fused_computation.32 | convolution fusion | flops 547880960 | bytes 9736192 | tf_op jit(solution)/shard_map/dot_general | solution.py:67
  192.6 6.3 %convolution_convert_fusion = bf16[128,2560]{1,0:T(8,128)(2,1)S(1)} fusion(bf16[2048,2560]{1,0:T(8,128)(2,1)} %param.18, f32[128,2048]{1,0:T(8,128)S(1)} %reshape.431, f32[16,8,16,128]{3,2,1,0:T(8,128)S(1)} %bitcast.126, f32[128,2048]{1,0:T(8,128)S(1)} %reshape.427, f32[16,8,16,128]{3,2,1,0:T(8,128)S(1)} %bitcast.125), kind=kOutput, calls=%fused_computation.27 | convolution fusion | flops 1343553536 | bytes 15335424 | tf_op jit(solution)/shard_map/dot_general | solution.py:162
  198.9 14.5 %all_to_all.15 = bf16[4,128,640]{2,1,0:T(8,128)(2,1)S(1)} all-to-all(bf16[4,128,640]{2,1,0:T(8,128)(2,1)S(1)} %bitcast.129), channel_id=1, replica_groups=mesh['grp'=4,'seq'=64] {'grp'}, dimensions={0} | all-to-all | bytes 1310720 | tf_op jit(solution)/shard_map/all_to_all | solution.py:50
  (119 shorter events, 28.9 us)
Async XLA Ops:
  6.5 17.5 %copy-start = (bf16[128,2560]{1,0:T(8,128)(2,1)S(1)}, bf16[128,2560]{1,0:T(8,128)(2,1)}, u32[]{:S(2)}) copy-start(bf16[128,2560]{1,0:T(8,128)(2,1)} %param.16) | copy-start | bytes 1966084
  6.5 95.9 %all-gather.2.cloned.1.call-start = ((), (), s32[]{:S(2)}) async-start(), calls=%async_computation.3 | async-start | bytes 3194880 | tf_op jit(solution)/shard_map/all_gather | solution.py:40
  9.4 22.4 %all-to-all-start = ((s32[64,1,16]{2,1,0:T(1,128)}), s32[64,1,16]{2,1,0:T(1,128)S(1)}, u32[]{:S(2)}, u32[]{:S(2)}) async-start(s32[64,1,16]{2,1,0:T(1,128)} %broadcast_in_dim.104), calls=%async_computation | async-start | bytes 65536 | tf_op jit(solution)/shard_map/all_to_all | solution.py:20
  23.1 11.2 %copy-start.2 = (bf16[1,1024,128]{2,1,0:T(8,128)(2,1)S(1)}, bf16[1,1024,128]{2,1,0:T(8,128)(2,1)}, u32[]{:S(2)}) copy-start(bf16[1,1024,128]{2,1,0:T(8,128)(2,1)} %param.13) | copy-start | bytes 786436
  40.4 138.7 %all-to-all-start.1 = ((bf16[64,1,64,320]{3,2,1,0:T(8,128)(2,1)}), bf16[64,1,64,320]{3,2,1,0:T(8,128)(2,1)}, u32[]{:S(2)}, u32[]{:S(2)}) async-start(bf16[64,1,64,320]{3,2,1,0:T(8,128)(2,1)} %fusion.17), calls=%async_computation.1 | async-start | bytes 6291456 | tf_op jit(solution)/shard_map/all_to_all | solution.py:125
  111.7 3.4 %copy-start.1 = (f32[2048,512]{0,1:T(8,128)S(1)}, f32[2048,512]{0,1:T(8,128)}, u32[]{:S(2)}) copy-start(f32[2048,512]{0,1:T(8,128)} %get-tuple-element.383) | copy-start | bytes 12582916 | tf_op jit(solution)/shard_map/while
  120.6 3.4 %copy-start.1 = (f32[2048,512]{0,1:T(8,128)S(1)}, f32[2048,512]{0,1:T(8,128)}, u32[]{:S(2)}) copy-start(f32[2048,512]{0,1:T(8,128)} %get-tuple-element.383) | copy-start | bytes 12582916 | tf_op jit(solution)/shard_map/while
  129.5 3.4 %copy-start.1 = (f32[2048,512]{0,1:T(8,128)S(1)}, f32[2048,512]{0,1:T(8,128)}, u32[]{:S(2)}) copy-start(f32[2048,512]{0,1:T(8,128)} %get-tuple-element.383) | copy-start | bytes 12582916 | tf_op jit(solution)/shard_map/while
  138.3 3.4 %copy-start.1 = (f32[2048,512]{0,1:T(8,128)S(1)}, f32[2048,512]{0,1:T(8,128)}, u32[]{:S(2)}) copy-start(f32[2048,512]{0,1:T(8,128)} %get-tuple-element.383) | copy-start | bytes 12582916 | tf_op jit(solution)/shard_map/while
  147.2 3.4 %copy-start.1 = (f32[2048,512]{0,1:T(8,128)S(1)}, f32[2048,512]{0,1:T(8,128)}, u32[]{:S(2)}) copy-start(f32[2048,512]{0,1:T(8,128)} %get-tuple-element.383) | copy-start | bytes 12582916 | tf_op jit(solution)/shard_map/while
  156.1 3.4 %copy-start.1 = (f32[2048,512]{0,1:T(8,128)S(1)}, f32[2048,512]{0,1:T(8,128)}, u32[]{:S(2)}) copy-start(f32[2048,512]{0,1:T(8,128)} %get-tuple-element.383) | copy-start | bytes 12582916 | tf_op jit(solution)/shard_map/while
  165.0 3.4 %copy-start.1 = (f32[2048,512]{0,1:T(8,128)S(1)}, f32[2048,512]{0,1:T(8,128)}, u32[]{:S(2)}) copy-start(f32[2048,512]{0,1:T(8,128)} %get-tuple-element.383) | copy-start | bytes 12582916 | tf_op jit(solution)/shard_map/while
  173.9 3.4 %copy-start.1 = (f32[2048,512]{0,1:T(8,128)S(1)}, f32[2048,512]{0,1:T(8,128)}, u32[]{:S(2)}) copy-start(f32[2048,512]{0,1:T(8,128)} %get-tuple-element.383) | copy-start | bytes 12582916 | tf_op jit(solution)/shard_map/while
Sparse Core Ops, SparseCore 0:
  10.1 92.2 all-gather.1
where the time goes:
time: 222 us; the launch traced here: 221 us
  waiting for transfers between devices  55.8 us (25%)
  matrix products  55.5 us (25%)
  other arithmetic  36.2 us (16%)
  local copies, waits for them, and re-layouts  23.7 us (11%)
  starting transfers between devices  21.4 us (10%)
  blocking collectives  14.5 us (7%)
  between operations  13.6 us (6%)
    all_gather x1, waiting for transfers between devices, sent_together(): lax.all_gather(both, axis, axis=dim, tiled=True)  53.7 us
    dot_general x9, matrix products, online_block(): lax.dot_general(query_rows, part_keys, (((1,), (1,)), ((), ())), preferre...  34.9 us
    reduce_sum x9, other arithmetic, online_block(): row_total = row_total * factor + jnp.sum(weights, axis=1)  26.1 us
    all_to_all x1, blocking collectives, sent_and_summed(): tiles = lax.all_to_all(cut_along(x, dim, peers), axis, 0, 0, tiled=True)  14.5 us
    dot_general x9, matrix products, online_block(): jnp.dot(weights.astype(jnp.bfloat16), part_values, preferred_element_type...  13.1 us
    all_to_all x1, starting transfers between devices, copy_for_each(): lax.all_to_all(jnp.broadcast_to(x[None], (peers, *x.shape)), axis, 0, 0,...  13 us
    all_to_all x1, starting transfers between devices, shards(): lax.all_to_all(outgoing, 'seq', split_axis=0, concat_axis=0, tiled=True)  8.36 us
    dot_general x1, matrix products, shards(): jnp.dot(attended, out_weight, preferred_element_type=jnp.float32)  6.32 us
  transfers between devices with their start and end apart: 3, of which 2 were waited for; matrix products, arithmetic and copies ran while one was open for 40% of the time, Pallas kernels for 0%

commit v1 on v0

v1 whole, which is shorter than its diff:
```python
import functools
import math

import jax
import jax.numpy as jnp
from jax import lax
from jax.experimental import pallas as pl
from jax.experimental.pallas import tpu as pltpu
from jax.sharding import PartitionSpec as P

BLK = 64
SEL = 16
TILE = 128
CSTRIDE = 16
CLEN = 32
DQK = 192
DV = 128
PACK = BLK + BLK + BLK // 2
NEGATIVE = -1e30
EXP_SCALE = DQK**-0.5 * math.log2(math.e)
Z, X, C = 8, 4, 2


def packed_blocks(keys, values):
    high = jnp.concatenate([keys[:, : BLK // 2, DV:], keys[:, BLK // 2 :, DV:]], axis=2)
    return jnp.concatenate([keys[:, :, :DV], values, high], axis=1)


def unpacked_keys(block):
    high = jnp.concatenate([block[2 * BLK :, :BLK], block[2 * BLK :, BLK:]], axis=0)
    return jnp.concatenate([block[:BLK], high], axis=1)


def copies_for(x, groups):
    peers = len(groups[0])
    return lax.all_to_all(
        jnp.broadcast_to(x[None], (peers, *x.shape)), "seq", 0, 0, axis_index_groups=groups, tiled=True
    )


def everywhere(block):
    along_z = [[(z * X + x) * C + c for z in range(Z)] for x in range(X) for c in range(C)]
    along_x = [[(z * X + x) * C + c for x in range(X)] for z in range(Z) for c in range(C)]
    along_c = [[(z * X + x) * C + c for c in range(C)] for z in range(Z) for x in range(X)]
    block = copies_for(block, along_z)
    block = copies_for(block, along_x)
    return copies_for(block, along_c).reshape(C * X * Z, PACK, DV)


def payload_kernel(wanted_ref, blocks_ref, out_ref):
    def one(t, carry):
        out_ref[t] = blocks_ref[wanted_ref[t]]
        return carry

    lax.fori_loop(0, out_ref.shape[0], one, 0, unroll=8)


def payload(wanted, blocks):
    tiles = wanted.shape[0]
    whole = lambda shape: pl.BlockSpec(shape, lambda i, w: (0, 0, 0))
    return pl.pallas_call(
        payload_kernel,
        grid_spec=pltpu.PrefetchScalarGridSpec(
            num_scalar_prefetch=1,
            grid=(1,),
            in_specs=[whole(blocks.shape)],
            out_specs=whole((tiles, PACK, DV)),
        ),
        out_shape=jax.ShapeDtypeStruct((tiles, PACK, DV), blocks.dtype),
        cost_estimate=pl.CostEstimate(flops=0, bytes_accessed=2 * tiles * PACK * DV * 2, transcendentals=0),
        compiler_params=pltpu.CompilerParams(vmem_limit_bytes=16 << 20),
        name="payload",
    )(wanted, blocks)


def coarse_kernel(info_ref, kv_ref, q_ref, gate_ref, out_ref, keys, values_t, scores):
    n_chunks = C * X
    rows = Z * BLK

    @pl.when(pl.program_id(0) == 0)
    def _():
        def one(n, carry):
            at = pl.multiple_of(n * 2 * BLK, 2 * BLK)
            keys[pl.ds(at, BLK), :] = unpacked_keys(kv_ref[2 * n])
            keys[pl.ds(at + BLK, BLK), :] = unpacked_keys(kv_ref[2 * n + 1])
            v = jnp.concatenate([kv_ref[2 * n, BLK : 2 * BLK], kv_ref[2 * n + 1, BLK : 2 * BLK]], axis=0)
            values_t[:, pl.ds(at, 2 * BLK)] = v.T
            return carry

        lax.fori_loop(0, n_chunks * Z // 2, one, 0)

    q = jnp.concatenate([q_ref[0], q_ref[1]], axis=1)
    width = q.shape[1]
    late = 2 * BLK
    row = lax.broadcasted_iota(jnp.int32, (late, width), 0)
    lane = lax.broadcasted_iota(jnp.int32, (late, width), 1)
    z = Z - 2 + row // BLK
    token0 = z * (X * C * BLK) + row % BLK
    query_pos = info_ref[0] + lane % TILE
    top = jnp.full((1, width), NEGATIVE, jnp.float32)
    for n in range(n_chunks):
        c, x = divmod(n, X)
        s = jnp.dot(keys[n * rows : (n + 1) * rows, :], q, preferred_element_type=jnp.float32)
        token = token0 + (x * C + c) * BLK
        tail = jnp.where(token * CSTRIDE + CLEN - 1 <= query_pos, s[rows - late :], NEGATIVE)
        scores[n * rows : (n + 1) * rows - late, :] = s[: rows - late]
        scores[(n + 1) * rows - late : (n + 1) * rows, :] = tail
        top = jnp.maximum(top, jnp.max(s[: rows - late], axis=0, keepdims=True))
        top = jnp.maximum(top, jnp.max(tail, axis=0, keepdims=True))
    total = jnp.zeros((1, width), jnp.float32)
    acc = jnp.zeros((DV, width), jnp.float32)
    for n in range(n_chunks):
        w = jnp.exp2((scores[n * rows : (n + 1) * rows, :] - top) * EXP_SCALE)
        total = total + jnp.sum(w, axis=0, keepdims=True)
        acc = acc + jnp.dot(
            values_t[:, n * rows : (n + 1) * rows], w.astype(jnp.bfloat16), preferred_element_type=jnp.float32
        )
    gate = jnp.concatenate([gate_ref[0], gate_ref[1]], axis=1)
    acc = acc * (gate / total)
    out_ref[0] = acc[:, :TILE]
    out_ref[1] = acc[:, TILE:]


def coarse_branch(info, coarse, queries_t, gate):
    heads = queries_t.shape[0]
    tokens = coarse.shape[0] * BLK
    pair = lambda shape: pl.BlockSpec((2, *shape), lambda p, i: (p, 0, 0))
    return pl.pallas_call(
        coarse_kernel,
        grid_spec=pltpu.PrefetchScalarGridSpec(
            num_scalar_prefetch=1,
            grid=(heads // 2,),
            in_specs=[
                pl.BlockSpec(coarse.shape, lambda p, i: (0, 0, 0), pipeline_mode=pl.Buffered(1)),
                pair((DQK, TILE)),
                pair((1, TILE)),
            ],
            out_specs=pair((DV, TILE)),
            scratch_shapes=[
                pltpu.VMEM((tokens, DQK), jnp.bfloat16),
                pltpu.VMEM((DV, tokens), jnp.bfloat16),
                pltpu.VMEM((tokens, 2 * TILE), jnp.float32),
            ],
        ),
        out_shape=jax.ShapeDtypeStruct((heads, DV, TILE), jnp.float32),
        cost_estimate=pl.CostEstimate(
            flops=2 * heads * TILE * tokens * (DQK + DV),
            bytes_accessed=tokens * (DQK + DV) * 2 + heads * TILE * (DQK * 2 + DV * 4),
            transcendentals=heads * TILE * tokens,
        ),
        compiler_params=pltpu.CompilerParams(vmem_limit_bytes=24 << 20),
        name="coarse",
    )(info, coarse, queries_t, gate)


def tail_kernel(
    n_grp, info_ref, incoming_ref, q_ref, gate_ref, coarse_ref, weight_ref, *rest
):
    outs, (blocks, keys, values_t, scores, attended, weight, block_sem, weight_sem) = rest[:n_grp], rest[n_grp:]
    heads = q_ref.shape[0]
    cols = weight.shape[2]
    base, grp = info_ref[0], info_ref[1]
    late = SEL - 1
    for j in range(SEL):
        late = jnp.where(info_ref[2 + j] * BLK >= base, j, late)
    copies = []
    for j in range(SEL):
        slot_from = jnp.where(late == j, SEL - 1, j) if j < SEL - 1 else late
        owner = info_ref[2 + slot_from] // (1024 // BLK)
        copies.append(pltpu.make_async_copy(incoming_ref.at[owner], blocks.at[j], block_sem.at[j]))
    for copy in copies:
        copy.start()
    weight_copies = []
    for k in range(n_grp):
        at = pl.multiple_of(lax.rem(grp + k, n_grp) * cols, DV)
        weight_copies.append(
            pltpu.make_async_copy(weight_ref.at[:, pl.ds(at, cols)], weight.at[k], weight_sem.at[k])
        )
    for copy in weight_copies:
        copy.start()
    for j in range(0, SEL, 2):
        copies[j].wait()
        copies[j + 1].wait()
        keys[j * BLK : (j + 1) * BLK, :] = unpacked_keys(blocks[j])
        keys[(j + 1) * BLK : (j + 2) * BLK, :] = unpacked_keys(blocks[j + 1])
        v = jnp.concatenate([blocks[j, BLK : 2 * BLK], blocks[j + 1, BLK : 2 * BLK]], axis=0)
        values_t[:, j * BLK : (j + 2) * BLK] = v.T
    width = 2 * TILE
    n_keys = SEL * BLK
    row = lax.broadcasted_iota(jnp.int32, (BLK, width), 0)
    lane = lax.broadcasted_iota(jnp.int32, (BLK, width), 1)
    seen = info_ref[2 + late] * BLK + row <= base + lane % TILE

    for p in range(heads // 2):
        q = jnp.concatenate([q_ref[2 * p], q_ref[2 * p + 1]], axis=1)
        s = jnp.dot(keys[...], q, preferred_element_type=jnp.float32)
        last = jnp.where(seen, s[n_keys - BLK :], NEGATIVE)
        top = jnp.maximum(
            jnp.max(s[: n_keys - BLK], axis=0, keepdims=True), jnp.max(last, axis=0, keepdims=True)
        )
        w = jnp.exp2((jnp.concatenate([s[: n_keys - BLK], last], axis=0) - top) * EXP_SCALE)
        total = jnp.sum(w, axis=0, keepdims=True)
        o = jnp.dot(values_t[...], w.astype(jnp.bfloat16), preferred_element_type=jnp.float32)
        gate = jnp.concatenate([gate_ref[2 * p], gate_ref[2 * p + 1]], axis=1)
        o = o * (gate / total)
        for i in range(2):
            h = 2 * p + i
            both = o[:, i * TILE : (i + 1) * TILE] + coarse_ref[h]
            attended[:, h * DV : (h + 1) * DV] = both.T.astype(jnp.bfloat16)
    for k in range(n_grp):
        weight_copies[k].wait()
    for k in range(n_grp):
        part = jnp.dot(attended[...], weight[k], preferred_element_type=jnp.float32)
        outs[k][...] = part.astype(outs[k].dtype)


def tail(info, incoming, queries_t, gate, coarse_out, out_weight, n_grp):
    heads = queries_t.shape[0]
    rows, model = out_weight.shape
    cols = model // n_grp
    vmem = lambda shape: pl.BlockSpec(shape, lambda i, s: (0,) * len(shape))
    anywhere = pl.BlockSpec(memory_space=pl.ANY)
    return pl.pallas_call(
        functools.partial(tail_kernel, n_grp),
        grid_spec=pltpu.PrefetchScalarGridSpec(
            num_scalar_prefetch=1,
            grid=(1,),
            in_specs=[
                anywhere,
                vmem(queries_t.shape),
                vmem(gate.shape),
                vmem(coarse_out.shape),
                anywhere,
            ],
            out_specs=[vmem((TILE, cols))] * n_grp,
            scratch_shapes=[
                pltpu.VMEM((SEL, PACK, DV), jnp.bfloat16),
                pltpu.VMEM((SEL * BLK, DQK), jnp.bfloat16),
                pltpu.VMEM((DV, SEL * BLK), jnp.bfloat16),
                pltpu.VMEM((SEL * BLK, 2 * TILE), jnp.float32),
                pltpu.VMEM((TILE, rows), jnp.bfloat16),
                pltpu.VMEM((n_grp, rows, cols), jnp.bfloat16),
                pltpu.SemaphoreType.DMA((SEL,)),
                pltpu.SemaphoreType.DMA((n_grp,)),
            ],
        ),
        out_shape=[jax.ShapeDtypeStruct((TILE, cols), jnp.float32)]
        + [jax.ShapeDtypeStruct((TILE, cols), jnp.bfloat16)] * (n_grp - 1),
        cost_estimate=pl.CostEstimate(
            flops=2 * heads * TILE * SEL * BLK * (DQK + DV) + 2 * TILE * rows * model,
            bytes_accessed=rows * model * 2,
            transcendentals=heads * TILE * SEL * BLK,
        ),
        compiler_params=pltpu.CompilerParams(vmem_limit_bytes=40 << 20),
        name="tail",
    )(info, incoming, queries_t, gate, coarse_out, out_weight)


def shards(
    queries,
    key_cache,
    group_value_cache,
    coarse_keys,
    coarse_values,
    hidden,
    gate_weight,
    out_weight,
    selected,
):
    seq_count = lax.axis_size("seq")
    n_grp = lax.axis_size("grp")
    seq_index = lax.axis_index("seq")
    grp_index = lax.axis_index("grp")
    ctx_dev = key_cache.shape[1]
    context = ctx_dev * seq_count
    heads = queries.shape[1]
    blocks_dev = ctx_dev // BLK

    own_list = selected[0, 0]
    owners = jnp.arange(seq_count, dtype=jnp.int32)
    mine = (own_list[None, :] // blocks_dev == owners[:, None]).astype(jnp.int32)
    wanted = jnp.sum(mine * (own_list % blocks_dev)[None, :], axis=1)
    wanted = jnp.broadcast_to(wanted[:, None, None], (seq_count, 1, SEL))
    wanted = lax.all_to_all(wanted, "seq", 0, 0, tiled=True)[:, 0, 0]

    blocks = packed_blocks(
        key_cache[0].reshape(blocks_dev, BLK, DQK), group_value_cache[0].reshape(blocks_dev, BLK, DV)
    )
    incoming = lax.all_to_all(payload(wanted, blocks), "seq", 0, 0, tiled=True)

    coarse = everywhere(packed_blocks(coarse_keys, coarse_values))

    first_pos = context - TILE * seq_count + seq_index * TILE
    info = jnp.concatenate([jnp.stack([first_pos, grp_index]).astype(jnp.int32), own_list])
    queries_t = jnp.transpose(queries, (1, 2, 0))
    gates = jax.nn.sigmoid(
        lax.dot_general(
            gate_weight[0], hidden, (((0,), (1,)), ((), ())), preferred_element_type=jnp.float32
        )
    )[:, None, :]
    coarse_out = coarse_branch(info, coarse, queries_t, gates[:heads])
    own, *others = tail(info, incoming, queries_t, gates[heads:], coarse_out, out_weight, n_grp)
    for k, part in enumerate(others, 1):
        perm = [(i, (i + k) % n_grp) for i in range(n_grp)]
        own = own + lax.ppermute(part, "grp", perm).astype(jnp.float32)
    return own.astype(jnp.bfloat16)


def solution(mesh):
    return jax.shard_map(
        shards,
        mesh=mesh,
        in_specs=(
            P("seq", "grp", None),
            P("grp", "seq", None),
            P("grp", "seq", None),
            P("grp", "seq", None),
            P("grp", "seq", None),
            P("seq", None),
            P("grp", None, None),
            P("grp", None),
            P("grp", "seq", None),
        ),
        out_specs=P("seq", "grp"),
        check_vma=False,
    )
```

time: 222 us -> 160 us (0.72)
  matrix products: 55.5 us -> 0.33 us
  other arithmetic: 36.2 us -> 2.55 us
  Pallas kernels: 0 us -> 29.5 us
  between operations: 13.6 us -> 0.16 us
  local copies, waits for them, and re-layouts: 23.7 us -> 12.3 us
  blocking collectives: 14.5 us -> 23.9 us
  waiting for transfers between devices: 55.8 us -> 63.4 us
  starting transfers between devices: 21.4 us -> 26.4 us
    all_to_all x2 -> x3, waiting for transfers between devices: 2.11 us -> 58.7 us  [the longest x1 39.8 us: shards(): incoming = lax.all_to_all(payload(wanted, blocks), 'seq', 0, 0, tiled=True)]
    dot_general x20 -> x1, matrix products: 55.5 us -> 0.33 us  [shards(): lax.dot_general(gate_weight[0], hidden, (((0,), (1,)), ((), ())), preferr...]
    all_gather x1 -> x0, waiting for transfers between devices: 53.7 us -> none  [sent_together(): lax.all_gather(both, axis, axis=dim, tiled=True)]
    pallas_call x0 -> x3, Pallas kernels: none -> 29.5 us  [the longest x1 17.4 us: coarse_branch(): pl.pallas_call(coarse_kernel, grid_spec=pltpu.PrefetchScalarGridSpec(num_...]
    reduce_sum x13 -> x1, other arithmetic: 27.2 us -> 0.09 us  [shards(): wanted = jnp.sum(mine * (own_list % blocks_dev)[None, :], axis=1)]
    all_to_all x1 -> x2, blocking collectives: 14.5 us -> 23.9 us  [copies_for(): lax.all_to_all(jnp.broadcast_to(x[None], (peers, *x.shape)), 'seq', 0, 0,...]
    gather x3 -> x0, local copies, waits for them, and re-layouts: 5.4 us -> none  [the longest x1 2.61 us: shards(): incoming[own_owner, own_rank].reshape(SEL * BLK, key_width + value_width)]
    ppermute x0 -> x3, starting transfers between devices: none -> 5.06 us  [shards(): own = own + lax.ppermute(part, 'grp', perm).astype(jnp.float32)]
  transfers between devices with their start and end apart: 3 -> 6, of which waited for: 2 -> 5; matrix products, arithmetic and copies ran while one was open for 40% -> 3% of each run, Pallas kernels for 0% -> 12%
where the time goes in v1:
time: 160 us; the launch traced here: 158 us
  waiting for transfers between devices  63.4 us (40%)
  Pallas kernels  29.5 us (18%)
  starting transfers between devices  26.4 us (16%)
  blocking collectives  23.9 us (15%)
  local copies, waits for them, and re-layouts  12.3 us (8%)
  other arithmetic  2.55 us (2%)
    all_to_all x1, waiting for transfers between devices, shards(): incoming = lax.all_to_all(payload(wanted, blocks), 'seq', 0, 0, tiled=True)  39.8 us
    all_to_all x2, blocking collectives, copies_for(): lax.all_to_all(jnp.broadcast_to(x[None], (peers, *x.shape)), 'seq', 0, 0,...  23.9 us
    pallas_call x1, Pallas kernels, coarse_branch(): pl.pallas_call(coarse_kernel, grid_spec=pltpu.PrefetchScalarGridSpec(num_...  17.4 us
    all_to_all x1, starting transfers between devices, shards(): wanted = lax.all_to_all(wanted, 'seq', 0, 0, tiled=True)[:, 0, 0]  13 us
    all_to_all x1, waiting for transfers between devices, copies_for(): lax.all_to_all(jnp.broadcast_to(x[None], (peers, *x.shape)), 'seq', 0, 0,...  11.8 us
    pallas_call x1, Pallas kernels, tail(): pl.pallas_call(functools.partial(tail_kernel, n_grp), grid_spec=pltpu.Pre...  9.79 us
    all_to_all x1, waiting for transfers between devices, shards(): wanted = lax.all_to_all(wanted, 'seq', 0, 0, tiled=True)[:, 0, 0]  7.07 us
    unnamed x21, local copies, waits for them, and re-layouts  7.02 us
  transfers between devices with their start and end apart: 6, of which 5 were waited for; matrix products, arithmetic and copies ran while one was open for 3% of the time, Pallas kernels for 12%

profile of v1, /device:TPU:1, one launch (start us, length us, event | category | flops | bytes accessed | tf_op | source)
XLA Modules:
  0.0 158.5 jit_solution(17250506306036323523)
XLA Ops:
  0.0 0.7 and_select_fusion.1
  0.8 0.8 broadcast_in_dim.14
  1.6 13.0 %all-to-all-start = ((s32[64,1,16]{2,1,0:T(1,128)}), s32[64,1,16]{2,1,0:T(1,128)S(1)}, u32[]{:S(2)}, u32[]{:S(2)}) async-start(s32[64,1,16]{2,1,0:T(1,128)} %broadcast_in_dim.14), calls=%async_computation | async-start | bytes 65536 | tf_op jit(solution)/shard_map/all_to_all | solution.py:284
  14.6 0.7 slice.39
  15.3 0.7 fusion.5
  16.0 0.8 maximum_bitcast_fusion
  16.8 7.1 %all-to-all-done = s32[64,1,16]{2,1,0:T(1,128)S(1)} async-done(((s32[64,1,16]{2,1,0:T(1,128)}), s32[64,1,16]{2,1,0:T(1,128)S(1)}, u32[]{:S(2)}, u32[]{:S(2)}) %all-to-all-start) | async-done | bytes 4128 | tf_op jit(solution)/shard_map/all_to_all | solution.py:284
  23.9 15.1 %all_to_all.25 = bf16[8,1,160,128]{3,2,1,0:T(8,128)(2,1)S(1)} all-to-all(bf16[8,1,160,128]{3,2,1,0:T(8,128)(2,1)S(1)} %broadcast_in_dim.16), channel_id=1, replica_groups={{0,8,16,24,32,40,48,56},{1,9,17,25,33,41,49,57},{2,10,18,26,34,42,50,58..., dimensions={0} | all-to-all | bytes 655360 | tf_op jit(solution)/shard_map/all_to_all | solution.py:36
  39.0 1.3 broadcast_in_dim.18
  40.3 3.7 %all-to-all-start.3 = ((bf16[4,8,1,160,128]{4,3,1,2,0:T(8,128)(2,1)}), bf16[4,8,1,160,128]{4,3,1,2,0:T(8,128)(2,1)S(1)}, u32[]{:S(2)}, u32[]{:S(2)}) async-start(bf16[4,8,1,160,128]{4,3,1,2,0:T(8,128)(2,1)} %broadcast_in_dim.18), calls=%async_computation.3 | async-start | bytes 2621440 | tf_op jit(solution)/shard_map/all_to_all | solution.py:36
  44.3 0.6 copy-done.7
  45.1 1.3 slice_reduce_fusion.wanted_ref
  46.3 2.3 %payload.1 = bf16[64,160,128]{2,1,0:T(8,128)(2,1)} custom-call(s32[64]{0:T(128)S(1)} %slice_reduce_fusion.wanted_ref, bf16[16,160,128]{2,1,0:T(8,128)(2,1)S(1)} %maximum_maximum_fusion.blocks_ref), custom_call_target="tpu_custom_call" | custom-call | bytes 5242880 | tf_op jit(solution)/shard_map/payload/pallas_call | solution.py:61
  48.6 11.8 %all-to-all-done.3 = bf16[4,8,1,160,128]{4,3,1,2,0:T(8,128)(2,1)S(1)} async-done(((bf16[4,8,1,160,128]{4,3,1,2,0:T(8,128)(2,1)}), bf16[4,8,1,160,128]{4,3,1,2,0:T(8,128)(2,1)S(1)}, u32[]{:S(2)}, u32[]{:S(2)}) %all-to-all-start.3) | async-done | bytes 1310752 | tf_op jit(solution)/shard_map/all_to_all | solution.py:36
  60.4 0.4 broadcast_in_dim.39
  60.8 8.8 %all_to_all.26 = bf16[2,4,8,1,160,128]{5,4,2,1,3,0:T(8,128)(2,1)} all-to-all(bf16[2,4,8,1,160,128]{5,4,2,1,3,0:T(8,128)(2,1)S(1)} %broadcast_in_dim.39), channel_id=1, replica_groups={{0,1},{2,3},{4,5},{6,7},{8,9},{10,11},{12,13},{14,15},{16,17},{18,19},{..., dimensions={0} | all-to-all | bytes 5242880 | tf_op jit(solution)/shard_map/all_to_all | solution.py:36
  69.6 4.7 %all-to-all-start.1 = ((bf16[64,160,128]{2,1,0:T(8,128)(2,1)}), bf16[64,160,128]{2,1,0:T(8,128)(2,1)S(1)}, u32[]{:S(2)}, u32[]{:S(2)}) async-start(bf16[64,160,128]{2,1,0:T(8,128)(2,1)} %payload.1), calls=%async_computation.1 | async-start | bytes 5242880 | tf_op jit(solution)/shard_map/all_to_all | solution.py:289
  74.4 0.3 fusion.2
  74.8 1.7 %copy-done.1 = bf16[2,4,8,1,160,128]{5,4,2,1,3,0:T(8,128)(2,1)S(1)} copy-done((bf16[2,4,8,1,160,128]{5,4,2,1,3,0:T(8,128)(2,1)S(1)}, bf16[2,4,8,1,160,128]{5,4,2,1,3,0:T(8,128)(2,1)}, u32[]{:S(2)}) %copy-start.1) | copy-done | bytes 2621464
  76.5 1.1 copy-done.4
  77.6 17.4 %coarse.1.coarse_ref = f32[16,128,128]{2,1,0:T(8,128)S(1)} custom-call(s32[18]{0:T(128)S(1)} %pad_add_fusion.info_ref, bf16[64,160,128]{2,1,0:T(8,128)(2,1)S(1)} %bitcast.25, bf16[16,192,128]{2,1,0:T(8,128)(2,1)S(1)} %bitcast.26, f32[16,1,128]{2,1,0:T(1,128)S(1)} %bitcast.29), custom_call_target="tpu_custom_call" | custom-call | flops 5368709120 | bytes 4456448 | tf_op jit(solution)/shard_map/coarse/pallas_call | solution.py:128
  95.1 1.0 copy-done.2
  96.0 39.8 %all-to-all-done.1.incoming_ref = bf16[64,160,128]{2,1,0:T(8,128)(2,1)S(1)} async-done(((bf16[64,160,128]{2,1,0:T(8,128)(2,1)}), bf16[64,160,128]{2,1,0:T(8,128)(2,1)S(1)}, u32[]{:S(2)}, u32[]{:S(2)}) %all-to-all-start.1) | async-done | bytes 2621472 | tf_op jit(solution)/shard_map/all_to_all | solution.py:289
  135.8 1.2 copy-done.3
  137.0 1.1 copy-done.5
  138.2 9.8 %tail.1 = (f32[128,640]{1,0:T(8,128)S(1)}, bf16[128,640]{1,0:T(8,128)(2,1)S(1)}, bf16[128,640]{1,0:T(8,128)(2,1)S(1)}, bf16[128,640]{1,0:T(8,128)(2,1)S(1)}) custom-call(s32[18]{0:T(128)S(1)} %pad_add_fusion.info_ref, bf16[64,160,128]{2,1,0:T(8,128)(2,1)S(1)} %all-to-all-done.1.incoming_ref, bf16[16,192,128]{2,1,0:T(8,128)(2,1)S(1)} %bitcast.27, ...), custom_call_target="tpu_custom_call" | custom-call | flops 2684354560 | bytes 10485760 | tf_op jit(solution)/shard_map/tail/pallas_call | solution.py:223
  148.0 1.4 collective-permute-start
  149.3 2.6 %collective-permute-start.1 = (bf16[128,640]{1,0:T(8,128)(2,1)S(1)}, bf16[128,640]{1,0:T(8,128)(2,1)S(1)}, u32[]{:S(2)}, u32[]{:S(2)}) collective-permute-start(bf16[128,640]{1,0:T(8,128)(2,1)S(1)} %get-tuple-element.11), channel_id=1, source_target_pairs={{0,128},{64,192},{128,0},{192,64},{1,129},{65,193},{129,1},{193,65... | collective-permute-start | bytes 491528 | tf_op jit(solution)/shard_map/ppermute | solution.py:305
  152.0 1.1 collective-permute-start.2
  153.0 0.5 collective-permute-done
  153.5 4.2 %collective-permute-done.1 = bf16[128,640]{1,0:T(8,128)(2,1)S(1)} collective-permute-done((bf16[128,640]{1,0:T(8,128)(2,1)S(1)}, bf16[128,640]{1,0:T(8,128)(2,1)S(1)}, u32[]{:S(2)}, u32[]{:S(2)}) %collective-permute-start.1) | collective-permute-done | bytes 163872 | tf_op jit(solution)/shard_map/ppermute | solution.py:305
  157.7 0.8 add_convert_fusion
  (23 shorter events, 0.7 us)
Async XLA Ops:
  0.0 74.4 %copy-start = (bf16[128,2560]{1,0:T(8,128)(2,1)S(1)}, bf16[128,2560]{1,0:T(8,128)(2,1)}, u32[]{:S(2)}) copy-start(bf16[128,2560]{1,0:T(8,128)(2,1)} %param.14) | copy-start | bytes 1966084
  1.6 22.3 %all-to-all-start = ((s32[64,1,16]{2,1,0:T(1,128)}), s32[64,1,16]{2,1,0:T(1,128)S(1)}, u32[]{:S(2)}, u32[]{:S(2)}) async-start(s32[64,1,16]{2,1,0:T(1,128)} %broadcast_in_dim.14), calls=%async_computation | async-start | bytes 65536 | tf_op jit(solution)/shard_map/all_to_all | solution.py:284
  40.3 3.7 %copy-start.6 = (bf16[1,1024,192]{1,2,0:T(8,128)(2,1)S(1)}, bf16[1,1024,192]{1,2,0:T(8,128)(2,1)}, u32[]{:S(2)}) copy-start(bf16[1,1024,192]{1,2,0:T(8,128)(2,1)} %param.10) | copy-start | bytes 1179652
  40.3 20.1 %all-to-all-start.3 = ((bf16[4,8,1,160,128]{4,3,1,2,0:T(8,128)(2,1)}), bf16[4,8,1,160,128]{4,3,1,2,0:T(8,128)(2,1)S(1)}, u32[]{:S(2)}, u32[]{:S(2)}) async-start(bf16[4,8,1,160,128]{4,3,1,2,0:T(8,128)(2,1)} %broadcast_in_dim.18), calls=%async_computation.3 | async-start | bytes 2621440 | tf_op jit(solution)/shard_map/all_to_all | solution.py:36
  44.0 1.0 copy-start.7
  69.6 4.7 %copy-start.9 = (s32[1,1,16]{2,1,0:T(1,128)S(1)}, s32[1,1,16]{2,1,0:T(1,128)}, u32[]{:S(2)}) copy-start(s32[1,1,16]{2,1,0:T(1,128)} %param.17) | copy-start | bytes 196
  69.6 4.8 %copy-start.8 = (bf16[1,2560,32]{1,2,0:T(8,128)(2,1)S(1)}, bf16[1,2560,32]{1,2,0:T(8,128)(2,1)}, u32[]{:S(2)}) copy-start(bf16[1,2560,32]{1,2,0:T(8,128)(2,1)} %param.15) | copy-start | bytes 491524
  69.6 66.2 %all-to-all-start.1 = ((bf16[64,160,128]{2,1,0:T(8,128)(2,1)}), bf16[64,160,128]{2,1,0:T(8,128)(2,1)S(1)}, u32[]{:S(2)}, u32[]{:S(2)}) async-start(bf16[64,160,128]{2,1,0:T(8,128)(2,1)} %payload.1), calls=%async_computation.1 | async-start | bytes 5242880 | tf_op jit(solution)/shard_map/all_to_all | solution.py:289
  74.8 1.7 %copy-start.1 = (bf16[2,4,8,1,160,128]{5,4,2,1,3,0:T(8,128)(2,1)S(1)}, bf16[2,4,8,1,160,128]{5,4,2,1,3,0:T(8,128)(2,1)}, u32[]{:S(2)}) copy-start(bf16[2,4,8,1,160,128]{5,4,2,1,3,0:T(8,128)(2,1)} %all_to_all.26) | copy-start | bytes 7864324
  76.5 1.1 copy-start.4
  95.1 1.0 copy-start.2
  135.8 1.2 copy-start.3
  137.0 1.1 copy-start.5
  148.0 5.5 %collective-permute-start = (bf16[128,640]{1,0:T(8,128)(2,1)S(1)}, bf16[128,640]{1,0:T(8,128)(2,1)S(1)}, u32[]{:S(2)}, u32[]{:S(2)}) collective-permute-start(bf16[128,640]{1,0:T(8,128)(2,1)S(1)} %get-tuple-element.10), channel_id=1, source_target_pairs={{0,64},{64,128},{128,192},{192,0},{1,65},{65,129},{129,193},{193,1... | collective-permute-start | bytes 491528 | tf_op jit(solution)/shard_map/ppermute | solution.py:305
  149.3 8.4 %collective-permute-start.1 = (bf16[128,640]{1,0:T(8,128)(2,1)S(1)}, bf16[128,640]{1,0:T(8,128)(2,1)S(1)}, u32[]{:S(2)}, u32[]{:S(2)}) collective-permute-start(bf16[128,640]{1,0:T(8,128)(2,1)S(1)} %get-tuple-element.11), channel_id=1, source_target_pairs={{0,128},{64,192},{128,0},{192,64},{1,129},{65,193},{129,1},{193,65... | collective-permute-start | bytes 491528 | tf_op jit(solution)/shard_map/ppermute | solution.py:305
  152.0 5.8 %collective-permute-start.2 = (bf16[128,640]{1,0:T(8,128)(2,1)S(1)}, bf16[128,640]{1,0:T(8,128)(2,1)S(1)}, u32[]{:S(2)}, u32[]{:S(2)}) collective-permute-start(bf16[128,640]{1,0:T(8,128)(2,1)S(1)} %get-tuple-element.12), channel_id=1, source_target_pairs={{0,192},{64,0},{128,64},{192,128},{1,193},{65,1},{129,65},{193,129... | collective-permute-start | bytes 491528 | tf_op jit(solution)/shard_map/ppermute | solution.py:305

commit v2 on v1

v2 whole, which is shorter than its diff:
```python
import functools
import math

import jax
import jax.numpy as jnp
from jax import lax
from jax.experimental import pallas as pl
from jax.experimental.pallas import tpu as pltpu
from jax.sharding import PartitionSpec as P

BLK = 64
SEL = 16
TILE = 128
CSTRIDE = 16
CLEN = 32
DQK = 192
DV = 128
PACK = BLK + BLK + BLK // 2
NEGATIVE = -1e30
EXP_SCALE = DQK**-0.5 * math.log2(math.e)
Z, X, C = 8, 4, 2


def packed_blocks(keys, values):
    high = jnp.concatenate([keys[:, : BLK // 2, DV:], keys[:, BLK // 2 :, DV:]], axis=2)
    return jnp.concatenate([keys[:, :, :DV], values, high], axis=1)


def unpacked_keys(block):
    high = jnp.concatenate([block[2 * BLK :, :BLK], block[2 * BLK :, BLK:]], axis=0)
    return jnp.concatenate([block[:BLK], high], axis=1)


def shifted(x, step):
    index = lambda z, x, c: ((z % Z) * X + x % X) * C + c % C
    dz, dx, dc = step
    perm = [(index(z, x, c), index(z + dz, x + dx, c + dc)) for z in range(Z) for x in range(X) for c in range(C)]
    return lax.ppermute(x, "seq", perm)


def everywhere(block, after):
    columns = jnp.concatenate([block] + [shifted(block, (k, 0, 0)) for k in range(1, Z)], axis=0)
    columns, _ = lax.optimization_barrier((columns, after))
    near = [columns] + [shifted(columns, (0, k, 0)) for k in range(1, X)]
    return near + [shifted(part, (0, 0, 1)) for part in near]


def payload_kernel(wanted_ref, blocks_ref, out_ref):
    def one(t, carry):
        out_ref[t] = blocks_ref[wanted_ref[t, 0, 0]]
        return carry

    lax.fori_loop(0, out_ref.shape[0], one, 0, unroll=8)


def payload(wanted, blocks):
    tiles = wanted.shape[0]
    whole = lambda shape: pl.BlockSpec(shape, lambda i, w: (0, 0, 0))
    return pl.pallas_call(
        payload_kernel,
        grid_spec=pltpu.PrefetchScalarGridSpec(
            num_scalar_prefetch=1,
            grid=(1,),
            in_specs=[whole(blocks.shape)],
            out_specs=whole((tiles, PACK, DV)),
        ),
        out_shape=jax.ShapeDtypeStruct((tiles, PACK, DV), blocks.dtype),
        cost_estimate=pl.CostEstimate(flops=0, bytes_accessed=2 * tiles * PACK * DV * 2, transcendentals=0),
        compiler_params=pltpu.CompilerParams(vmem_limit_bytes=16 << 20),
        name="payload",
    )(wanted, blocks)


def coarse_kernel(first_late, info_ref, *rest):
    kv_refs, (q_ref, gate_ref, out_ref, keys, values_t, scores) = rest[: C * X], rest[C * X :]
    n_tokens = keys.shape[0]

    @pl.when(pl.program_id(0) == 0)
    def _():
        me = info_ref[2]
        my_c, my_x, my_z = me % C, me // C % X, me // (C * X)

        def one(dx, x, dz, swapped):
            z = (my_z + Z - dz) % Z
            at = pl.multiple_of((z * X + x) * (C * BLK), C * BLK)
            first = kv_refs[swapped * X + dx].at[dz]
            second = kv_refs[(1 - swapped) * X + dx].at[dz]
            keys[pl.ds(at, BLK), :] = unpacked_keys(first)
            keys[pl.ds(at + BLK, BLK), :] = unpacked_keys(second)
            v = jnp.concatenate([first[BLK : 2 * BLK], second[BLK : 2 * BLK]], axis=0)
            values_t[:, pl.ds(at, C * BLK)] = v.T

        for swapped in range(C):

            @pl.when(my_c == swapped)
            def _(swapped=swapped):
                for dx in range(X):
                    x = (my_x + X - dx) % X

                    def step(dz, carry, dx=dx, x=x):
                        one(dx, x, dz, swapped)
                        return carry

                    lax.fori_loop(0, Z, step, 0)

    q = jnp.concatenate([q_ref[0], q_ref[1]], axis=1)
    width = q.shape[1]
    rows = 512
    row = lax.broadcasted_iota(jnp.int32, (rows, width), 0)
    query_pos = info_ref[0] + lax.broadcasted_iota(jnp.int32, (rows, width), 1) % TILE
    top = jnp.full((1, width), NEGATIVE, jnp.float32)
    for at in range(0, n_tokens, rows):
        s = jnp.dot(keys[at : at + rows, :], q, preferred_element_type=jnp.float32)
        if at + rows > first_late:
            s = jnp.where((at + row) * CSTRIDE + CLEN - 1 <= query_pos, s, NEGATIVE)
        scores[at : at + rows, :] = s
        top = jnp.maximum(top, jnp.max(s, axis=0, keepdims=True))
    total = jnp.zeros((1, width), jnp.float32)
    acc = jnp.zeros((DV, width), jnp.float32)
    for at in range(0, n_tokens, rows):
        w = jnp.exp2((scores[at : at + rows, :] - top) * EXP_SCALE)
        total = total + jnp.sum(w, axis=0, keepdims=True)
        acc = acc + jnp.dot(
            values_t[:, at : at + rows], w.astype(jnp.bfloat16), preferred_element_type=jnp.float32
        )
    gate = jnp.concatenate([gate_ref[0], gate_ref[1]], axis=1)
    acc = acc * (gate / total)
    out_ref[0] = acc[:, :TILE]
    out_ref[1] = acc[:, TILE:]


def coarse_branch(info, coarse, queries_t, gate, first_query):
    heads = queries_t.shape[0]
    tokens = C * X * Z * BLK
    pair = lambda shape: pl.BlockSpec((2, *shape), lambda p, i: (p, 0, 0))
    return pl.pallas_call(
        functools.partial(coarse_kernel, (first_query - CLEN + 1) // CSTRIDE + 1),
        grid_spec=pltpu.PrefetchScalarGridSpec(
            num_scalar_prefetch=1,
            grid=(heads // 2,),
            in_specs=[
                *[pl.BlockSpec(part.shape, lambda p, i: (0, 0, 0), pipeline_mode=pl.Buffered(1)) for part in coarse],
                pair((DQK, TILE)),
                pair((1, TILE)),
            ],
            out_specs=pair((DV, TILE)),
            scratch_shapes=[
                pltpu.VMEM((tokens, DQK), jnp.bfloat16),
                pltpu.VMEM((DV, tokens), jnp.bfloat16),
                pltpu.VMEM((tokens, 2 * TILE), jnp.float32),
            ],
        ),
        out_shape=jax.ShapeDtypeStruct((heads, DV, TILE), jnp.float32),
        cost_estimate=pl.CostEstimate(
            flops=2 * heads * TILE * tokens * (DQK + DV),
            bytes_accessed=tokens * (DQK + DV) * 2 + heads * TILE * (DQK * 2 + DV * 4),
            transcendentals=heads * TILE * tokens,
        ),
        compiler_params=pltpu.CompilerParams(vmem_limit_bytes=24 << 20),
        name="coarse",
    )(info, *coarse, queries_t, gate)


def tail_kernel(
    n_grp, info_ref, incoming_ref, q_ref, gate_ref, coarse_ref, weight_ref, *rest
):
    outs, scratch = rest[:n_grp], rest[n_grp:]
    blocks, keys, values_t, queries, coarse, attended, weight, block_sem, in_sem, weight_sem = scratch
    heads = q_ref.shape[0]
    cols = weight.shape[2]
    base, grp = info_ref[0], info_ref[1]
    late = SEL - 1
    for j in range(SEL):
        late = jnp.where(info_ref[3 + j] * BLK >= base, j, late)
    copies = []
    for j in range(SEL):
        slot_from = jnp.where(late == j, SEL - 1, j) if j < SEL - 1 else late
        owner = info_ref[3 + slot_from] // (1024 // BLK)
        copies.append(pltpu.make_async_copy(incoming_ref.at[owner], blocks.at[j], block_sem.at[j]))
    copies.append(pltpu.make_async_copy(q_ref, queries, in_sem.at[0]))
    copies.append(pltpu.make_async_copy(coarse_ref, coarse, in_sem.at[1]))
    for copy in copies:
        copy.start()
    weight_copies = []
    for k in range(n_grp):
        at = pl.multiple_of(lax.rem(grp + k, n_grp) * cols, DV)
        weight_copies.append(
            pltpu.make_async_copy(weight_ref.at[:, pl.ds(at, cols)], weight.at[k], weight_sem.at[k])
        )
    for copy in weight_copies:
        copy.start()
    for j in range(0, SEL, 2):
        copies[j].wait()
        copies[j + 1].wait()
        keys[j * BLK : (j + 1) * BLK, :] = unpacked_keys(blocks[j])
        keys[(j + 1) * BLK : (j + 2) * BLK, :] = unpacked_keys(blocks[j + 1])
        v = jnp.concatenate([blocks[j, BLK : 2 * BLK], blocks[j + 1, BLK : 2 * BLK]], axis=0)
        values_t[:, j * BLK : (j + 2) * BLK] = v.T
    copies[SEL].wait()
    copies[SEL + 1].wait()
    width = 2 * TILE
    n_keys = SEL * BLK
    row = lax.broadcasted_iota(jnp.int32, (BLK, width), 0)
    lane = lax.broadcasted_iota(jnp.int32, (BLK, width), 1)
    seen = info_ref[3 + late] * BLK + row <= base + lane % TILE

    for p in range(heads // 2):
        q = jnp.concatenate([queries[2 * p], queries[2 * p + 1]], axis=1)
        s = jnp.dot(keys[...], q, preferred_element_type=jnp.float32)
        last = jnp.where(seen, s[n_keys - BLK :], NEGATIVE)
        top = jnp.maximum(
            jnp.max(s[: n_keys - BLK], axis=0, keepdims=True), jnp.max(last, axis=0, keepdims=True)
        )
        w = jnp.exp2((jnp.concatenate([s[: n_keys - BLK], last], axis=0) - top) * EXP_SCALE)
        total = jnp.sum(w, axis=0, keepdims=True)
        o = jnp.dot(values_t[...], w.astype(jnp.bfloat16), preferred_element_type=jnp.float32)
        gate = jnp.concatenate([gate_ref[2 * p], gate_ref[2 * p + 1]], axis=1)
        o = o * (gate / total)
        for i in range(2):
            h = 2 * p + i
            both = o[:, i * TILE : (i + 1) * TILE] + coarse[h]
            attended[:, h * DV : (h + 1) * DV] = both.T.astype(jnp.bfloat16)
    for k in range(n_grp):
        weight_copies[k].wait()
    for k in range(n_grp):
        part = jnp.dot(attended[...], weight[k], preferred_element_type=jnp.float32)
        outs[k][...] = part.astype(outs[k].dtype)


def in_hbm(x):
    return pltpu.with_memory_space_constraint(x, pltpu.HBM)


def tail(info, incoming, queries_t, gate, coarse_out, out_weight, n_grp):
    heads = queries_t.shape[0]
    rows, model = out_weight.shape
    cols = model // n_grp
    vmem = lambda shape: pl.BlockSpec(shape, lambda i, s: (0,) * len(shape))
    hbm = pl.BlockSpec(memory_space=pltpu.HBM)
    return pl.pallas_call(
        functools.partial(tail_kernel, n_grp),
        grid_spec=pltpu.PrefetchScalarGridSpec(
            num_scalar_prefetch=1,
            grid=(1,),
            in_specs=[
                pl.BlockSpec(memory_space=pl.ANY),
                hbm,
                vmem(gate.shape),
                hbm,
                hbm,
            ],
            out_specs=[vmem((TILE, cols))] * n_grp,
            scratch_shapes=[
                pltpu.VMEM((SEL, PACK, DV), jnp.bfloat16),
                pltpu.VMEM((SEL * BLK, DQK), jnp.bfloat16),
                pltpu.VMEM((DV, SEL * BLK), jnp.bfloat16),
                pltpu.VMEM(queries_t.shape, queries_t.dtype),
                pltpu.VMEM(coarse_out.shape, coarse_out.dtype),
                pltpu.VMEM((TILE, rows), jnp.bfloat16),
                pltpu.VMEM((n_grp, rows, cols), jnp.bfloat16),
                pltpu.SemaphoreType.DMA((SEL,)),
                pltpu.SemaphoreType.DMA((2,)),
                pltpu.SemaphoreType.DMA((n_grp,)),
            ],
        ),
        out_shape=[jax.ShapeDtypeStruct((TILE, cols), jnp.float32)]
        + [jax.ShapeDtypeStruct((TILE, cols), jnp.bfloat16)] * (n_grp - 1),
        cost_estimate=pl.CostEstimate(
            flops=2 * heads * TILE * SEL * BLK * (DQK + DV) + 2 * TILE * rows * model,
            bytes_accessed=rows * model * 2,
            transcendentals=heads * TILE * SEL * BLK,
        ),
        compiler_params=pltpu.CompilerParams(vmem_limit_bytes=24 << 20),
        name="tail",
    )(info, incoming, in_hbm(queries_t), gate, in_hbm(coarse_out), in_hbm(out_weight))


def shards(
    queries,
    key_cache,
    group_value_cache,
    coarse_keys,
    coarse_values,
    hidden,
    gate_weight,
    out_weight,
    selected,
):
    seq_count = lax.axis_size("seq")
    n_grp = lax.axis_size("grp")
    seq_index = lax.axis_index("seq")
    grp_index = lax.axis_index("grp")
    ctx_dev = key_cache.shape[1]
    context = ctx_dev * seq_count
    heads = queries.shape[1]
    blocks_dev = ctx_dev // BLK

    own_list = selected[0, 0]
    owners = jnp.arange(seq_count, dtype=jnp.int32)
    mine = (own_list[None, :] // blocks_dev == owners[:, None]).astype(jnp.int32)
    wanted = jnp.sum(mine * (own_list % blocks_dev)[None, :], axis=1)
    wanted = lax.all_to_all(wanted[:, None, None], "seq", 0, 0, tiled=True)

    blocks = packed_blocks(
        key_cache[0].reshape(blocks_dev, BLK, DQK), group_value_cache[0].reshape(blocks_dev, BLK, DV)
    )
    outgoing = payload(wanted, blocks)
    coarse = everywhere(packed_blocks(coarse_keys, coarse_values), outgoing)
    incoming = lax.all_to_all(outgoing, "seq", 0, 0, tiled=True)

    first_query = context - TILE * seq_count
    first_pos = first_query + seq_index * TILE
    info = jnp.concatenate([jnp.stack([first_pos, grp_index, seq_index]).astype(jnp.int32), own_list])
    queries_t = jnp.transpose(queries, (1, 2, 0))
    gates = jax.nn.sigmoid(
        lax.dot_general(
            gate_weight[0], hidden, (((0,), (1,)), ((), ())), preferred_element_type=jnp.float32
        )
    )[:, None, :]
    coarse_out = coarse_branch(info, coarse, queries_t, gates[:heads], first_query)
    own, *others = tail(info, incoming, queries_t, gates[heads:], coarse_out, out_weight, n_grp)
    for k, part in enumerate(others, 1):
        perm = [(i, (i + k) % n_grp) for i in range(n_grp)]
        own = own + lax.ppermute(part, "grp", perm).astype(jnp.float32)
    return own.astype(jnp.bfloat16)


def solution(mesh):
    return jax.shard_map(
        shards,
        mesh=mesh,
        in_specs=(
            P("seq", "grp", None),
            P("grp", "seq", None),
            P("grp", "seq", None),
            P("grp", "seq", None),
            P("grp", "seq", None),
            P("seq", None),
            P("grp", None, None),
            P("grp", None),
            P("grp", "seq", None),
        ),
        out_specs=P("seq", "grp"),
        check_vma=False,
    )
```

time: 160 us -> 174 us (1.087)
  starting transfers between devices: 26.4 us -> 52.3 us
  blocking collectives: 23.9 us -> 0 us
  waiting for transfers between devices: 63.4 us -> 73.8 us
  Pallas kernels: 29.5 us -> 35.9 us
  local copies, waits for them, and re-layouts: 12.3 us -> 8.45 us
    ppermute x0 -> x14, waiting for transfers between devices: none -> 59.6 us  [shifted(): return lax.ppermute(x, 'seq', perm)]
    all_to_all x3 -> x2, waiting for transfers between devices: 58.7 us -> 7.86 us  [the longest x1 7.86 us: shards(): wanted = lax.all_to_all(wanted[:, None, None], 'seq', 0, 0, tiled=True)]
    ppermute x0 -> x14, starting transfers between devices: none -> 29.3 us  [shifted(): return lax.ppermute(x, 'seq', perm)]
    all_to_all x2 -> x0, blocking collectives: 23.9 us -> none  [copies_for(): lax.all_to_all(jnp.broadcast_to(x[None], (peers, *x.shape)), 'seq', 0, 0,...]
    all_to_all x3 -> x2, starting transfers between devices: 21.3 us -> 18 us  [the longest x1 13 us: shards(): wanted = lax.all_to_all(wanted[:, None, None], 'seq', 0, 0, tiled=True)]
    pallas_call x1, Pallas kernels: 9.79 us -> 12.9 us  [tail(): pl.pallas_call(functools.partial(tail_kernel, n_grp), grid_spec=pltpu.Pre...]
    pallas_call x1, Pallas kernels: 17.4 us -> 20.2 us  [coarse_branch(): pl.pallas_call(functools.partial(coarse_kernel, (first_query - CLEN + 1)...]
    broadcast_in_dim x4 -> x1, local copies, waits for them, and re-layouts: 2.47 us -> 0.71 us  [shards(): wanted = lax.all_to_all(wanted[:, None, None], 'seq', 0, 0, tiled=True)]
  transfers between devices with their start and end apart: 6 -> 19, of which waited for: 5 -> 8; matrix products, arithmetic and copies ran while one was open for 3% -> 4% of each run, Pallas kernels for 12% -> 12%
where the time goes in v2:
time: 174 us; the launch traced here: 173 us
  waiting for transfers between devices  73.8 us (42%)
  starting transfers between devices  52.3 us (30%)
  Pallas kernels  35.9 us (21%)
  local copies, waits for them, and re-layouts  8.45 us (5%)
  other arithmetic  2.46 us (1%)
    ppermute x14, waiting for transfers between devices, shifted(): return lax.ppermute(x, 'seq', perm)  59.6 us
    ppermute x14, starting transfers between devices, shifted(): return lax.ppermute(x, 'seq', perm)  29.3 us
    pallas_call x1, Pallas kernels, coarse_branch(): pl.pallas_call(functools.partial(coarse_kernel, (first_query - CLEN + 1)...  20.2 us
    all_to_all x1, starting transfers between devices, shards(): wanted = lax.all_to_all(wanted[:, None, None], 'seq', 0, 0, tiled=True)  13 us
    pallas_call x1, Pallas kernels, tail(): pl.pallas_call(functools.partial(tail_kernel, n_grp), grid_spec=pltpu.Pre...  12.9 us
    all_to_all x1, waiting for transfers between devices, shards(): wanted = lax.all_to_all(wanted[:, None, None], 'seq', 0, 0, tiled=True)  7.86 us
    unnamed x23, local copies, waits for them, and re-layouts  7.02 us
    ppermute x3, waiting for transfers between devices, shards(): own = own + lax.ppermute(part, 'grp', perm).astype(jnp.float32)  6.39 us
  transfers between devices with their start and end apart: 19, of which 8 were waited for; matrix products, arithmetic and copies ran while one was open for 4% of the time, Pallas kernels for 12%

profile of v2, /device:TPU:1, one launch (start us, length us, event | category | flops | bytes accessed | tf_op | source)
XLA Modules:
  0.0 173.4 jit_solution(9705688257314932257)
XLA Ops:
  0.0 0.7 and_select_fusion.1
  0.8 0.7 copy.13
  1.6 13.0 %all-to-all-start = ((s32[64,1,1]{2,1,0:T(1,128)}), s32[64,1,1]{2,1,0:T(1,128)S(1)}, u32[]{:S(2)}, u32[]{:S(2)}) async-start(s32[64,1,1]{2,1,0:T(1,128)} %copy.13), calls=%async_computation | async-start | bytes 65536 | tf_op jit(solution)/shard_map/all_to_all | solution.py:302
  14.5 1.2 copy.14
  16.0 7.9 %all-to-all-done.wanted_ref = s32[64,1,1]{2,1,0:T(1,128)S(1)} async-done(((s32[64,1,1]{2,1,0:T(1,128)}), s32[64,1,1]{2,1,0:T(1,128)S(1)}, u32[]{:S(2)}, u32[]{:S(2)}) %all-to-all-start) | async-done | bytes 288 | tf_op jit(solution)/shard_map/all_to_all | solution.py:302
  23.9 2.8 %payload.1 = bf16[64,160,128]{2,1,0:T(8,128)(2,1)} custom-call(s32[64,1,1]{2,1,0:T(1,128)S(1)} %all-to-all-done.wanted_ref, bf16[16,160,128]{2,1,0:T(8,128)(2,1)S(1)} %maximum_maximum_fusion.blocks_ref), custom_call_target="tpu_custom_call" | custom-call | bytes 5242880 | tf_op jit(solution)/shard_map/payload/pallas_call | solution.py:59
  26.6 5.0 %all-to-all-start.1 = ((bf16[64,160,128]{2,1,0:T(8,128)(2,1)}), bf16[64,160,128]{2,1,0:T(8,128)(2,1)S(1)}, u32[]{:S(2)}, u32[]{:S(2)}) async-start(bf16[64,160,128]{2,1,0:T(8,128)(2,1)} %payload.1), calls=%async_computation.1 | async-start | bytes 5242880 | tf_op jit(solution)/shard_map/all_to_all | solution.py:309
  31.7 0.7 constant_dynamic-update-slice_fusion.7
  32.4 1.4 collective-permute-start
  33.8 2.7 %collective-permute-start.5 = (bf16[1,160,128]{2,1,0:T(8,128)(2,1)S(1)}, bf16[1,160,128]{2,1,0:T(8,128)(2,1)S(1)}, u32[]{:S(2)}, u32[]{:S(2)}) collective-permute-start(bf16[1,160,128]{2,1,0:T(8,128)(2,1)S(1)} %get-tuple-element.16), channel_id=1, source_target_pairs={{0,48},{1,49},{2,50},{3,51},{4,52},{5,53},{6,54},{7,55},{8,56},{9,... | collective-permute-start | bytes 122888 | tf_op jit(solution)/shard_map/ppermute | solution.py:38
  36.5 4.0 %collective-permute-start.4 = (bf16[1,160,128]{2,1,0:T(8,128)(2,1)S(1)}, bf16[1,160,128]{2,1,0:T(8,128)(2,1)S(1)}, u32[]{:S(2)}, u32[]{:S(2)}) collective-permute-start(bf16[1,160,128]{2,1,0:T(8,128)(2,1)S(1)} %get-tuple-element.16), channel_id=1, source_target_pairs={{0,40},{1,41},{2,42},{3,43},{4,44},{5,45},{6,46},{7,47},{8,48},{9,... | collective-permute-start | bytes 122888 | tf_op jit(solution)/shard_map/ppermute | solution.py:38
  40.7 1.8 %collective-permute-start.2 = (bf16[1,160,128]{2,1,0:T(8,128)(2,1)S(1)}, bf16[1,160,128]{2,1,0:T(8,128)(2,1)S(1)}, u32[]{:S(2)}, u32[]{:S(2)}) collective-permute-start(bf16[1,160,128]{2,1,0:T(8,128)(2,1)S(1)} %get-tuple-element.16), channel_id=1, source_target_pairs={{0,24},{1,25},{2,26},{3,27},{4,28},{5,29},{6,30},{7,31},{8,32},{9,... | collective-permute-start | bytes 122888 | tf_op jit(solution)/shard_map/ppermute | solution.py:38
  42.5 48.1 %collective-permute-done = bf16[1,160,128]{2,1,0:T(8,128)(2,1)S(1)} collective-permute-done((bf16[1,160,128]{2,1,0:T(8,128)(2,1)S(1)}, bf16[1,160,128]{2,1,0:T(8,128)(2,1)S(1)}, u32[]{:S(2)}, u32[]{:S(2)}) %collective-permute-start) | collective-permute-done | bytes 40992 | tf_op jit(solution)/shard_map/ppermute | solution.py:38
  90.7 1.4 collective-permute-start.1
  92.7 5.1 %collective-permute-done.1 = bf16[1,160,128]{2,1,0:T(8,128)(2,1)S(1)} collective-permute-done((bf16[1,160,128]{2,1,0:T(8,128)(2,1)S(1)}, bf16[1,160,128]{2,1,0:T(8,128)(2,1)S(1)}, u32[]{:S(2)}, u32[]{:S(2)}) %collective-permute-start.1) | collective-permute-done | bytes 40992 | tf_op jit(solution)/shard_map/ppermute | solution.py:38
  97.8 1.5 collective-permute-start.6
  103.0 2.6 %collective-permute-start.9 = (bf16[8,160,128]{2,1,0:T(8,128)(2,1)}, bf16[8,160,128]{2,1,0:T(8,128)(2,1)}, u32[]{:S(2)}, u32[]{:S(2)}) collective-permute-start(bf16[8,160,128]{2,1,0:T(8,128)(2,1)} %constant_dynamic-update-slice_fusion.rest_0_), channel_id=1, source_target_pairs={{0,6},{1,7},{2,0},{3,1},{4,2},{5,3},{6,4},{7,5},{8,14},{9,15},{10,... | collective-permute-start | bytes 983048 | tf_op jit(solution)/shard_map/ppermute | solution.py:38
  107.0 2.6 %collective-permute-start.10 = (bf16[8,160,128]{2,1,0:T(8,128)(2,1)}, bf16[8,160,128]{2,1,0:T(8,128)(2,1)S(1)}, u32[]{:S(2)}, u32[]{:S(2)}) collective-permute-start(bf16[8,160,128]{2,1,0:T(8,128)(2,1)} %constant_dynamic-update-slice_fusion.rest_0_), channel_id=1, source_target_pairs={{0,1},{1,0},{2,3},{3,2},{4,5},{5,4},{6,7},{7,6},{8,9},{9,8},{10,11... | collective-permute-start | bytes 983048 | tf_op jit(solution)/shard_map/ppermute | solution.py:38
  109.6 1.8 %collective-permute-done.9.rest_3_ = bf16[8,160,128]{2,1,0:T(8,128)(2,1)} collective-permute-done((bf16[8,160,128]{2,1,0:T(8,128)(2,1)}, bf16[8,160,128]{2,1,0:T(8,128)(2,1)}, u32[]{:S(2)}, u32[]{:S(2)}) %collective-permute-start.9) | collective-permute-done | bytes 327712 | tf_op jit(solution)/shard_map/ppermute | solution.py:38
  111.4 9.4 %collective-permute-start.13 = (bf16[8,160,128]{2,1,0:T(8,128)(2,1)}, bf16[8,160,128]{2,1,0:T(8,128)(2,1)S(1)}, u32[]{:S(2)}, u32[]{:S(2)}) collective-permute-start(bf16[8,160,128]{2,1,0:T(8,128)(2,1)} %collective-permute-done.9.rest_3_), channel_id=1, source_target_pairs={{0,1},{1,0},{2,3},{3,2},{4,5},{5,4},{6,7},{7,6},{8,9},{9,8},{10,11... | collective-permute-start | bytes 983048 | tf_op jit(solution)/shard_map/ppermute | solution.py:38
  120.8 3.2 %collective-permute-done.7.rest_1_ = bf16[8,160,128]{2,1,0:T(8,128)(2,1)} collective-permute-done((bf16[8,160,128]{2,1,0:T(8,128)(2,1)}, bf16[8,160,128]{2,1,0:T(8,128)(2,1)}, u32[]{:S(2)}, u32[]{:S(2)}) %collective-permute-start.7) | collective-permute-done | bytes 327712 | tf_op jit(solution)/shard_map/ppermute | solution.py:38
  124.6 1.4 collective-permute-done.11.rest_5_
  126.0 1.1 copy-done.2
  127.1 20.2 %coarse.1.coarse_ref = f32[16,128,128]{2,1,0:T(8,128)S(1)} custom-call(s32[19]{0:T(128)S(1)} %pad_add_fusion.info_ref, bf16[8,160,128]{2,1,0:T(8,128)(2,1)} %constant_dynamic-update-slice_fusion.rest_0_, bf16[8,160,128]{2,1,0:T(8,128)(2,1)} %collective-permute-done.7.rest_1_, bf16[8,160,128]{2,1,0:T(8,128)(2,1)} %collective-permute-done.8.rest_2_, ...), custom_call_target="tpu_custom_call" | custom-call | flops 5368709120 | bytes 4456448 | tf_op jit(solution)/shard_map/coarse/pallas_call | solution.py:136
  147.3 1.0 copy-done.1
  148.3 12.9 %tail.1 = (f32[128,640]{1,0:T(8,128)S(1)}, bf16[128,640]{1,0:T(8,128)(2,1)S(1)}, bf16[128,640]{1,0:T(8,128)(2,1)S(1)}, bf16[128,640]{1,0:T(8,128)(2,1)S(1)}) custom-call(s32[19]{0:T(128)S(1)} %pad_add_fusion.info_ref, bf16[64,160,128]{2,1,0:T(8,128)(2,1)S(1)} %all-to-all-done.1.incoming_ref, bf16[16,192,128]{2,1,0:T(8,128)(2,1)} %bitcast.22, ...), custom_call_target="tpu_custom_call" | custom-call | flops 2684354560 | bytes 10485760 | tf_op jit(solution)/shard_map/tail/pallas_call | solution.py:240
  161.2 1.4 collective-permute-start.14
  162.6 2.6 %collective-permute-start.15 = (bf16[128,640]{1,0:T(8,128)(2,1)S(1)}, bf16[128,640]{1,0:T(8,128)(2,1)S(1)}, u32[]{:S(2)}, u32[]{:S(2)}) collective-permute-start(bf16[128,640]{1,0:T(8,128)(2,1)S(1)} %get-tuple-element.13), channel_id=1, source_target_pairs={{0,128},{64,192},{128,0},{192,64},{1,129},{65,193},{129,1},{193,65... | collective-permute-start | bytes 491528 | tf_op jit(solution)/shard_map/ppermute | solution.py:324
  165.2 1.1 collective-permute-start.16
  166.3 1.8 %collective-permute-done.14 = bf16[128,640]{1,0:T(8,128)(2,1)S(1)} collective-permute-done((bf16[128,640]{1,0:T(8,128)(2,1)S(1)}, bf16[128,640]{1,0:T(8,128)(2,1)S(1)}, u32[]{:S(2)}, u32[]{:S(2)}) %collective-permute-start.14) | collective-permute-done | bytes 163872 | tf_op jit(solution)/shard_map/ppermute | solution.py:324
  168.1 4.6 %collective-permute-done.15 = bf16[128,640]{1,0:T(8,128)(2,1)S(1)} collective-permute-done((bf16[128,640]{1,0:T(8,128)(2,1)S(1)}, bf16[128,640]{1,0:T(8,128)(2,1)S(1)}, u32[]{:S(2)}, u32[]{:S(2)}) %collective-permute-start.15) | collective-permute-done | bytes 163872 | tf_op jit(solution)/shard_map/ppermute | solution.py:324
  172.7 0.8 add_convert_fusion
  (47 shorter events, 6.9 us)
Async XLA Ops:
  0.0 106.7 %copy-start = (bf16[128,2560]{1,0:T(8,128)(2,1)S(1)}, bf16[128,2560]{1,0:T(8,128)(2,1)}, u32[]{:S(2)}) copy-start(bf16[128,2560]{1,0:T(8,128)(2,1)} %param.14) | copy-start | bytes 1966084
  0.0 15.9 %copy-start.3 = (bf16[1,1024,128]{2,1,0:T(8,128)(2,1)S(1)}, bf16[1,1024,128]{2,1,0:T(8,128)(2,1)}, u32[]{:S(2)}) copy-start(bf16[1,1024,128]{2,1,0:T(8,128)(2,1)} %param.11) | copy-start | bytes 786436
  1.6 22.3 %all-to-all-start = ((s32[64,1,1]{2,1,0:T(1,128)}), s32[64,1,1]{2,1,0:T(1,128)S(1)}, u32[]{:S(2)}, u32[]{:S(2)}) async-start(s32[64,1,1]{2,1,0:T(1,128)} %copy.13), calls=%async_computation | async-start | bytes 65536 | tf_op jit(solution)/shard_map/all_to_all | solution.py:302
  26.6 5.0 %copy-start.5 = (bf16[1,64,192]{2,1,0:T(8,128)(2,1)S(1)}, bf16[1,64,192]{2,1,0:T(8,128)(2,1)}, u32[]{:S(2)}) copy-start(bf16[1,64,192]{2,1,0:T(8,128)(2,1)} %param.12) | copy-start | bytes 73732
  26.6 5.0 %slice-start = ((bf16[1,64,192]{2,1,0:T(8,128)(2,1)}), bf16[1,64,128]{2,1,0:T(8,128)(2,1)S(1)}, s32[]{:S(2)}) async-start(bf16[1,64,192]{2,1,0:T(8,128)(2,1)} %param.12), calls=%async_computation.2 | async-start | bytes 32768 | tf_op jit(solution)/shard_map/slice | solution.py:26
  26.6 5.0 %copy-start.6 = (bf16[1,64,128]{2,1,0:T(8,128)(2,1)S(1)}, bf16[1,64,128]{2,1,0:T(8,128)(2,1)}, u32[]{:S(2)}) copy-start(bf16[1,64,128]{2,1,0:T(8,128)(2,1)} %param.13) | copy-start | bytes 49156
  26.6 80.1 %copy-start.4 = (bf16[1,2560,32]{1,2,0:T(8,128)(2,1)S(1)}, bf16[1,2560,32]{1,2,0:T(8,128)(2,1)}, u32[]{:S(2)}) copy-start(bf16[1,2560,32]{1,2,0:T(8,128)(2,1)} %param.15) | copy-start | bytes 491524
  26.6 121.6 %all-to-all-start.1 = ((bf16[64,160,128]{2,1,0:T(8,128)(2,1)}), bf16[64,160,128]{2,1,0:T(8,128)(2,1)S(1)}, u32[]{:S(2)}, u32[]{:S(2)}) async-start(bf16[64,160,128]{2,1,0:T(8,128)(2,1)} %payload.1), calls=%async_computation.1 | async-start | bytes 5242880 | tf_op jit(solution)/shard_map/all_to_all | solution.py:309
  31.6 92.9 %copy-start.7 = (s32[1,1,16]{2,1,0:T(1,128)S(1)}, s32[1,1,16]{2,1,0:T(1,128)}, u32[]{:S(2)}) copy-start(s32[1,1,16]{2,1,0:T(1,128)} %param.17) | copy-start | bytes 196
  32.4 58.3 %collective-permute-start = (bf16[1,160,128]{2,1,0:T(8,128)(2,1)S(1)}, bf16[1,160,128]{2,1,0:T(8,128)(2,1)S(1)}, u32[]{:S(2)}, u32[]{:S(2)}) collective-permute-start(bf16[1,160,128]{2,1,0:T(8,128)(2,1)S(1)} %get-tuple-element.16), channel_id=1, source_target_pairs={{0,8},{1,9},{2,10},{3,11},{4,12},{5,13},{6,14},{7,15},{8,16},{9,17... | collective-permute-start | bytes 122888 | tf_op jit(solution)/shard_map/ppermute | solution.py:38
  33.8 68.0 %collective-permute-start.5 = (bf16[1,160,128]{2,1,0:T(8,128)(2,1)S(1)}, bf16[1,160,128]{2,1,0:T(8,128)(2,1)S(1)}, u32[]{:S(2)}, u32[]{:S(2)}) collective-permute-start(bf16[1,160,128]{2,1,0:T(8,128)(2,1)S(1)} %get-tuple-element.16), channel_id=1, source_target_pairs={{0,48},{1,49},{2,50},{3,51},{4,52},{5,53},{6,54},{7,55},{8,56},{9,... | collective-permute-start | bytes 122888 | tf_op jit(solution)/shard_map/ppermute | solution.py:38
  36.5 64.6 %collective-permute-start.4 = (bf16[1,160,128]{2,1,0:T(8,128)(2,1)S(1)}, bf16[1,160,128]{2,1,0:T(8,128)(2,1)S(1)}, u32[]{:S(2)}, u32[]{:S(2)}) collective-permute-start(bf16[1,160,128]{2,1,0:T(8,128)(2,1)S(1)} %get-tuple-element.16), channel_id=1, source_target_pairs={{0,40},{1,41},{2,42},{3,43},{4,44},{5,45},{6,46},{7,47},{8,48},{9,... | collective-permute-start | bytes 122888 | tf_op jit(solution)/shard_map/ppermute | solution.py:38
  40.5 60.0 %collective-permute-start.3 = (bf16[1,160,128]{2,1,0:T(8,128)(2,1)S(1)}, bf16[1,160,128]{2,1,0:T(8,128)(2,1)S(1)}, u32[]{:S(2)}, u32[]{:S(2)}) collective-permute-start(bf16[1,160,128]{2,1,0:T(8,128)(2,1)S(1)} %get-tuple-element.16), channel_id=1, source_target_pairs={{0,32},{1,33},{2,34},{3,35},{4,36},{5,37},{6,38},{7,39},{8,40},{9,... | collective-permute-start | bytes 122888 | tf_op jit(solution)/shard_map/ppermute | solution.py:38
  40.7 59.2 %collective-permute-start.2 = (bf16[1,160,128]{2,1,0:T(8,128)(2,1)S(1)}, bf16[1,160,128]{2,1,0:T(8,128)(2,1)S(1)}, u32[]{:S(2)}, u32[]{:S(2)}) collective-permute-start(bf16[1,160,128]{2,1,0:T(8,128)(2,1)S(1)} %get-tuple-element.16), channel_id=1, source_target_pairs={{0,24},{1,25},{2,26},{3,27},{4,28},{5,29},{6,30},{7,31},{8,32},{9,... | collective-permute-start | bytes 122888 | tf_op jit(solution)/shard_map/ppermute | solution.py:38
  90.7 7.1 %collective-permute-start.1 = (bf16[1,160,128]{2,1,0:T(8,128)(2,1)S(1)}, bf16[1,160,128]{2,1,0:T(8,128)(2,1)S(1)}, u32[]{:S(2)}, u32[]{:S(2)}) collective-permute-start(bf16[1,160,128]{2,1,0:T(8,128)(2,1)S(1)} %get-tuple-element.16), channel_id=1, source_target_pairs={{0,16},{1,17},{2,18},{3,19},{4,20},{5,21},{6,22},{7,23},{8,24},{9,... | collective-permute-start | bytes 122888 | tf_op jit(solution)/shard_map/ppermute | solution.py:38
  97.8 4.6 %collective-permute-start.6 = (bf16[1,160,128]{2,1,0:T(8,128)(2,1)S(1)}, bf16[1,160,128]{2,1,0:T(8,128)(2,1)S(1)}, u32[]{:S(2)}, u32[]{:S(2)}) collective-permute-start(bf16[1,160,128]{2,1,0:T(8,128)(2,1)S(1)} %get-tuple-element.16), channel_id=1, source_target_pairs={{0,56},{1,57},{2,58},{3,59},{4,60},{5,61},{6,62},{7,63},{8,0},{9,1... | collective-permute-start | bytes 122888 | tf_op jit(solution)/shard_map/ppermute | solution.py:38
  103.0 8.4 %collective-permute-start.9 = (bf16[8,160,128]{2,1,0:T(8,128)(2,1)}, bf16[8,160,128]{2,1,0:T(8,128)(2,1)}, u32[]{:S(2)}, u32[]{:S(2)}) collective-permute-start(bf16[8,160,128]{2,1,0:T(8,128)(2,1)} %constant_dynamic-update-slice_fusion.rest_0_), channel_id=1, source_target_pairs={{0,6},{1,7},{2,0},{3,1},{4,2},{5,3},{6,4},{7,5},{8,14},{9,15},{10,... | collective-permute-start | bytes 983048 | tf_op jit(solution)/shard_map/ppermute | solution.py:38
  105.6 15.3 %collective-permute-start.8 = (bf16[8,160,128]{2,1,0:T(8,128)(2,1)}, bf16[8,160,128]{2,1,0:T(8,128)(2,1)}, u32[]{:S(2)}, u32[]{:S(2)}) collective-permute-start(bf16[8,160,128]{2,1,0:T(8,128)(2,1)} %constant_dynamic-update-slice_fusion.rest_0_), channel_id=1, source_target_pairs={{0,4},{1,5},{2,6},{3,7},{4,0},{5,1},{6,2},{7,3},{8,12},{9,13},{10,... | collective-permute-start | bytes 983048 | tf_op jit(solution)/shard_map/ppermute | solution.py:38
  106.1 17.9 %collective-permute-start.7 = (bf16[8,160,128]{2,1,0:T(8,128)(2,1)}, bf16[8,160,128]{2,1,0:T(8,128)(2,1)}, u32[]{:S(2)}, u32[]{:S(2)}) collective-permute-start(bf16[8,160,128]{2,1,0:T(8,128)(2,1)} %constant_dynamic-update-slice_fusion.rest_0_), channel_id=1, source_target_pairs={{0,2},{1,3},{2,4},{3,5},{4,6},{5,7},{6,0},{7,1},{8,10},{9,11},{10,... | collective-permute-start | bytes 983048 | tf_op jit(solution)/shard_map/ppermute | solution.py:38
  107.0 17.6 %collective-permute-start.10 = (bf16[8,160,128]{2,1,0:T(8,128)(2,1)}, bf16[8,160,128]{2,1,0:T(8,128)(2,1)S(1)}, u32[]{:S(2)}, u32[]{:S(2)}) collective-permute-start(bf16[8,160,128]{2,1,0:T(8,128)(2,1)} %constant_dynamic-update-slice_fusion.rest_0_), channel_id=1, source_target_pairs={{0,1},{1,0},{2,3},{3,2},{4,5},{5,4},{6,7},{7,6},{8,9},{9,8},{10,11... | collective-permute-start | bytes 983048 | tf_op jit(solution)/shard_map/ppermute | solution.py:38
  111.4 13.2 %collective-permute-start.13 = (bf16[8,160,128]{2,1,0:T(8,128)(2,1)}, bf16[8,160,128]{2,1,0:T(8,128)(2,1)S(1)}, u32[]{:S(2)}, u32[]{:S(2)}) collective-permute-start(bf16[8,160,128]{2,1,0:T(8,128)(2,1)} %collective-permute-done.9.rest_3_), channel_id=1, source_target_pairs={{0,1},{1,0},{2,3},{3,2},{4,5},{5,4},{6,7},{7,6},{8,9},{9,8},{10,11... | collective-permute-start | bytes 983048 | tf_op jit(solution)/shard_map/ppermute | solution.py:38
  120.8 3.8 %collective-permute-start.12 = (bf16[8,160,128]{2,1,0:T(8,128)(2,1)}, bf16[8,160,128]{2,1,0:T(8,128)(2,1)S(1)}, u32[]{:S(2)}, u32[]{:S(2)}) collective-permute-start(bf16[8,160,128]{2,1,0:T(8,128)(2,1)} %collective-permute-done.8.rest_2_), channel_id=1, source_target_pairs={{0,1},{1,0},{2,3},{3,2},{4,5},{5,4},{6,7},{7,6},{8,9},{9,8},{10,11... | collective-permute-start | bytes 983048 | tf_op jit(solution)/shard_map/ppermute | solution.py:38
  124.0 2.0 %collective-permute-start.11 = (bf16[8,160,128]{2,1,0:T(8,128)(2,1)}, bf16[8,160,128]{2,1,0:T(8,128)(2,1)S(1)}, u32[]{:S(2)}, u32[]{:S(2)}) collective-permute-start(bf16[8,160,128]{2,1,0:T(8,128)(2,1)} %collective-permute-done.7.rest_1_), channel_id=1, source_target_pairs={{0,1},{1,0},{2,3},{3,2},{4,5},{5,4},{6,7},{7,6},{8,9},{9,8},{10,11... | collective-permute-start | bytes 983048 | tf_op jit(solution)/shard_map/ppermute | solution.py:38
  126.0 1.1 copy-start.2
  147.3 1.0 copy-start.1
  161.2 6.8 %collective-permute-start.14 = (bf16[128,640]{1,0:T(8,128)(2,1)S(1)}, bf16[128,640]{1,0:T(8,128)(2,1)S(1)}, u32[]{:S(2)}, u32[]{:S(2)}) collective-permute-start(bf16[128,640]{1,0:T(8,128)(2,1)S(1)} %get-tuple-element.12), channel_id=1, source_target_pairs={{0,64},{64,128},{128,192},{192,0},{1,65},{65,129},{129,193},{193,1... | collective-permute-start | bytes 491528 | tf_op jit(solution)/shard_map/ppermute | solution.py:324
  162.6 10.1 %collective-permute-start.15 = (bf16[128,640]{1,0:T(8,128)(2,1)S(1)}, bf16[128,640]{1,0:T(8,128)(2,1)S(1)}, u32[]{:S(2)}, u32[]{:S(2)}) collective-permute-start(bf16[128,640]{1,0:T(8,128)(2,1)S(1)} %get-tuple-element.13), channel_id=1, source_target_pairs={{0,128},{64,192},{128,0},{192,64},{1,129},{65,193},{129,1},{193,65... | collective-permute-start | bytes 491528 | tf_op jit(solution)/shard_map/ppermute | solution.py:324
  165.2 7.5 %collective-permute-start.16 = (bf16[128,640]{1,0:T(8,128)(2,1)S(1)}, bf16[128,640]{1,0:T(8,128)(2,1)S(1)}, u32[]{:S(2)}, u32[]{:S(2)}) collective-permute-start(bf16[128,640]{1,0:T(8,128)(2,1)S(1)} %get-tuple-element.14), channel_id=1, source_target_pairs={{0,192},{64,0},{128,64},{192,128},{1,193},{65,1},{129,65},{193,129... | collective-permute-start | bytes 491528 | tf_op jit(solution)/shard_map/ppermute | solution.py:324

commit v3 on v1

--- a/solution.py
+++ b/solution.py
@@ -16,6 +16,7 @@
 DQK = 192
 DV = 128
 PACK = BLK + BLK + BLK // 2
+PADDED = 512
 NEGATIVE = -1e30
 EXP_SCALE = DQK**-0.5 * math.log2(math.e)
 Z, X, C = 8, 4, 2
@@ -31,25 +32,18 @@
     return jnp.concatenate([block[:BLK], high], axis=1)
 
 
-def copies_for(x, groups):
-    peers = len(groups[0])
-    return lax.all_to_all(
-        jnp.broadcast_to(x[None], (peers, *x.shape)), "seq", 0, 0, axis_index_groups=groups, tiled=True
-    )
-
-
-def everywhere(block):
+def everywhere(block, after):
     along_z = [[(z * X + x) * C + c for z in range(Z)] for x in range(X) for c in range(C)]
-    along_x = [[(z * X + x) * C + c for x in range(X)] for z in range(Z) for c in range(C)]
-    along_c = [[(z * X + x) * C + c for c in range(C)] for z in range(Z) for x in range(X)]
-    block = copies_for(block, along_z)
-    block = copies_for(block, along_x)
-    return copies_for(block, along_c).reshape(C * X * Z, PACK, DV)
+    in_plane = [[(z * X + x) * C + c for x in range(X) for c in range(C)] for z in range(Z)]
+    padded = jnp.pad(block, ((0, 0), (0, PADDED - PACK), (0, 0)))
+    columns = lax.all_gather(padded, "seq", axis=0, tiled=True, axis_index_groups=along_z)
+    columns, _ = lax.optimization_barrier((columns, after))
+    return lax.all_gather(columns[:, :PACK], "seq", axis=0, tiled=True, axis_index_groups=in_plane)
 
 
 def payload_kernel(wanted_ref, blocks_ref, out_ref):
     def one(t, carry):
-        out_ref[t] = blocks_ref[wanted_ref[t]]
+        out_ref[t] = blocks_ref[wanted_ref[t, 0, 0]]
         return carry
 
     lax.fori_loop(0, out_ref.shape[0], one, 0, unroll=8)
@@ -73,16 +67,18 @@
     )(wanted, blocks)
 
 
-def coarse_kernel(info_ref, kv_ref, q_ref, gate_ref, out_ref, keys, values_t, scores):
-    n_chunks = C * X
+def coarse_kernel(
+    info_ref, kv_ref, q_ref, gate_ref, out_ref, keys, values_t, scores
+):
+    n_chunks = X * C
     rows = Z * BLK
 
     @pl.when(pl.program_id(0) == 0)
     def _():
         def one(n, carry):
             at = pl.multiple_of(n * 2 * BLK, 2 * BLK)
-            keys[pl.ds(at, BLK), :] = unpacked_keys(kv_ref[2 * n])
-            keys[pl.ds(at + BLK, BLK), :] = unpacked_keys(kv_ref[2 * n + 1])
+            keys[pl.ds(at, BLK), :] = unpacked_keys(kv_ref.at[2 * n])
+            keys[pl.ds(at + BLK, BLK), :] = unpacked_keys(kv_ref.at[2 * n + 1])
             v = jnp.concatenate([kv_ref[2 * n, BLK : 2 * BLK], kv_ref[2 * n + 1, BLK : 2 * BLK]], axis=0)
             values_t[:, pl.ds(at, 2 * BLK)] = v.T
             return carry
@@ -94,15 +90,12 @@
     late = 2 * BLK
     row = lax.broadcasted_iota(jnp.int32, (late, width), 0)
     lane = lax.broadcasted_iota(jnp.int32, (late, width), 1)
-    z = Z - 2 + row // BLK
-    token0 = z * (X * C * BLK) + row % BLK
+    token0 = (Z - 2 + row // BLK) * (X * C * BLK) + row % BLK
     query_pos = info_ref[0] + lane % TILE
     top = jnp.full((1, width), NEGATIVE, jnp.float32)
     for n in range(n_chunks):
-        c, x = divmod(n, X)
         s = jnp.dot(keys[n * rows : (n + 1) * rows, :], q, preferred_element_type=jnp.float32)
-        token = token0 + (x * C + c) * BLK
-        tail = jnp.where(token * CSTRIDE + CLEN - 1 <= query_pos, s[rows - late :], NEGATIVE)
+        tail = jnp.where((token0 + n * BLK) * CSTRIDE + CLEN - 1 <= query_pos, s[rows - late :], NEGATIVE)
         scores[n * rows : (n + 1) * rows - late, :] = s[: rows - late]
         scores[(n + 1) * rows - late : (n + 1) * rows, :] = tail
         top = jnp.maximum(top, jnp.max(s[: rows - late], axis=0, keepdims=True))
@@ -119,6 +112,10 @@
     acc = acc * (gate / total)
     out_ref[0] = acc[:, :TILE]
     out_ref[1] = acc[:, TILE:]
+
+
+def in_hbm(x):
+    return pltpu.with_memory_space_constraint(x, pltpu.HBM)
 
 
 def coarse_branch(info, coarse, queries_t, gate):
@@ -148,28 +145,35 @@
             bytes_accessed=tokens * (DQK + DV) * 2 + heads * TILE * (DQK * 2 + DV * 4),
             transcendentals=heads * TILE * tokens,
         ),
-        compiler_params=pltpu.CompilerParams(vmem_limit_bytes=24 << 20),
+        compiler_params=pltpu.CompilerParams(vmem_limit_bytes=20 << 20),
         name="coarse",
     )(info, coarse, queries_t, gate)
 
 
-def tail_kernel(
-    n_grp, info_ref, incoming_ref, q_ref, gate_ref, coarse_ref, weight_ref, *rest
-):
-    outs, (blocks, keys, values_t, scores, attended, weight, block_sem, weight_sem) = rest[:n_grp], rest[n_grp:]
-    heads = q_ref.shape[0]
+def tail_kernel(n_grp, info_ref, incoming, q_ref, gate_ref, coarse_ref, weight_ref, *rest):
+    outs, (queries, coarse, weight, keys, values_t, attended, in_sem, weight_sem) = rest[:n_grp], rest[n_grp:]
+    heads = queries.shape[0]
     cols = weight.shape[2]
     base, grp = info_ref[0], info_ref[1]
+    q_copy = pltpu.make_async_copy(q_ref, queries, in_sem.at[0])
+    coarse_copy = pltpu.make_async_copy(coarse_ref, coarse, in_sem.at[1])
+    q_copy.start()
+    coarse_copy.start()
     late = SEL - 1
     for j in range(SEL):
-        late = jnp.where(info_ref[2 + j] * BLK >= base, j, late)
-    copies = []
+        late = jnp.where(info_ref[3 + j] * BLK >= base, j, late)
+    owners = []
     for j in range(SEL):
         slot_from = jnp.where(late == j, SEL - 1, j) if j < SEL - 1 else late
-        owner = info_ref[2 + slot_from] // (1024 // BLK)
-        copies.append(pltpu.make_async_copy(incoming_ref.at[owner], blocks.at[j], block_sem.at[j]))
-    for copy in copies:
-        copy.start()
+        owners.append(info_ref[3 + slot_from] // (1024 // BLK))
+    for j in range(0, SEL, 2):
+        first, second = incoming.at[owners[j]], incoming.at[owners[j + 1]]
+        keys[j * BLK : (j + 1) * BLK, :] = unpacked_keys(first)
+        keys[(j + 1) * BLK : (j + 2) * BLK, :] = unpacked_keys(second)
+        v = jnp.concatenate([first[BLK : 2 * BLK], second[BLK : 2 * BLK]], axis=0)
+        values_t[:, j * BLK : (j + 2) * BLK] = v.T
+    q_copy.wait()
+    coarse_copy.wait()
     weight_copies = []
     for k in range(n_grp):
         at = pl.multiple_of(lax.rem(grp + k, n_grp) * cols, DV)
@@ -178,21 +182,14 @@
         )
     for copy in weight_copies:
         copy.start()
-    for j in range(0, SEL, 2):
-        copies[j].wait()
-        copies[j + 1].wait()
-        keys[j * BLK : (j + 1) * BLK, :] = unpacked_keys(blocks[j])
-        keys[(j + 1) * BLK : (j + 2) * BLK, :] = unpacked_keys(blocks[j + 1])
-        v = jnp.concatenate([blocks[j, BLK : 2 * BLK], blocks[j + 1, BLK : 2 * BLK]], axis=0)
-        values_t[:, j * BLK : (j + 2) * BLK] = v.T
     width = 2 * TILE
     n_keys = SEL * BLK
     row = lax.broadcasted_iota(jnp.int32, (BLK, width), 0)
     lane = lax.broadcasted_iota(jnp.int32, (BLK, width), 1)
-    seen = info_ref[2 + late] * BLK + row <= base + lane % TILE
+    seen = info_ref[3 + late] * BLK + row <= base + lane % TILE
 
     for p in range(heads // 2):
-        q = jnp.concatenate([q_ref[2 * p], q_ref[2 * p + 1]], axis=1)
+        q = jnp.concatenate([queries[2 * p], queries[2 * p + 1]], axis=1)
         s = jnp.dot(keys[...], q, preferred_element_type=jnp.float32)
         last = jnp.where(seen, s[n_keys - BLK :], NEGATIVE)
         top = jnp.maximum(
@@ -205,11 +202,10 @@
         o = o * (gate / total)
         for i in range(2):
             h = 2 * p + i
-            both = o[:, i * TILE : (i + 1) * TILE] + coarse_ref[h]
+            both = o[:, i * TILE : (i + 1) * TILE] + coarse[h]
             attended[:, h * DV : (h + 1) * DV] = both.T.astype(jnp.bfloat16)
-    for k in range(n_grp):
+    for k in (*range(1, n_grp), 0):
         weight_copies[k].wait()
-    for k in range(n_grp):
         part = jnp.dot(attended[...], weight[k], preferred_element_type=jnp.float32)
         outs[k][...] = part.astype(outs[k].dtype)
 
@@ -219,28 +215,29 @@
     rows, model = out_weight.shape
     cols = model // n_grp
     vmem = lambda shape: pl.BlockSpec(shape, lambda i, s: (0,) * len(shape))
-    anywhere = pl.BlockSpec(memory_space=pl.ANY)
+    on_chip = pl.BlockSpec(memory_space=pltpu.VMEM)
+    hbm = pl.BlockSpec(memory_space=pltpu.HBM)
     return pl.pallas_call(
         functools.partial(tail_kernel, n_grp),
         grid_spec=pltpu.PrefetchScalarGridSpec(
             num_scalar_prefetch=1,
             grid=(1,),
             in_specs=[
-                anywhere,
-                vmem(queries_t.shape),
+                on_chip,
+                hbm,
                 vmem(gate.shape),
-                vmem(coarse_out.shape),
-                anywhere,
+                hbm,
+                hbm,
             ],
             out_specs=[vmem((TILE, cols))] * n_grp,
             scratch_shapes=[
-                pltpu.VMEM((SEL, PACK, DV), jnp.bfloat16),
+                pltpu.VMEM(queries_t.shape, queries_t.dtype),
+                pltpu.VMEM(coarse_out.shape, coarse_out.dtype),
+                pltpu.VMEM((n_grp, rows, cols), jnp.bfloat16),
                 pltpu.VMEM((SEL * BLK, DQK), jnp.bfloat16),
                 pltpu.VMEM((DV, SEL * BLK), jnp.bfloat16),
-                pltpu.VMEM((SEL * BLK, 2 * TILE), jnp.float32),
                 pltpu.VMEM((TILE, rows), jnp.bfloat16),
-                pltpu.VMEM((n_grp, rows, cols), jnp.bfloat16),
-                pltpu.SemaphoreType.DMA((SEL,)),
+                pltpu.SemaphoreType.DMA((2,)),
                 pltpu.SemaphoreType.DMA((n_grp,)),
             ],
         ),
@@ -251,9 +248,9 @@
             bytes_accessed=rows * model * 2,
             transcendentals=heads * TILE * SEL * BLK,
         ),
-        compiler_params=pltpu.CompilerParams(vmem_limit_bytes=40 << 20),
+        compiler_params=pltpu.CompilerParams(vmem_limit_bytes=24 << 20),
         name="tail",
-    )(info, incoming, queries_t, gate, coarse_out, out_weight)
+    )(info, incoming, in_hbm(queries_t), gate, in_hbm(coarse_out), in_hbm(out_weight))
 
 
 def shards(
@@ -280,18 +277,18 @@
     owners = jnp.arange(seq_count, dtype=jnp.int32)
     mine = (own_list[None, :] // blocks_dev == owners[:, None]).astype(jnp.int32)
     wanted = jnp.sum(mine * (own_list % blocks_dev)[None, :], axis=1)
-    wanted = jnp.broadcast_to(wanted[:, None, None], (seq_count, 1, SEL))
-    wanted = lax.all_to_all(wanted, "seq", 0, 0, tiled=True)[:, 0, 0]
+    wanted = lax.all_to_all(wanted[:, None, None], "seq", 0, 0, tiled=True)
 
     blocks = packed_blocks(
         key_cache[0].reshape(blocks_dev, BLK, DQK), group_value_cache[0].reshape(blocks_dev, BLK, DV)
     )
-    incoming = lax.all_to_all(payload(wanted, blocks), "seq", 0, 0, tiled=True)
-
-    coarse = everywhere(packed_blocks(coarse_keys, coarse_values))
-
-    first_pos = context - TILE * seq_count + seq_index * TILE
-    info = jnp.concatenate([jnp.stack([first_pos, grp_index]).astype(jnp.int32), own_list])
+    outgoing = payload(wanted, blocks)
+    coarse = everywhere(packed_blocks(coarse_keys, coarse_values), outgoing)
+    incoming = lax.all_to_all(outgoing, "seq", 0, 0, tiled=True)
+
+    first_query = context - TILE * seq_count
+    first_pos = first_query + seq_index * TILE
+    info = jnp.concatenate([jnp.stack([first_pos, grp_index, seq_index]).astype(jnp.int32), own_list])
     queries_t = jnp.transpose(queries, (1, 2, 0))
     gates = jax.nn.sigmoid(
         lax.dot_general(

time: 160 us -> 151 us (0.944)
  blocking collectives: 23.9 us -> 0 us
  between operations: 0.16 us -> 13.5 us
  waiting for transfers between devices: 63.4 us -> 68.2 us
  Pallas kernels: 29.5 us -> 33.1 us
  starting transfers between devices: 26.4 us -> 23 us
  local copies, waits for them, and re-layouts: 12.3 us -> 9.09 us
    all_gather x0 -> x2, waiting for transfers between devices: none -> 53.9 us  [the longest x1 43.7 us: everywhere(): lax.all_gather(columns[:, :PACK], 'seq', axis=0, tiled=True, axis_index_g...]
    all_to_all x3 -> x2, waiting for transfers between devices: 58.7 us -> 8.04 us  [the longest x1 8.04 us: shards(): wanted = lax.all_to_all(wanted[:, None, None], 'seq', 0, 0, tiled=True)]
    all_to_all x2 -> x0, blocking collectives: 23.9 us -> none  [copies_for(): lax.all_to_all(jnp.broadcast_to(x[None], (peers, *x.shape)), 'seq', 0, 0,...]
    all_to_all x3 -> x2, starting transfers between devices: 21.3 us -> 17.9 us  [the longest x1 13 us: shards(): wanted = lax.all_to_all(wanted[:, None, None], 'seq', 0, 0, tiled=True)]
    pallas_call x1, Pallas kernels: 9.79 us -> 12.9 us  [tail(): pl.pallas_call(functools.partial(tail_kernel, n_grp), grid_spec=pltpu.Pre...]
    unnamed x21 -> x15, local copies, waits for them, and re-layouts: 7.02 us -> 5.04 us
    broadcast_in_dim x4 -> x1, local copies, waits for them, and re-layouts: 2.47 us -> 0.7 us  [shards(): wanted = lax.all_to_all(wanted[:, None, None], 'seq', 0, 0, tiled=True)]
  transfers between devices with their start and end apart: 6 -> 7, of which waited for: 5 -> 5; matrix products, arithmetic and copies ran while one was open for 3% -> 3% of each run, Pallas kernels for 12% -> 13%
where the time goes in v3:
time: 151 us; the launch traced here: 150 us
  waiting for transfers between devices  68.2 us (45%)
  Pallas kernels  33.1 us (22%)
  starting transfers between devices  23 us (15%)
  between operations  13.5 us (9%)
  local copies, waits for them, and re-layouts  9.09 us (6%)
  other arithmetic  3.15 us (2%)
    all_gather x1, waiting for transfers between devices, everywhere(): lax.all_gather(columns[:, :PACK], 'seq', axis=0, tiled=True, axis_index_g...  43.7 us
    pallas_call x1, Pallas kernels, coarse_branch(): pl.pallas_call(coarse_kernel, grid_spec=pltpu.PrefetchScalarGridSpec(num_...  17.4 us
    all_to_all x1, starting transfers between devices, shards(): wanted = lax.all_to_all(wanted[:, None, None], 'seq', 0, 0, tiled=True)  13 us
    pallas_call x1, Pallas kernels, tail(): pl.pallas_call(functools.partial(tail_kernel, n_grp), grid_spec=pltpu.Pre...  12.9 us
    all_gather x1, waiting for transfers between devices, everywhere(): lax.all_gather(padded, 'seq', axis=0, tiled=True, axis_index_groups=along_z)  10.2 us
    all_to_all x1, waiting for transfers between devices, shards(): wanted = lax.all_to_all(wanted[:, None, None], 'seq', 0, 0, tiled=True)  8.04 us
    ppermute x3, waiting for transfers between devices, shards(): own = own + lax.ppermute(part, 'grp', perm).astype(jnp.float32)  6.26 us
    unnamed x15, local copies, waits for them, and re-layouts  5.04 us
  transfers between devices with their start and end apart: 7, of which 5 were waited for; matrix products, arithmetic and copies ran while one was open for 3% of the time, Pallas kernels for 13%

profile of v3, /device:TPU:1, one launch (start us, length us, event | category | flops | bytes accessed | tf_op | source)
XLA Modules:
  0.0 150.3 jit_solution(10943759994208905554)
XLA Ops:
  6.5 0.8 slice.38
  7.3 0.7 fusion.12
  8.1 1.5 fusion.9
  9.5 0.0 all-gather.3.cloned.1.call-update
  9.5 0.7 and_select_fusion.1
  10.2 0.1 select_reduce_fusion
  10.3 0.7 copy.16
  11.0 13.0 %all-to-all-start = ((s32[64,1,1]{2,1,0:T(1,128)}), s32[64,1,1]{2,1,0:T(1,128)S(1)}, u32[]{:S(2)}, u32[]{:S(2)}) async-start(s32[64,1,1]{2,1,0:T(1,128)} %copy.16), calls=%async_computation | async-start | bytes 65536 | tf_op jit(solution)/shard_map/all_to_all | solution.py:280
  24.0 1.2 copy.17
  25.2 0.1 fusion.11
  25.3 0.1 maximum_maximum_fusion.blocks_ref
  25.4 8.0 %all-to-all-done.wanted_ref = s32[64,1,1]{2,1,0:T(1,128)S(1)} async-done(((s32[64,1,1]{2,1,0:T(1,128)}), s32[64,1,1]{2,1,0:T(1,128)S(1)}, u32[]{:S(2)}, u32[]{:S(2)}) %all-to-all-start) | async-done | bytes 288 | tf_op jit(solution)/shard_map/all_to_all | solution.py:280
  33.5 2.8 %payload.1 = bf16[64,160,128]{2,1,0:T(8,128)(2,1)} custom-call(s32[64,1,1]{2,1,0:T(1,128)S(1)} %all-to-all-done.wanted_ref, bf16[16,160,128]{2,1,0:T(8,128)(2,1)S(1)} %maximum_maximum_fusion.blocks_ref), custom_call_target="tpu_custom_call" | custom-call | bytes 5242880 | tf_op jit(solution)/shard_map/payload/pallas_call | solution.py:55
  36.3 4.9 %all-to-all-start.1 = ((bf16[64,160,128]{2,1,0:T(8,128)(2,1)}), bf16[64,160,128]{2,1,0:T(8,128)(2,1)S(1)}, u32[]{:S(2)}, u32[]{:S(2)}) async-start(bf16[64,160,128]{2,1,0:T(8,128)(2,1)} %payload.1), calls=%async_computation.1 | async-start | bytes 5242880 | tf_op jit(solution)/shard_map/all_to_all | solution.py:287
  41.2 0.0 all-gather.5.cloned.1.call-start
  41.3 10.2 %all-gather.3.cloned.1.call-done = bf16[8,512,128]{2,1,0:T(8,128)(2,1)} async-done(((bf16[1,512,128]{2,1,0:T(8,128)(2,1)}), bf16[8,512,128]{2,1,0:T(8,128)(2,1)}) %all-gather.3.cloned.1.call-update) | async-done | bytes 1048592 | tf_op jit(solution)/shard_map/all_gather | solution.py:39
  51.4 1.7 %slice.41 = bf16[8,160,128]{2,1,0:T(8,128)(2,1)} slice(bf16[8,512,128]{2,1,0:T(8,128)(2,1)} %all-gather.3.cloned.1.call-done), slice={[0:8], [0:160], [0:128]} | slice | bytes 655360 | tf_op jit(solution)/shard_map/slice | solution.py:41
  53.1 0.0 all-gather.5.cloned.1.call-update
  53.2 0.1 pad_add_fusion.info_ref
  53.3 0.3 fusion.2
  53.6 43.7 %all-gather.5.cloned.1.call-done.kv_ref = bf16[64,160,128]{2,1,0:T(8,128)(2,1)} async-done(((bf16[8,160,128]{2,1,0:T(8,128)(2,1)}), bf16[64,160,128]{2,1,0:T(8,128)(2,1)}) %all-gather.5.cloned.1.call-update) | async-done | bytes 2621456 | tf_op jit(solution)/shard_map/all_gather | solution.py:41
  97.3 1.1 copy-done.2
  98.5 1.7 %copy-done.3 = bf16[64,160,128]{2,1,0:T(8,128)(2,1)S(1)} copy-done((bf16[64,160,128]{2,1,0:T(8,128)(2,1)S(1)}, bf16[64,160,128]{2,1,0:T(8,128)(2,1)}, u32[]{:S(2)}) %copy-start.3) | copy-done | bytes 2621464
  100.2 17.4 %coarse.1.coarse_ref = f32[16,128,128]{2,1,0:T(8,128)S(1)} custom-call(s32[19]{0:T(128)S(1)} %pad_add_fusion.info_ref, bf16[64,160,128]{2,1,0:T(8,128)(2,1)S(1)} %copy-done.3, bf16[16,192,128]{2,1,0:T(8,128)(2,1)S(1)} %bitcast.23, f32[16,1,128]{2,1,0:T(1,128)S(1)} %bitcast.25), custom_call_target="tpu_custom_call" | custom-call | flops 5368709120 | bytes 4456448 | tf_op jit(solution)/shard_map/coarse/pallas_call | solution.py:125
  117.6 1.0 copy-done.1
  118.5 12.9 %tail.1 = (f32[128,640]{1,0:T(8,128)S(1)}, bf16[128,640]{1,0:T(8,128)(2,1)S(1)}, bf16[128,640]{1,0:T(8,128)(2,1)S(1)}, bf16[128,640]{1,0:T(8,128)(2,1)S(1)}) custom-call(s32[19]{0:T(128)S(1)} %pad_add_fusion.info_ref, bf16[64,160,128]{2,1,0:T(8,128)(2,1)S(1)} %all-to-all-done.1.incoming, bf16[16,192,128]{2,1,0:T(8,128)(2,1)} %bitcast.22, ...), custom_call_target="tpu_custom_call" | custom-call | flops 2684354560 | bytes 10485760 | tf_op jit(solution)/shard_map/tail/pallas_call | solution.py:220
  131.5 1.2 collective-permute-start
  132.6 2.5 %collective-permute-start.1 = (bf16[128,640]{1,0:T(8,128)(2,1)S(1)}, bf16[128,640]{1,0:T(8,128)(2,1)S(1)}, u32[]{:S(2)}, u32[]{:S(2)}) collective-permute-start(bf16[128,640]{1,0:T(8,128)(2,1)S(1)} %get-tuple-element.13), channel_id=1, source_target_pairs={{0,128},{64,192},{128,0},{192,64},{1,129},{65,193},{129,1},{193,65... | collective-permute-start | bytes 491528 | tf_op jit(solution)/shard_map/ppermute | solution.py:302
  135.1 1.3 collective-permute-start.2
  136.4 1.8 %collective-permute-done = bf16[128,640]{1,0:T(8,128)(2,1)S(1)} collective-permute-done((bf16[128,640]{1,0:T(8,128)(2,1)S(1)}, bf16[128,640]{1,0:T(8,128)(2,1)S(1)}, u32[]{:S(2)}, u32[]{:S(2)}) %collective-permute-start) | collective-permute-done | bytes 163872 | tf_op jit(solution)/shard_map/ppermute | solution.py:302
  138.3 4.4 %collective-permute-done.1 = bf16[128,640]{1,0:T(8,128)(2,1)S(1)} collective-permute-done((bf16[128,640]{1,0:T(8,128)(2,1)S(1)}, bf16[128,640]{1,0:T(8,128)(2,1)S(1)}, u32[]{:S(2)}, u32[]{:S(2)}) %collective-permute-start.1) | collective-permute-done | bytes 163872 | tf_op jit(solution)/shard_map/ppermute | solution.py:302
  142.7 0.8 add_convert_fusion
  (16 shorter events, 0.1 us)
Async XLA Ops:
  6.5 46.7 %copy-start = (bf16[128,2560]{1,0:T(8,128)(2,1)S(1)}, bf16[128,2560]{1,0:T(8,128)(2,1)}, u32[]{:S(2)}) copy-start(bf16[128,2560]{1,0:T(8,128)(2,1)} %param.14) | copy-start | bytes 1966084
  6.5 18.8 %copy-start.4 = (bf16[1,1024,128]{2,1,0:T(8,128)(2,1)S(1)}, bf16[1,1024,128]{2,1,0:T(8,128)(2,1)}, u32[]{:S(2)}) copy-start(bf16[1,1024,128]{2,1,0:T(8,128)(2,1)} %param.11) | copy-start | bytes 786436
  6.5 44.9 %all-gather.3.cloned.1.call-start = ((), (), s32[]{:S(2)}) async-start(), calls=%async_computation.2 | async-start | bytes 1179648 | tf_op jit(solution)/shard_map/all_gather | solution.py:39
  11.0 22.5 %all-to-all-start = ((s32[64,1,1]{2,1,0:T(1,128)}), s32[64,1,1]{2,1,0:T(1,128)S(1)}, u32[]{:S(2)}, u32[]{:S(2)}) async-start(s32[64,1,1]{2,1,0:T(1,128)} %copy.16), calls=%async_computation | async-start | bytes 65536 | tf_op jit(solution)/shard_map/all_to_all | solution.py:280
  36.3 16.9 %copy-start.6 = (s32[1,1,16]{2,1,0:T(1,128)S(1)}, s32[1,1,16]{2,1,0:T(1,128)}, u32[]{:S(2)}) copy-start(s32[1,1,16]{2,1,0:T(1,128)} %param.17) | copy-start | bytes 196
  36.3 17.0 %copy-start.5 = (bf16[1,2560,32]{1,2,0:T(8,128)(2,1)S(1)}, bf16[1,2560,32]{1,2,0:T(8,128)(2,1)}, u32[]{:S(2)}) copy-start(bf16[1,2560,32]{1,2,0:T(8,128)(2,1)} %param.15) | copy-start | bytes 491524
  36.3 82.3 %all-to-all-start.1 = ((bf16[64,160,128]{2,1,0:T(8,128)(2,1)}), bf16[64,160,128]{2,1,0:T(8,128)(2,1)S(1)}, u32[]{:S(2)}, u32[]{:S(2)}) async-start(bf16[64,160,128]{2,1,0:T(8,128)(2,1)} %payload.1), calls=%async_computation.1 | async-start | bytes 5242880 | tf_op jit(solution)/shard_map/all_to_all | solution.py:287
  41.2 56.1 %all-gather.5.cloned.1.call-start = ((), (), s32[]{:S(2)}) async-start(), calls=%async_computation.3 | async-start | bytes 2949120 | tf_op jit(solution)/shard_map/all_gather | solution.py:41
  97.3 1.1 copy-start.2
  98.5 1.7 %copy-start.3 = (bf16[64,160,128]{2,1,0:T(8,128)(2,1)S(1)}, bf16[64,160,128]{2,1,0:T(8,128)(2,1)}, u32[]{:S(2)}) copy-start(bf16[64,160,128]{2,1,0:T(8,128)(2,1)} %all-gather.5.cloned.1.call-done.kv_ref) | copy-start | bytes 7864324
  117.6 1.0 copy-start.1
  131.5 6.8 %collective-permute-start = (bf16[128,640]{1,0:T(8,128)(2,1)S(1)}, bf16[128,640]{1,0:T(8,128)(2,1)S(1)}, u32[]{:S(2)}, u32[]{:S(2)}) collective-permute-start(bf16[128,640]{1,0:T(8,128)(2,1)S(1)} %get-tuple-element.12), channel_id=1, source_target_pairs={{0,64},{64,128},{128,192},{192,0},{1,65},{65,129},{129,193},{193,1... | collective-permute-start | bytes 491528 | tf_op jit(solution)/shard_map/ppermute | solution.py:302
  132.6 10.1 %collective-permute-start.1 = (bf16[128,640]{1,0:T(8,128)(2,1)S(1)}, bf16[128,640]{1,0:T(8,128)(2,1)S(1)}, u32[]{:S(2)}, u32[]{:S(2)}) collective-permute-start(bf16[128,640]{1,0:T(8,128)(2,1)S(1)} %get-tuple-element.13), channel_id=1, source_target_pairs={{0,128},{64,192},{128,0},{192,64},{1,129},{65,193},{129,1},{193,65... | collective-permute-start | bytes 491528 | tf_op jit(solution)/shard_map/ppermute | solution.py:302
  135.1 7.6 %collective-permute-start.2 = (bf16[128,640]{1,0:T(8,128)(2,1)S(1)}, bf16[128,640]{1,0:T(8,128)(2,1)S(1)}, u32[]{:S(2)}, u32[]{:S(2)}) collective-permute-start(bf16[128,640]{1,0:T(8,128)(2,1)S(1)} %get-tuple-element.14), channel_id=1, source_target_pairs={{0,192},{64,0},{128,64},{192,128},{1,193},{65,1},{129,65},{193,129... | collective-permute-start | bytes 491528 | tf_op jit(solution)/shard_map/ppermute | solution.py:302
Sparse Core Ops, SparseCore 0:
  9.7 41.7 all-gather.2
  53.3 43.9 all-gather.4

commit v4 on v3

v4 whole, which is shorter than its diff:
```python
import functools
import math

import jax
import jax.numpy as jnp
from jax import lax
from jax.experimental import pallas as pl
from jax.experimental.pallas import tpu as pltpu
from jax.sharding import PartitionSpec as P

BLK = 64
SEL = 16
TILE = 128
CSTRIDE = 16
CLEN = 32
DQK = 192
DV = 128
PACK = BLK + BLK + BLK // 2
LETTER = PACK + 8
OWNED = 16
EARLY = 16
NEGATIVE = -1e30
EXP_SCALE = DQK**-0.5 * math.log2(math.e)
Z, X, C = 8, 4, 2


def packed_blocks(keys, values):
    high = jnp.concatenate([keys[:, : BLK // 2, DV:], keys[:, BLK // 2 :, DV:]], axis=2)
    return jnp.concatenate([keys[:, :, :DV], values, high], axis=1)


def unpacked_keys(block):
    high = jnp.concatenate([block[2 * BLK : PACK, :BLK], block[2 * BLK : PACK, BLK:]], axis=0)
    return jnp.concatenate([block[:BLK], high], axis=1)


def index(z, x, c):
    return ((z % Z) * X + x % X) * C + c % C


SITES = [(z, x, c) for z in range(Z) for x in range(X) for c in range(C)]
ALONG_Z = [[index(z, x, c) for z in range(Z)] for x in range(X) for c in range(C)]
IN_PLANE = [[index(z, x, c) for x in range(X) for c in range(C)] for z in range(Z)]


def shifted(x, dx, dc):
    return lax.ppermute(x, "seq", [(index(*s), index(s[0], s[1] + dx, s[2] + dc)) for s in SITES])


def letter_kernel(list_ref, keys_ref, values_ref, out_ref):
    keys = keys_ref[0]
    high = jnp.concatenate([keys[: BLK // 2, DV:], keys[BLK // 2 :, DV:]], axis=1)
    lane = lax.broadcasted_iota(jnp.int32, (LETTER - PACK, DV), 1)
    for z in range(Z):
        out_ref[z, :BLK] = keys[:, :DV]
        out_ref[z, BLK : 2 * BLK] = values_ref[0]
        out_ref[z, 2 * BLK : PACK] = high
        wanted = jnp.zeros(lane.shape, jnp.float32)
        for j in range(SEL):
            block = list_ref[j]
            at = block // OWNED - z * (X * C)
            wanted = jnp.where(lane == at, (block % OWNED).astype(jnp.float32), wanted)
        out_ref[z, PACK:] = wanted.astype(jnp.bfloat16)


def letters(own_list, keys, values):
    return pl.pallas_call(
        letter_kernel,
        grid_spec=pltpu.PrefetchScalarGridSpec(
            num_scalar_prefetch=1,
            grid=(1,),
            in_specs=[pl.BlockSpec(a.shape, lambda i, s: (0, 0, 0)) for a in (keys, values)],
            out_specs=pl.BlockSpec((Z, LETTER, DV), lambda i, s: (0, 0, 0)),
        ),
        out_shape=jax.ShapeDtypeStruct((Z, LETTER, DV), keys.dtype),
        cost_estimate=pl.CostEstimate(flops=0, bytes_accessed=Z * LETTER * DV * 2, transcendentals=0),
        name="letters",
    )(own_list, keys, values)


def payload_kernel(wanted_ref, blocks_ref, out_ref):
    def one(t, carry):
        out_ref[t] = blocks_ref[wanted_ref[t % (X * C), 0, t // (X * C)]]
        return carry

    lax.fori_loop(0, out_ref.shape[0], one, 0, unroll=8)


def payload(wanted, blocks):
    tiles = wanted.shape[0] * wanted.shape[2]
    whole = lambda shape: pl.BlockSpec(shape, lambda i, w: (0, 0, 0))
    return pl.pallas_call(
        payload_kernel,
        grid_spec=pltpu.PrefetchScalarGridSpec(
            num_scalar_prefetch=1,
            grid=(1,),
            in_specs=[whole(blocks.shape)],
            out_specs=whole((tiles, PACK, DV)),
        ),
        out_shape=jax.ShapeDtypeStruct((tiles, PACK, DV), blocks.dtype),
        cost_estimate=pl.CostEstimate(flops=0, bytes_accessed=2 * tiles * PACK * DV * 2, transcendentals=0),
        compiler_params=pltpu.CompilerParams(vmem_limit_bytes=16 << 20),
        name="payload",
    )(wanted, blocks)


def coarse_kernel(info_ref, *rest):
    kv_refs, (q_ref, out_ref, lse_ref, keys, values_t, scores) = rest[:X], rest[X:]
    rows = Z * BLK
    base, x, c = info_ref[0], info_ref[1], info_ref[2]

    @pl.when(pl.program_id(0) == 0)
    def _():
        for n in range(X):
            kv_ref = kv_refs[n]
            for z in range(0, Z, 2):
                at = n * rows + z * BLK
                keys[at : at + BLK, :] = unpacked_keys(kv_ref.at[z])
                keys[at + BLK : at + 2 * BLK, :] = unpacked_keys(kv_ref.at[z + 1])
                v = jnp.concatenate([kv_ref[z, BLK : 2 * BLK], kv_ref[z + 1, BLK : 2 * BLK]], axis=0)
                values_t[:, at : at + 2 * BLK] = v.T

    q = jnp.concatenate([q_ref[0], q_ref[1]], axis=1)
    width = q.shape[1]
    late = 2 * BLK
    row = lax.broadcasted_iota(jnp.int32, (late, width), 0)
    lane = lax.broadcasted_iota(jnp.int32, (late, width), 1)
    token0 = (Z - 2 + row // BLK) * (X * C * BLK) + row % BLK
    query_pos = base + lane % TILE
    top = jnp.full((1, width), NEGATIVE, jnp.float32)
    for n in range(X):
        s = jnp.dot(keys[n * rows : (n + 1) * rows, :], q, preferred_element_type=jnp.float32)
        token = token0 + ((x + X - n) % X * C + c) * BLK
        tail = jnp.where(token * CSTRIDE + CLEN - 1 <= query_pos, s[rows - late :], NEGATIVE)
        scores[n * rows : (n + 1) * rows - late, :] = s[: rows - late]
        scores[(n + 1) * rows - late : (n + 1) * rows, :] = tail
        top = jnp.maximum(top, jnp.max(s[: rows - late], axis=0, keepdims=True))
        top = jnp.maximum(top, jnp.max(tail, axis=0, keepdims=True))
    total = jnp.zeros((1, width), jnp.float32)
    acc = jnp.zeros((DV, width), jnp.float32)
    for n in range(X):
        w = jnp.exp2((scores[n * rows : (n + 1) * rows, :] - top) * EXP_SCALE)
        total = total + jnp.sum(w, axis=0, keepdims=True)
        acc = acc + jnp.dot(
            values_t[:, n * rows : (n + 1) * rows], w.astype(jnp.bfloat16), preferred_element_type=jnp.float32
        )
    acc = acc * (1.0 / total)
    lse = top * EXP_SCALE + jnp.log(total) * math.log2(math.e)
    for i in range(2):
        out_ref[i] = acc[:, i * TILE : (i + 1) * TILE].astype(out_ref.dtype)
        lse_ref[i] = lse[:, i * TILE : (i + 1) * TILE]


def in_hbm(x):
    return pltpu.with_memory_space_constraint(x, pltpu.HBM)


def coarse_half(info, coarse, queries_t, dtype):
    heads = queries_t.shape[0]
    tokens = X * Z * BLK
    pair = lambda shape: pl.BlockSpec((2, *shape), lambda p, i: (p, 0, 0))
    return pl.pallas_call(
        coarse_kernel,
        grid_spec=pltpu.PrefetchScalarGridSpec(
            num_scalar_prefetch=1,
            grid=(heads // 2,),
            in_specs=[
                *[pl.BlockSpec(a.shape, lambda p, i: (0, 0, 0), pipeline_mode=pl.Buffered(1)) for a in coarse],
                pair((DQK, TILE)),
            ],
            out_specs=[pair((DV, TILE)), pair((1, TILE))],
            scratch_shapes=[
                pltpu.VMEM((tokens, DQK), jnp.bfloat16),
                pltpu.VMEM((DV, tokens), jnp.bfloat16),
                pltpu.VMEM((tokens, 2 * TILE), jnp.float32),
            ],
        ),
        out_shape=[
            jax.ShapeDtypeStruct((heads, DV, TILE), dtype),
            jax.ShapeDtypeStruct((heads, 1, TILE), jnp.float32),
        ],
        cost_estimate=pl.CostEstimate(
            flops=EARLY * 2 * heads * TILE * tokens * (DQK + DV),
            bytes_accessed=tokens * (DQK + DV) * 2 + heads * TILE * (DQK * 2 + DV * 4),
            transcendentals=EARLY * heads * TILE * tokens,
        ),
        compiler_params=pltpu.CompilerParams(vmem_limit_bytes=20 << 20),
        name="coarse",
    )(info, *coarse, queries_t)


def tail_kernel(n_grp, info_ref, incoming, q_ref, gate_ref, lse_ref, lse2_ref, coarse_ref, coarse2_ref, weight_ref, *rest):
    outs, scratch = rest[:n_grp], rest[n_grp:]
    queries, coarse, coarse2, weight, keys, values_t, attended, in_sem, weight_sem = scratch
    heads = queries.shape[0]
    cols = weight.shape[2]
    base, grp = info_ref[0], info_ref[1]
    q_copy = pltpu.make_async_copy(q_ref, queries, in_sem.at[0])
    coarse_copy = pltpu.make_async_copy(coarse_ref, coarse, in_sem.at[1])
    coarse2_copy = pltpu.make_async_copy(coarse2_ref, coarse2, in_sem.at[2])
    q_copy.start()
    coarse_copy.start()
    coarse2_copy.start()
    late = SEL - 1
    for j in range(SEL):
        late = jnp.where(info_ref[3 + j] * BLK >= base, j, late)
    owners = []
    for j in range(SEL):
        slot_from = jnp.where(late == j, SEL - 1, j) if j < SEL - 1 else late
        owners.append(info_ref[3 + slot_from] // OWNED)
    for j in range(0, SEL, 2):
        first, second = incoming.at[owners[j]], incoming.at[owners[j + 1]]
        keys[j * BLK : (j + 1) * BLK, :] = unpacked_keys(first)
        keys[(j + 1) * BLK : (j + 2) * BLK, :] = unpacked_keys(second)
        v = jnp.concatenate([first[BLK : 2 * BLK], second[BLK : 2 * BLK]], axis=0)
        values_t[:, j * BLK : (j + 2) * BLK] = v.T
    q_copy.wait()
    coarse_copy.wait()
    coarse2_copy.wait()
    weight_copies = []
    for k in range(n_grp):
        at = pl.multiple_of(lax.rem(grp + k, n_grp) * cols, DV)
        weight_copies.append(
            pltpu.make_async_copy(weight_ref.at[:, pl.ds(at, cols)], weight.at[k], weight_sem.at[k])
        )
    for copy in weight_copies:
        copy.start()
    width = 2 * TILE
    n_keys = SEL * BLK
    row = lax.broadcasted_iota(jnp.int32, (BLK, width), 0)
    lane = lax.broadcasted_iota(jnp.int32, (BLK, width), 1)
    seen = info_ref[3 + late] * BLK + row <= base + lane % TILE

    for p in range(heads // 2):
        q = jnp.concatenate([queries[2 * p], queries[2 * p + 1]], axis=1)
        s = jnp.dot(keys[...], q, preferred_element_type=jnp.float32)
        last = jnp.where(seen, s[n_keys - BLK :], NEGATIVE)
        top = jnp.maximum(
            jnp.max(s[: n_keys - BLK], axis=0, keepdims=True), jnp.max(last, axis=0, keepdims=True)
        )
        w = jnp.exp2((jnp.concatenate([s[: n_keys - BLK], last], axis=0) - top) * EXP_SCALE)
        total = jnp.sum(w, axis=0, keepdims=True)
        o = jnp.dot(values_t[...], w.astype(jnp.bfloat16), preferred_element_type=jnp.float32)
        gate = jnp.concatenate([gate_ref[heads + 2 * p], gate_ref[heads + 2 * p + 1]], axis=1)
        o = o * (gate / total)
        for i in range(2):
            h = 2 * p + i
            gap = lse2_ref[h] - lse_ref[h]
            both = o[:, i * TILE : (i + 1) * TILE] + coarse[h] * (gate_ref[h] / (1.0 + jnp.exp2(gap)))
            both = both + coarse2[h].astype(jnp.float32) * (gate_ref[h] / (1.0 + jnp.exp2(-gap)))
            attended[:, h * DV : (h + 1) * DV] = both.T.astype(jnp.bfloat16)
    for k in (*range(1, n_grp), 0):
        weight_copies[k].wait()
        part = jnp.dot(attended[...], weight[k], preferred_element_type=jnp.float32)
        outs[k][...] = part.astype(outs[k].dtype)


def tail(info, incoming, queries_t, gate, coarse, coarse2, out_weight, n_grp):
    heads = queries_t.shape[0]
    rows, model = out_weight.shape
    cols = model // n_grp
    vmem = lambda shape: pl.BlockSpec(shape, lambda i, s: (0,) * len(shape))
    on_chip = pl.BlockSpec(memory_space=pltpu.VMEM)
    hbm = pl.BlockSpec(memory_space=pltpu.HBM)
    return pl.pallas_call(
        functools.partial(tail_kernel, n_grp),
        grid_spec=pltpu.PrefetchScalarGridSpec(
            num_scalar_prefetch=1,
            grid=(1,),
            in_specs=[
                on_chip,
                hbm,
                vmem(gate.shape),
                vmem(coarse[1].shape),
                vmem(coarse[1].shape),
                hbm,
                hbm,
                hbm,
            ],
            out_specs=[vmem((TILE, cols))] * n_grp,
            scratch_shapes=[
                pltpu.VMEM(queries_t.shape, queries_t.dtype),
                pltpu.VMEM(coarse[0].shape, coarse[0].dtype),
                pltpu.VMEM(coarse2[0].shape, coarse2[0].dtype),
                pltpu.VMEM((n_grp, rows, cols), jnp.bfloat16),
                pltpu.VMEM((SEL * BLK, DQK), jnp.bfloat16),
                pltpu.VMEM((DV, SEL * BLK), jnp.bfloat16),
                pltpu.VMEM((TILE, rows), jnp.bfloat16),
                pltpu.SemaphoreType.DMA((3,)),
                pltpu.SemaphoreType.DMA((n_grp,)),
            ],
        ),
        out_shape=[jax.ShapeDtypeStruct((TILE, cols), jnp.float32)]
        + [jax.ShapeDtypeStruct((TILE, cols), jnp.bfloat16)] * (n_grp - 1),
        cost_estimate=pl.CostEstimate(
            flops=2 * heads * TILE * SEL * BLK * (DQK + DV) + 2 * TILE * rows * model,
            bytes_accessed=rows * model * 2,
            transcendentals=heads * TILE * SEL * BLK,
        ),
        compiler_params=pltpu.CompilerParams(vmem_limit_bytes=24 << 20),
        name="tail",
    )(
        info,
        incoming,
        in_hbm(queries_t),
        gate,
        coarse[1],
        coarse2[1],
        in_hbm(coarse[0]),
        in_hbm(coarse2[0]),
        in_hbm(out_weight),
    )


def shards(
    queries,
    key_cache,
    group_value_cache,
    coarse_keys,
    coarse_values,
    hidden,
    gate_weight,
    out_weight,
    selected,
):
    seq_count = lax.axis_size("seq")
    n_grp = lax.axis_size("grp")
    seq_index = lax.axis_index("seq")
    grp_index = lax.axis_index("grp")
    ctx_dev = key_cache.shape[1]
    context = ctx_dev * seq_count
    heads = queries.shape[1]
    blocks_dev = ctx_dev // BLK

    own_list = selected[0, 0]
    queries_t = jnp.transpose(queries, (1, 2, 0))
    other_q = shifted(queries_t, 0, 1)

    came = lax.all_to_all(
        letters(own_list, coarse_keys, coarse_values), "seq", 0, 0, axis_index_groups=ALONG_Z, tiled=True
    )
    wanted = jnp.transpose(came[:, PACK, : X * C])[:, None, :].astype(jnp.int32)
    wanted = lax.all_to_all(wanted, "seq", 0, 0, axis_index_groups=IN_PLANE, tiled=True)

    column, wanted, other_q = lax.optimization_barrier((came, wanted, other_q))
    coarse = [column] + [shifted(column, k, 0) for k in range(1, X)]

    blocks = packed_blocks(
        key_cache[0].reshape(blocks_dev, BLK, DQK), group_value_cache[0].reshape(blocks_dev, BLK, DV)
    )
    incoming = lax.all_to_all(payload(wanted, blocks), "seq", 0, 0, tiled=True)

    first_query = context - TILE * seq_count
    x_index, c_index = seq_index // C % X, seq_index % C
    scalars = lambda *values: jnp.stack(values).astype(jnp.int32)
    other_index = seq_index + 1 - 2 * c_index
    gates = jax.nn.sigmoid(
        lax.dot_general(
            gate_weight[0], hidden, (((0,), (1,)), ((), ())), preferred_element_type=jnp.float32
        )
    )[:, None, :]
    first_pos = first_query + seq_index * TILE
    theirs = coarse_half(scalars(first_query + other_index * TILE, x_index, c_index), coarse, other_q, jnp.bfloat16)
    coarse2 = [shifted(a, 0, 1) for a in theirs]
    coarse1 = coarse_half(scalars(first_pos, x_index, c_index), coarse, queries_t, jnp.float32)
    info = jnp.concatenate([scalars(first_pos, grp_index, seq_index), own_list])
    own, *others = tail(info, incoming, queries_t, gates, coarse1, coarse2, out_weight, n_grp)
    for k, part in enumerate(others, 1):
        perm = [(i, (i + k) % n_grp) for i in range(n_grp)]
        own = own + lax.ppermute(part, "grp", perm).astype(jnp.float32)
    return own.astype(jnp.bfloat16)


def solution(mesh):
    return jax.shard_map(
        shards,
        mesh=mesh,
        in_specs=(
            P("seq", "grp", None),
            P("grp", "seq", None),
            P("grp", "seq", None),
            P("grp", "seq", None),
            P("grp", "seq", None),
            P("seq", None),
            P("grp", None, None),
            P("grp", None),
            P("grp", "seq", None),
        ),
        out_specs=P("seq", "grp"),
        check_vma=False,
    )
```

time: 151 us -> 137 us (0.907)
  waiting for transfers between devices: 68.2 us -> 54.2 us
  between operations: 13.5 us -> 0.15 us
  starting transfers between devices: 23 us -> 33.9 us
  Pallas kernels: 33.1 us -> 43.1 us
  local copies, waits for them, and re-layouts: 9.09 us -> 3.13 us
    all_gather x2 -> x0, waiting for transfers between devices: 53.9 us -> none  [the longest x1 43.7 us: everywhere(): lax.all_gather(columns[:, :PACK], 'seq', axis=0, tiled=True, axis_index_g...]
    all_to_all x2 -> x3, waiting for transfers between devices: 8.04 us -> 35.1 us  [the longest x1 19.6 us: shards(): incoming = lax.all_to_all(payload(wanted, blocks), 'seq', 0, 0, tiled=True)]
    pallas_call x1 -> x3, Pallas kernels: 17.4 us -> 27.4 us  [the longest x2 24.7 us: coarse_half(): pl.pallas_call(coarse_kernel, grid_spec=pltpu.PrefetchScalarGridSpec(num_...]
    ppermute x0 -> x6, waiting for transfers between devices: none -> 10 us  [shifted(): lax.ppermute(x, 'seq', [(index(*s), index(s[0], s[1] + dx, s[2] + dc)) fo...]
    ppermute x0 -> x6, starting transfers between devices: none -> 8.69 us  [shifted(): lax.ppermute(x, 'seq', [(index(*s), index(s[0], s[1] + dx, s[2] + dc)) fo...]
    all_to_all x2 -> x3, starting transfers between devices: 17.9 us -> 21.4 us  [the longest x1 9.15 us: shards(): lax.all_to_all(letters(own_list, coarse_keys, coarse_values), 'seq', 0, 0...]
    ppermute x3, waiting for transfers between devices: 6.26 us -> 9.12 us  [shards(): own = own + lax.ppermute(part, 'grp', perm).astype(jnp.float32)]
    unnamed x15 -> x19, local copies, waits for them, and re-layouts: 5.04 us -> 2.37 us
  transfers between devices with their start and end apart: 7 -> 12, of which waited for: 5 -> 8; matrix products, arithmetic and copies ran while one was open for 3% -> 2% of each run, Pallas kernels for 13% -> 20%
where the time goes in v4:
time: 137 us
  waiting for transfers between devices  54.2 us (40%)
  Pallas kernels  43.1 us (31%)
  starting transfers between devices  33.9 us (25%)
  local copies, waits for them, and re-layouts  3.13 us (2%)
  other arithmetic  1.74 us (1%)
    pallas_call x2, Pallas kernels, coarse_half(): pl.pallas_call(coarse_kernel, grid_spec=pltpu.PrefetchScalarGridSpec(num_...  24.7 us
    all_to_all x1, waiting for transfers between devices, shards(): incoming = lax.all_to_all(payload(wanted, blocks), 'seq', 0, 0, tiled=True)  19.6 us
    pallas_call x1, Pallas kernels, tail(): pl.pallas_call(functools.partial(tail_kernel, n_grp), grid_spec=pltpu.Pre...  13 us
    all_to_all x1, waiting for transfers between devices, shards(): lax.all_to_all(letters(own_list, coarse_keys, coarse_values), 'seq', 0, 0...  10.9 us
    ppermute x6, waiting for transfers between devices, shifted(): lax.ppermute(x, 'seq', [(index(*s), index(s[0], s[1] + dx, s[2] + dc)) fo...  10 us
    all_to_all x1, starting transfers between devices, shards(): lax.all_to_all(letters(own_list, coarse_keys, coarse_values), 'seq', 0, 0...  9.15 us
    ppermute x3, waiting for transfers between devices, shards(): own = own + lax.ppermute(part, 'grp', perm).astype(jnp.float32)  9.12 us
    ppermute x6, starting transfers between devices, shifted(): lax.ppermute(x, 'seq', [(index(*s), index(s[0], s[1] + dx, s[2] + dc)) fo...  8.69 us
  transfers between devices with their start and end apart: 12, of which 8 were waited for; matrix products, arithmetic and copies ran while one was open for 2% of the time, Pallas kernels for 20%

profile of v4, /device:TPU:1, one launch (start us, length us, event | category | flops | bytes accessed | tf_op | source)
XLA Modules:
  0.0 136.6 jit_solution(5429088196060139769)
XLA Ops:
  0.0 2.7 %letters.1 = bf16[8,168,128]{2,1,0:T(8,128)(2,1)} custom-call(s32[16]{0:T(128)} %bitcast.28, bf16[1,64,192]{2,1,0:T(8,128)(2,1)} %keys_ref.1, bf16[1,64,128]{2,1,0:T(8,128)(2,1)} %values_ref.1), custom_call_target="tpu_custom_call" | custom-call | bytes 344064 | tf_op jit(solution)/shard_map/letters/pallas_call | solution.py:67
  2.7 9.1 %all-to-all-start = ((bf16[8,168,128]{2,1,0:T(8,128)(2,1)}), bf16[8,168,128]{2,1,0:T(8,128)(2,1)}, u32[]{:S(2)}, u32[]{:S(2)}) async-start(bf16[8,168,128]{2,1,0:T(8,128)(2,1)} %letters.1), calls=%async_computation | async-start | bytes 688128 | tf_op jit(solution)/shard_map/all_to_all | solution.py:339
  11.8 1.0 collective-permute-start
  12.8 0.2 copy.12
  13.4 10.9 %all-to-all-done.rest_0_ = bf16[8,168,128]{2,1,0:T(8,128)(2,1)} async-done(((bf16[8,168,128]{2,1,0:T(8,128)(2,1)}), bf16[8,168,128]{2,1,0:T(8,128)(2,1)}, u32[]{:S(2)}, u32[]{:S(2)}) %all-to-all-start) | async-done | bytes 344096 | tf_op jit(solution)/shard_map/all_to_all | solution.py:339
  24.3 0.7 slice_convert_fusion
  25.0 0.7 copy.11
  25.7 6.5 %all-to-all-start.1 = ((s32[8,1,8]{2,1,0:T(1,128)}), s32[8,1,8]{2,1,0:T(1,128)S(1)}, u32[]{:S(2)}, u32[]{:S(2)}) async-start(s32[8,1,8]{2,1,0:T(1,128)} %copy.11), calls=%async_computation.1 | async-start | bytes 8192 | tf_op jit(solution)/shard_map/all_to_all | solution.py:343
  32.2 4.5 %all-to-all-done.1.wanted_ref = s32[8,1,8]{2,1,0:T(1,128)S(1)} async-done(((s32[8,1,8]{2,1,0:T(1,128)}), s32[8,1,8]{2,1,0:T(1,128)S(1)}, u32[]{:S(2)}, u32[]{:S(2)}) %all-to-all-start.1) | async-done | bytes 288 | tf_op jit(solution)/shard_map/all_to_all | solution.py:343
  36.7 0.3 collective-permute-start.1
  37.0 1.8 %collective-permute-start.2 = (bf16[8,168,128]{2,1,0:T(8,128)(2,1)}, bf16[8,168,128]{2,1,0:T(8,128)(2,1)}, u32[]{:S(2)}, u32[]{:S(2)}) collective-permute-start(bf16[8,168,128]{2,1,0:T(8,128)(2,1)} %all-to-all-done.rest_0_), channel_id=1, source_target_pairs={{0,4},{1,5},{2,6},{3,7},{4,0},{5,1},{6,2},{7,3},{8,12},{9,13},{10,... | collective-permute-start | bytes 1032200 | tf_op jit(solution)/shard_map/ppermute | solution.py:47
  38.8 0.9 collective-permute-start.3
  39.8 0.3 fusion.2
  40.1 2.6 %payload.1 = bf16[64,160,128]{2,1,0:T(8,128)(2,1)} custom-call(s32[8,1,8]{2,1,0:T(1,128)S(1)} %all-to-all-done.1.wanted_ref, bf16[16,160,128]{2,1,0:T(8,128)(2,1)S(1)} %maximum_maximum_fusion.blocks_ref), custom_call_target="tpu_custom_call" | custom-call | bytes 5242880 | tf_op jit(solution)/shard_map/payload/pallas_call | solution.py:92
  42.7 5.7 %all-to-all-start.2 = ((bf16[64,160,128]{2,1,0:T(8,128)(2,1)}), bf16[64,160,128]{2,1,0:T(8,128)(2,1)S(1)}, u32[]{:S(2)}, u32[]{:S(2)}) async-start(bf16[64,160,128]{2,1,0:T(8,128)(2,1)} %payload.1), calls=%async_computation.2 | async-start | bytes 5242880 | tf_op jit(solution)/shard_map/all_to_all | solution.py:351
  48.5 5.5 %collective-permute-done.2.rest_2_ = bf16[8,168,128]{2,1,0:T(8,128)(2,1)} collective-permute-done((bf16[8,168,128]{2,1,0:T(8,128)(2,1)}, bf16[8,168,128]{2,1,0:T(8,128)(2,1)}, u32[]{:S(2)}, u32[]{:S(2)}) %collective-permute-start.2) | collective-permute-done | bytes 344096 | tf_op jit(solution)/shard_map/ppermute | solution.py:47
  54.0 4.5 %collective-permute-done.3.rest_3_ = bf16[8,168,128]{2,1,0:T(8,128)(2,1)} collective-permute-done((bf16[8,168,128]{2,1,0:T(8,128)(2,1)}, bf16[8,168,128]{2,1,0:T(8,128)(2,1)}, u32[]{:S(2)}, u32[]{:S(2)}) %collective-permute-start.3) | collective-permute-done | bytes 344096 | tf_op jit(solution)/shard_map/ppermute | solution.py:47
  58.5 1.1 copy-done.4
  59.6 12.4 %coarse.3 = (bf16[16,128,128]{2,1,0:T(8,128)(2,1)S(1)}, f32[16,1,128]{2,1,0:T(1,128)S(1)}) custom-call(s32[3]{0:T(128)S(1)} %get-tuple-element.30.info_ref, bf16[8,168,128]{2,1,0:T(8,128)(2,1)} %all-to-all-done.rest_0_, bf16[8,168,128]{2,1,0:T(8,128)(2,1)} %collective-permute-done.1.rest_1_, bf16[8,168,128]{2,1,0:T(8,128)(2,1)} %collective-permute-done.2.rest_2_, ...), custom_call_target="tpu_custom_call" | custom-call | flops 42949672960 | bytes 3145728 | tf_op jit(solution)/shard_map/coarse/pallas_call | solution.py:162
  72.0 4.5 %collective-permute-start.4 = (f32[16,1,128]{2,1,0:T(1,128)S(1)}, f32[16,1,128]{2,1,0:T(1,128)S(1)}, u32[]{:S(2)}, u32[]{:S(2)}) collective-permute-start(f32[16,1,128]{2,1,0:T(1,128)S(1)} %get-tuple-element.20), channel_id=1, source_target_pairs={{0,1},{1,0},{2,3},{3,2},{4,5},{5,4},{6,7},{7,6},{8,9},{9,8},{10,11... | collective-permute-start | bytes 24584 | tf_op jit(solution)/shard_map/ppermute | solution.py:47
  76.5 0.3 collective-permute-start.5
  76.8 12.4 %coarse.2 = (f32[16,128,128]{2,1,0:T(8,128)S(1)}, f32[16,1,128]{2,1,0:T(1,128)S(1)}) custom-call(s32[3]{0:T(128)S(1)} %get-tuple-element.29.info_ref, bf16[8,168,128]{2,1,0:T(8,128)(2,1)} %all-to-all-done.rest_0_, bf16[8,168,128]{2,1,0:T(8,128)(2,1)} %collective-permute-done.1.rest_1_, bf16[8,168,128]{2,1,0:T(8,128)(2,1)} %collective-permute-done.2.rest_2_, ...), custom_call_target="tpu_custom_call" | custom-call | flops 42949672960 | bytes 3145728 | tf_op jit(solution)/shard_map/coarse/pallas_call | solution.py:162
  89.2 1.0 copy-done.1
  90.2 19.6 %all-to-all-done.2.incoming = bf16[64,160,128]{2,1,0:T(8,128)(2,1)S(1)} async-done(((bf16[64,160,128]{2,1,0:T(8,128)(2,1)}), bf16[64,160,128]{2,1,0:T(8,128)(2,1)S(1)}, u32[]{:S(2)}, u32[]{:S(2)}) %all-to-all-start.2) | async-done | bytes 2621472 | tf_op jit(solution)/shard_map/all_to_all | solution.py:351
  109.8 13.0 %tail.1 = (f32[128,640]{1,0:T(8,128)S(1)}, bf16[128,640]{1,0:T(8,128)(2,1)S(1)}, bf16[128,640]{1,0:T(8,128)(2,1)S(1)}, bf16[128,640]{1,0:T(8,128)(2,1)S(1)}) custom-call(s32[19]{0:T(128)S(1)} %pad_add_fusion.info_ref, bf16[64,160,128]{2,1,0:T(8,128)(2,1)S(1)} %all-to-all-done.2.incoming, bf16[16,192,128]{2,1,0:T(8,128)(2,1)} %bitcast.21, ...), custom_call_target="tpu_custom_call" | custom-call | flops 2684354560 | bytes 10485760 | tf_op jit(solution)/shard_map/tail/pallas_call | solution.py:265
  122.9 2.8 %collective-permute-start.8 = (bf16[128,640]{1,0:T(8,128)(2,1)S(1)}, bf16[128,640]{1,0:T(8,128)(2,1)S(1)}, u32[]{:S(2)}, u32[]{:S(2)}) collective-permute-start(bf16[128,640]{1,0:T(8,128)(2,1)S(1)} %get-tuple-element.26), channel_id=1, source_target_pairs={{0,192},{64,0},{128,64},{192,128},{1,193},{65,1},{129,65},{193,129... | collective-permute-start | bytes 491528 | tf_op jit(solution)/shard_map/ppermute | solution.py:370
  125.7 0.3 collective-permute-start.7
  126.0 0.7 collective-permute-start.6
  126.7 2.1 %collective-permute-done.8 = bf16[128,640]{1,0:T(8,128)(2,1)S(1)} collective-permute-done((bf16[128,640]{1,0:T(8,128)(2,1)S(1)}, bf16[128,640]{1,0:T(8,128)(2,1)S(1)}, u32[]{:S(2)}, u32[]{:S(2)}) %collective-permute-start.8) | collective-permute-done | bytes 163872 | tf_op jit(solution)/shard_map/ppermute | solution.py:370
  128.8 2.7 %collective-permute-done.7 = bf16[128,640]{1,0:T(8,128)(2,1)S(1)} collective-permute-done((bf16[128,640]{1,0:T(8,128)(2,1)S(1)}, bf16[128,640]{1,0:T(8,128)(2,1)S(1)}, u32[]{:S(2)}, u32[]{:S(2)}) %collective-permute-start.7) | collective-permute-done | bytes 163872 | tf_op jit(solution)/shard_map/ppermute | solution.py:370
  131.4 4.4 %collective-permute-done.6 = bf16[128,640]{1,0:T(8,128)(2,1)S(1)} collective-permute-done((bf16[128,640]{1,0:T(8,128)(2,1)S(1)}, bf16[128,640]{1,0:T(8,128)(2,1)S(1)}, u32[]{:S(2)}, u32[]{:S(2)}) %collective-permute-start.6) | collective-permute-done | bytes 163872 | tf_op jit(solution)/shard_map/ppermute | solution.py:370
  135.8 0.8 add_convert_fusion
  (25 shorter events, 0.4 us)
Async XLA Ops:
  0.0 39.8 %copy-start = (bf16[128,2560]{1,0:T(8,128)(2,1)S(1)}, bf16[128,2560]{1,0:T(8,128)(2,1)}, u32[]{:S(2)}) copy-start(bf16[128,2560]{1,0:T(8,128)(2,1)} %param.14) | copy-start | bytes 1966084
  0.0 12.8 %copy-start.5 = (bf16[1,1024,192]{1,2,0:T(8,128)(2,1)S(1)}, bf16[1,1024,192]{1,2,0:T(8,128)(2,1)}, u32[]{:S(2)}) copy-start(bf16[1,1024,192]{1,2,0:T(8,128)(2,1)} %param.10) | copy-start | bytes 1179652
  2.7 10.6 %copy-start.6 = (bf16[1,1024,128]{2,1,0:T(8,128)(2,1)S(1)}, bf16[1,1024,128]{2,1,0:T(8,128)(2,1)}, u32[]{:S(2)}) copy-start(bf16[1,1024,128]{2,1,0:T(8,128)(2,1)} %param.11) | copy-start | bytes 786436
  2.7 21.6 %all-to-all-start = ((bf16[8,168,128]{2,1,0:T(8,128)(2,1)}), bf16[8,168,128]{2,1,0:T(8,128)(2,1)}, u32[]{:S(2)}, u32[]{:S(2)}) async-start(bf16[8,168,128]{2,1,0:T(8,128)(2,1)} %letters.1), calls=%async_computation | async-start | bytes 688128 | tf_op jit(solution)/shard_map/all_to_all | solution.py:339
  11.8 24.9 %collective-permute-start = (bf16[16,192,128]{2,1,0:T(8,128)(2,1)}, bf16[16,192,128]{2,1,0:T(8,128)(2,1)S(1)}, u32[]{:S(2)}, u32[]{:S(2)}) collective-permute-start(bf16[16,192,128]{2,1,0:T(8,128)(2,1)} %bitcast.20), channel_id=1, source_target_pairs={{0,1},{1,0},{2,3},{3,2},{4,5},{5,4},{6,7},{7,6},{8,9},{9,8},{10,11... | collective-permute-start | bytes 2359304 | tf_op jit(solution)/shard_map/ppermute | solution.py:47
  13.0 26.7 %copy-start.8 = (s32[1,1,16]{2,1,0:T(1,128)S(1)}, s32[1,1,16]{2,1,0:T(1,128)}, u32[]{:S(2)}) copy-start(s32[1,1,16]{2,1,0:T(1,128)} %param.17) | copy-start | bytes 196
  13.0 26.7 %copy-start.7 = (bf16[1,2560,32]{1,2,0:T(8,128)(2,1)S(1)}, bf16[1,2560,32]{1,2,0:T(8,128)(2,1)}, u32[]{:S(2)}) copy-start(bf16[1,2560,32]{1,2,0:T(8,128)(2,1)} %param.15) | copy-start | bytes 491524
  25.7 11.0 %all-to-all-start.1 = ((s32[8,1,8]{2,1,0:T(1,128)}), s32[8,1,8]{2,1,0:T(1,128)S(1)}, u32[]{:S(2)}, u32[]{:S(2)}) async-start(s32[8,1,8]{2,1,0:T(1,128)} %copy.11), calls=%async_computation.1 | async-start | bytes 8192 | tf_op jit(solution)/shard_map/all_to_all | solution.py:343
  36.7 6.0 %copy-start.3 = (bf16[16,192,128]{2,1,0:T(8,128)(2,1)}, bf16[16,192,128]{2,1,0:T(8,128)(2,1)S(1)}, u32[]{:S(2)}) copy-start(bf16[16,192,128]{2,1,0:T(8,128)(2,1)S(1)} %collective-permute-done.rest_4_) | copy-start | bytes 2359300
  36.7 11.8 %collective-permute-start.1 = (bf16[8,168,128]{2,1,0:T(8,128)(2,1)}, bf16[8,168,128]{2,1,0:T(8,128)(2,1)}, u32[]{:S(2)}, u32[]{:S(2)}) collective-permute-start(bf16[8,168,128]{2,1,0:T(8,128)(2,1)} %all-to-all-done.rest_0_), channel_id=1, source_target_pairs={{0,2},{1,3},{2,4},{3,5},{4,6},{5,7},{6,0},{7,1},{8,10},{9,11},{10,... | collective-permute-start | bytes 1032200 | tf_op jit(solution)/shard_map/ppermute | solution.py:47
  37.0 17.0 %collective-permute-start.2 = (bf16[8,168,128]{2,1,0:T(8,128)(2,1)}, bf16[8,168,128]{2,1,0:T(8,128)(2,1)}, u32[]{:S(2)}, u32[]{:S(2)}) collective-permute-start(bf16[8,168,128]{2,1,0:T(8,128)(2,1)} %all-to-all-done.rest_0_), channel_id=1, source_target_pairs={{0,4},{1,5},{2,6},{3,7},{4,0},{5,1},{6,2},{7,3},{8,12},{9,13},{10,... | collective-permute-start | bytes 1032200 | tf_op jit(solution)/shard_map/ppermute | solution.py:47
  38.8 19.7 %collective-permute-start.3 = (bf16[8,168,128]{2,1,0:T(8,128)(2,1)}, bf16[8,168,128]{2,1,0:T(8,128)(2,1)}, u32[]{:S(2)}, u32[]{:S(2)}) collective-permute-start(bf16[8,168,128]{2,1,0:T(8,128)(2,1)} %all-to-all-done.rest_0_), channel_id=1, source_target_pairs={{0,6},{1,7},{2,0},{3,1},{4,2},{5,3},{6,4},{7,5},{8,14},{9,15},{10,... | collective-permute-start | bytes 1032200 | tf_op jit(solution)/shard_map/ppermute | solution.py:47
  42.7 67.1 %all-to-all-start.2 = ((bf16[64,160,128]{2,1,0:T(8,128)(2,1)}), bf16[64,160,128]{2,1,0:T(8,128)(2,1)S(1)}, u32[]{:S(2)}, u32[]{:S(2)}) async-start(bf16[64,160,128]{2,1,0:T(8,128)(2,1)} %payload.1), calls=%async_computation.2 | async-start | bytes 5242880 | tf_op jit(solution)/shard_map/all_to_all | solution.py:351
  58.5 1.1 copy-start.4
  59.6 17.2 %copy-start.2 = (bf16[128,16,192]{0,2,1:T(8,128)(2,1)S(1)}, bf16[128,16,192]{0,2,1:T(8,128)(2,1)}, u32[]{:S(2)}) copy-start(bf16[128,16,192]{0,2,1:T(8,128)(2,1)} %param.9) | copy-start | bytes 2359300
  72.0 18.2 %collective-permute-start.4 = (f32[16,1,128]{2,1,0:T(1,128)S(1)}, f32[16,1,128]{2,1,0:T(1,128)S(1)}, u32[]{:S(2)}, u32[]{:S(2)}) collective-permute-start(f32[16,1,128]{2,1,0:T(1,128)S(1)} %get-tuple-element.20), channel_id=1, source_target_pairs={{0,1},{1,0},{2,3},{3,2},{4,5},{5,4},{6,7},{7,6},{8,9},{9,8},{10,11... | collective-permute-start | bytes 24584 | tf_op jit(solution)/shard_map/ppermute | solution.py:47
  76.5 13.7 %collective-permute-start.5 = (bf16[16,128,128]{2,1,0:T(8,128)(2,1)S(1)}, bf16[16,128,128]{2,1,0:T(8,128)(2,1)}, u32[]{:S(2)}, u32[]{:S(2)}) collective-permute-start(bf16[16,128,128]{2,1,0:T(8,128)(2,1)S(1)} %get-tuple-element.22), channel_id=1, source_target_pairs={{0,1},{1,0},{2,3},{3,2},{4,5},{5,4},{6,7},{7,6},{8,9},{9,8},{10,11... | collective-permute-start | bytes 1572872 | tf_op jit(solution)/shard_map/ppermute | solution.py:47
  89.2 1.0 copy-start.1
  122.9 5.9 %collective-permute-start.8 = (bf16[128,640]{1,0:T(8,128)(2,1)S(1)}, bf16[128,640]{1,0:T(8,128)(2,1)S(1)}, u32[]{:S(2)}, u32[]{:S(2)}) collective-permute-start(bf16[128,640]{1,0:T(8,128)(2,1)S(1)} %get-tuple-element.26), channel_id=1, source_target_pairs={{0,192},{64,0},{128,64},{192,128},{1,193},{65,1},{129,65},{193,129... | collective-permute-start | bytes 491528 | tf_op jit(solution)/shard_map/ppermute | solution.py:370
  125.7 5.8 %collective-permute-start.7 = (bf16[128,640]{1,0:T(8,128)(2,1)S(1)}, bf16[128,640]{1,0:T(8,128)(2,1)S(1)}, u32[]{:S(2)}, u32[]{:S(2)}) collective-permute-start(bf16[128,640]{1,0:T(8,128)(2,1)S(1)} %get-tuple-element.25), channel_id=1, source_target_pairs={{0,128},{64,192},{128,0},{192,64},{1,129},{65,193},{129,1},{193,65... | collective-permute-start | bytes 491528 | tf_op jit(solution)/shard_map/ppermute | solution.py:370
  126.0 9.8 %collective-permute-start.6 = (bf16[128,640]{1,0:T(8,128)(2,1)S(1)}, bf16[128,640]{1,0:T(8,128)(2,1)S(1)}, u32[]{:S(2)}, u32[]{:S(2)}) collective-permute-start(bf16[128,640]{1,0:T(8,128)(2,1)S(1)} %get-tuple-element.24), channel_id=1, source_target_pairs={{0,64},{64,128},{128,192},{192,0},{1,65},{65,129},{129,193},{193,1... | collective-permute-start | bytes 491528 | tf_op jit(solution)/shard_map/ppermute | solution.py:370

commit v5 on v4

--- a/solution.py
+++ b/solution.py
@@ -17,7 +17,8 @@
 DV = 128
 PACK = BLK + BLK + BLK // 2
 LETTER = PACK + 8
-OWNED = 16
+OWNED_BITS = 4
+OWNED = 1 << OWNED_BITS
 EARLY = 16
 NEGATIVE = -1e30
 EXP_SCALE = DQK**-0.5 * math.log2(math.e)
@@ -51,15 +52,14 @@
     keys = keys_ref[0]
     high = jnp.concatenate([keys[: BLK // 2, DV:], keys[BLK // 2 :, DV:]], axis=1)
     lane = lax.broadcasted_iota(jnp.int32, (LETTER - PACK, DV), 1)
+    wishes = [(list_ref[j] >> OWNED_BITS, (list_ref[j] & (OWNED - 1)).astype(jnp.float32)) for j in range(SEL)]
     for z in range(Z):
         out_ref[z, :BLK] = keys[:, :DV]
         out_ref[z, BLK : 2 * BLK] = values_ref[0]
         out_ref[z, 2 * BLK : PACK] = high
         wanted = jnp.zeros(lane.shape, jnp.float32)
-        for j in range(SEL):
-            block = list_ref[j]
-            at = block // OWNED - z * (X * C)
-            wanted = jnp.where(lane == at, (block % OWNED).astype(jnp.float32), wanted)
+        for owner, block in wishes:
+            wanted = jnp.where(lane == owner - z * (X * C), block, wanted)
         out_ref[z, PACK:] = wanted.astype(jnp.bfloat16)
 
 
@@ -79,23 +79,22 @@
 
 
 def payload_kernel(wanted_ref, blocks_ref, out_ref):
-    def one(t, carry):
-        out_ref[t] = blocks_ref[wanted_ref[t % (X * C), 0, t // (X * C)]]
-        return carry
-
-    lax.fori_loop(0, out_ref.shape[0], one, 0, unroll=8)
+    z0 = pl.program_id(0) * (out_ref.shape[0] // (X * C))
+    for t in range(out_ref.shape[0]):
+        z, at = divmod(t, X * C)
+        out_ref[t] = blocks_ref[wanted_ref[at, 0, z0 + z]]
 
 
 def payload(wanted, blocks):
     tiles = wanted.shape[0] * wanted.shape[2]
-    whole = lambda shape: pl.BlockSpec(shape, lambda i, w: (0, 0, 0))
+    steps = 4
     return pl.pallas_call(
         payload_kernel,
         grid_spec=pltpu.PrefetchScalarGridSpec(
             num_scalar_prefetch=1,
-            grid=(1,),
-            in_specs=[whole(blocks.shape)],
-            out_specs=whole((tiles, PACK, DV)),
+            grid=(steps,),
+            in_specs=[pl.BlockSpec(blocks.shape, lambda i, w: (0, 0, 0))],
+            out_specs=pl.BlockSpec((tiles // steps, PACK, DV), lambda i, w: (i, 0, 0)),
         ),
         out_shape=jax.ShapeDtypeStruct((tiles, PACK, DV), blocks.dtype),
         cost_estimate=pl.CostEstimate(flops=0, bytes_accessed=2 * tiles * PACK * DV * 2, transcendentals=0),
@@ -193,7 +192,7 @@
     outs, scratch = rest[:n_grp], rest[n_grp:]
     queries, coarse, coarse2, weight, keys, values_t, attended, in_sem, weight_sem = scratch
     heads = queries.shape[0]
-    cols = weight.shape[2]
+    cols = weight.shape[1] // n_grp
     base, grp = info_ref[0], info_ref[1]
     q_copy = pltpu.make_async_copy(q_ref, queries, in_sem.at[0])
     coarse_copy = pltpu.make_async_copy(coarse_ref, coarse, in_sem.at[1])
@@ -207,7 +206,7 @@
     owners = []
     for j in range(SEL):
         slot_from = jnp.where(late == j, SEL - 1, j) if j < SEL - 1 else late
-        owners.append(info_ref[3 + slot_from] // OWNED)
+        owners.append(info_ref[3 + slot_from] >> OWNED_BITS)
     for j in range(0, SEL, 2):
         first, second = incoming.at[owners[j]], incoming.at[owners[j + 1]]
         keys[j * BLK : (j + 1) * BLK, :] = unpacked_keys(first)
@@ -217,12 +216,12 @@
     q_copy.wait()
     coarse_copy.wait()
     coarse2_copy.wait()
+    n_copies = weight_sem.shape[0]
+    per_copy = weight.shape[0] // n_copies
     weight_copies = []
-    for k in range(n_grp):
-        at = pl.multiple_of(lax.rem(grp + k, n_grp) * cols, DV)
-        weight_copies.append(
-            pltpu.make_async_copy(weight_ref.at[:, pl.ds(at, cols)], weight.at[k], weight_sem.at[k])
-        )
+    for k in range(n_copies):
+        rows = pl.ds(k * per_copy, per_copy)
+        weight_copies.append(pltpu.make_async_copy(weight_ref.at[rows], weight.at[rows], weight_sem.at[k]))
     for copy in weight_copies:
         copy.start()
     width = 2 * TILE
@@ -231,27 +230,41 @@
     lane = lax.broadcasted_iota(jnp.int32, (BLK, width), 1)
     seen = info_ref[3 + late] * BLK + row <= base + lane % TILE
 
+    piece = 2 * BLK
     for p in range(heads // 2):
         q = jnp.concatenate([queries[2 * p], queries[2 * p + 1]], axis=1)
-        s = jnp.dot(keys[...], q, preferred_element_type=jnp.float32)
-        last = jnp.where(seen, s[n_keys - BLK :], NEGATIVE)
-        top = jnp.maximum(
-            jnp.max(s[: n_keys - BLK], axis=0, keepdims=True), jnp.max(last, axis=0, keepdims=True)
-        )
-        w = jnp.exp2((jnp.concatenate([s[: n_keys - BLK], last], axis=0) - top) * EXP_SCALE)
-        total = jnp.sum(w, axis=0, keepdims=True)
-        o = jnp.dot(values_t[...], w.astype(jnp.bfloat16), preferred_element_type=jnp.float32)
+        top = jnp.full((1, width), NEGATIVE, jnp.float32)
+        pieces = []
+        for at in range(0, n_keys, piece):
+            s = jnp.dot(keys[at : at + piece, :], q, preferred_element_type=jnp.float32)
+            if at + piece == n_keys:
+                s = jnp.concatenate([s[: piece - BLK], jnp.where(seen, s[piece - BLK :], NEGATIVE)], axis=0)
+            pieces.append(s)
+            top = jnp.maximum(top, jnp.max(s, axis=0, keepdims=True))
+        top = top * EXP_SCALE
+        total = jnp.zeros((1, width), jnp.float32)
+        o = jnp.zeros((DV, width), jnp.float32)
+        for n, s in enumerate(pieces):
+            w = jnp.exp2(s * EXP_SCALE - top)
+            total = total + jnp.sum(w, axis=0, keepdims=True)
+            o = o + jnp.dot(
+                values_t[:, n * piece : (n + 1) * piece], w.astype(jnp.bfloat16), preferred_element_type=jnp.float32
+            )
         gate = jnp.concatenate([gate_ref[heads + 2 * p], gate_ref[heads + 2 * p + 1]], axis=1)
         o = o * (gate / total)
+        both = []
         for i in range(2):
             h = 2 * p + i
             gap = lse2_ref[h] - lse_ref[h]
-            both = o[:, i * TILE : (i + 1) * TILE] + coarse[h] * (gate_ref[h] / (1.0 + jnp.exp2(gap)))
-            both = both + coarse2[h].astype(jnp.float32) * (gate_ref[h] / (1.0 + jnp.exp2(-gap)))
-            attended[:, h * DV : (h + 1) * DV] = both.T.astype(jnp.bfloat16)
+            out = o[:, i * TILE : (i + 1) * TILE] + coarse[h] * (gate_ref[h] / (1.0 + jnp.exp2(gap)))
+            out = out + coarse2[h].astype(jnp.float32) * (gate_ref[h] / (1.0 + jnp.exp2(-gap)))
+            both.append(out.T.astype(jnp.bfloat16))
+        attended[:, 2 * p * DV : 2 * (p + 1) * DV] = jnp.concatenate(both, axis=1)
+    for copy in weight_copies:
+        copy.wait()
     for k in (*range(1, n_grp), 0):
-        weight_copies[k].wait()
-        part = jnp.dot(attended[...], weight[k], preferred_element_type=jnp.float32)
+        at = pl.multiple_of(lax.rem(grp + k, n_grp) * cols, DV)
+        part = jnp.dot(attended[...], weight[:, pl.ds(at, cols)], preferred_element_type=jnp.float32)
         outs[k][...] = part.astype(outs[k].dtype)
 
 
@@ -282,12 +295,12 @@
                 pltpu.VMEM(queries_t.shape, queries_t.dtype),
                 pltpu.VMEM(coarse[0].shape, coarse[0].dtype),
                 pltpu.VMEM(coarse2[0].shape, coarse2[0].dtype),
-                pltpu.VMEM((n_grp, rows, cols), jnp.bfloat16),
+                pltpu.VMEM((rows, model), jnp.bfloat16),
                 pltpu.VMEM((SEL * BLK, DQK), jnp.bfloat16),
                 pltpu.VMEM((DV, SEL * BLK), jnp.bfloat16),
                 pltpu.VMEM((TILE, rows), jnp.bfloat16),
                 pltpu.SemaphoreType.DMA((3,)),
-                pltpu.SemaphoreType.DMA((n_grp,)),
+                pltpu.SemaphoreType.DMA((4,)),
             ],
         ),
         out_shape=[jax.ShapeDtypeStruct((TILE, cols), jnp.float32)]

time: 137 us -> 132 us (0.964)
  Pallas kernels: 43.1 us -> 38.2 us
    pallas_call x1, Pallas kernels: 13 us -> 8.43 us  [tail(): pl.pallas_call(functools.partial(tail_kernel, n_grp), grid_spec=pltpu.Pre...]
  transfers between devices with their start and end apart: 12 -> 12, of which waited for: 8 -> 8; matrix products, arithmetic and copies ran while one was open for 2% -> 2% of each run, Pallas kernels for 20% -> 21%
where the time goes in v5:
time: 132 us
  waiting for transfers between devices  54.2 us (41%)
  Pallas kernels  38.2 us (29%)
  starting transfers between devices  33.9 us (26%)
  local copies, waits for them, and re-layouts  3.13 us (2%)
  other arithmetic  1.74 us (1%)
    pallas_call x2, Pallas kernels, coarse_half(): pl.pallas_call(coarse_kernel, grid_spec=pltpu.PrefetchScalarGridSpec(num_...  24.7 us
    all_to_all x1, waiting for transfers between devices, shards(): incoming = lax.all_to_all(payload(wanted, blocks), 'seq', 0, 0, tiled=True)  19.7 us
    all_to_all x1, waiting for transfers between devices, shards(): lax.all_to_all(letters(own_list, coarse_keys, coarse_values), 'seq', 0, 0...  10.9 us
    ppermute x6, waiting for transfers between devices, shifted(): lax.ppermute(x, 'seq', [(index(*s), index(s[0], s[1] + dx, s[2] + dc)) fo...  10 us
    all_to_all x1, starting transfers between devices, shards(): lax.all_to_all(letters(own_list, coarse_keys, coarse_values), 'seq', 0, 0...  9.15 us
    ppermute x3, waiting for transfers between devices, shards(): own = own + lax.ppermute(part, 'grp', perm).astype(jnp.float32)  9.13 us
    ppermute x6, starting transfers between devices, shifted(): lax.ppermute(x, 'seq', [(index(*s), index(s[0], s[1] + dx, s[2] + dc)) fo...  8.69 us
    pallas_call x1, Pallas kernels, tail(): pl.pallas_call(functools.partial(tail_kernel, n_grp), grid_spec=pltpu.Pre...  8.43 us
  transfers between devices with their start and end apart: 12, of which 8 were waited for; matrix products, arithmetic and copies ran while one was open for 2% of the time, Pallas kernels for 21%

profile of v5, /device:TPU:1, one launch (start us, length us, event | category | flops | bytes accessed | tf_op | source)
XLA Modules:
  0.0 131.7 jit_solution(3190801939976564429)
XLA Ops:
  0.0 2.4 %letters.1 = bf16[8,168,128]{2,1,0:T(8,128)(2,1)} custom-call(s32[16]{0:T(128)} %bitcast.28, bf16[1,64,192]{2,1,0:T(8,128)(2,1)} %keys_ref.1, bf16[1,64,128]{2,1,0:T(8,128)(2,1)} %values_ref.1), custom_call_target="tpu_custom_call" | custom-call | bytes 344064 | tf_op jit(solution)/shard_map/letters/pallas_call | solution.py:67
  2.4 9.1 %all-to-all-start = ((bf16[8,168,128]{2,1,0:T(8,128)(2,1)}), bf16[8,168,128]{2,1,0:T(8,128)(2,1)}, u32[]{:S(2)}, u32[]{:S(2)}) async-start(bf16[8,168,128]{2,1,0:T(8,128)(2,1)} %letters.1), calls=%async_computation | async-start | bytes 688128 | tf_op jit(solution)/shard_map/all_to_all | solution.py:352
  11.5 1.0 collective-permute-start
  12.5 0.2 copy.12
  13.0 10.9 %all-to-all-done.rest_0_ = bf16[8,168,128]{2,1,0:T(8,128)(2,1)} async-done(((bf16[8,168,128]{2,1,0:T(8,128)(2,1)}), bf16[8,168,128]{2,1,0:T(8,128)(2,1)}, u32[]{:S(2)}, u32[]{:S(2)}) %all-to-all-start) | async-done | bytes 344096 | tf_op jit(solution)/shard_map/all_to_all | solution.py:352
  24.0 0.7 slice_convert_fusion
  24.7 0.7 copy.11
  25.4 6.5 %all-to-all-start.1 = ((s32[8,1,8]{2,1,0:T(1,128)}), s32[8,1,8]{2,1,0:T(1,128)S(1)}, u32[]{:S(2)}, u32[]{:S(2)}) async-start(s32[8,1,8]{2,1,0:T(1,128)} %copy.11), calls=%async_computation.1 | async-start | bytes 8192 | tf_op jit(solution)/shard_map/all_to_all | solution.py:356
  31.9 4.5 %all-to-all-done.1.wanted_ref = s32[8,1,8]{2,1,0:T(1,128)S(1)} async-done(((s32[8,1,8]{2,1,0:T(1,128)}), s32[8,1,8]{2,1,0:T(1,128)S(1)}, u32[]{:S(2)}, u32[]{:S(2)}) %all-to-all-start.1) | async-done | bytes 288 | tf_op jit(solution)/shard_map/all_to_all | solution.py:356
  36.4 0.3 collective-permute-start.1
  36.7 1.8 %collective-permute-start.2 = (bf16[8,168,128]{2,1,0:T(8,128)(2,1)}, bf16[8,168,128]{2,1,0:T(8,128)(2,1)}, u32[]{:S(2)}, u32[]{:S(2)}) collective-permute-start(bf16[8,168,128]{2,1,0:T(8,128)(2,1)} %all-to-all-done.rest_0_), channel_id=1, source_target_pairs={{0,4},{1,5},{2,6},{3,7},{4,0},{5,1},{6,2},{7,3},{8,12},{9,13},{10,... | collective-permute-start | bytes 1032200 | tf_op jit(solution)/shard_map/ppermute | solution.py:48
  38.5 0.9 collective-permute-start.3
  39.4 0.3 fusion.2
  39.8 2.6 %payload.1 = bf16[64,160,128]{2,1,0:T(8,128)(2,1)} custom-call(s32[8,1,8]{2,1,0:T(1,128)S(1)} %all-to-all-done.1.wanted_ref, bf16[16,160,128]{2,1,0:T(8,128)(2,1)S(1)} %maximum_maximum_fusion.blocks_ref), custom_call_target="tpu_custom_call" | custom-call | bytes 5242880 | tf_op jit(solution)/shard_map/payload/pallas_call | solution.py:91
  42.4 5.7 %all-to-all-start.2 = ((bf16[64,160,128]{2,1,0:T(8,128)(2,1)}), bf16[64,160,128]{2,1,0:T(8,128)(2,1)S(1)}, u32[]{:S(2)}, u32[]{:S(2)}) async-start(bf16[64,160,128]{2,1,0:T(8,128)(2,1)} %payload.1), calls=%async_computation.2 | async-start | bytes 5242880 | tf_op jit(solution)/shard_map/all_to_all | solution.py:364
  48.2 5.5 %collective-permute-done.2.rest_2_ = bf16[8,168,128]{2,1,0:T(8,128)(2,1)} collective-permute-done((bf16[8,168,128]{2,1,0:T(8,128)(2,1)}, bf16[8,168,128]{2,1,0:T(8,128)(2,1)}, u32[]{:S(2)}, u32[]{:S(2)}) %collective-permute-start.2) | collective-permute-done | bytes 344096 | tf_op jit(solution)/shard_map/ppermute | solution.py:48
  53.6 4.5 %collective-permute-done.3.rest_3_ = bf16[8,168,128]{2,1,0:T(8,128)(2,1)} collective-permute-done((bf16[8,168,128]{2,1,0:T(8,128)(2,1)}, bf16[8,168,128]{2,1,0:T(8,128)(2,1)}, u32[]{:S(2)}, u32[]{:S(2)}) %collective-permute-start.3) | collective-permute-done | bytes 344096 | tf_op jit(solution)/shard_map/ppermute | solution.py:48
  58.2 1.1 copy-done.4
  59.3 12.4 %coarse.3 = (bf16[16,128,128]{2,1,0:T(8,128)(2,1)S(1)}, f32[16,1,128]{2,1,0:T(1,128)S(1)}) custom-call(s32[3]{0:T(128)S(1)} %get-tuple-element.30.info_ref, bf16[8,168,128]{2,1,0:T(8,128)(2,1)} %all-to-all-done.rest_0_, bf16[8,168,128]{2,1,0:T(8,128)(2,1)} %collective-permute-done.1.rest_1_, bf16[8,168,128]{2,1,0:T(8,128)(2,1)} %collective-permute-done.2.rest_2_, ...), custom_call_target="tpu_custom_call" | custom-call | flops 42949672960 | bytes 3145728 | tf_op jit(solution)/shard_map/coarse/pallas_call | solution.py:161
  71.7 4.5 %collective-permute-start.4 = (f32[16,1,128]{2,1,0:T(1,128)S(1)}, f32[16,1,128]{2,1,0:T(1,128)S(1)}, u32[]{:S(2)}, u32[]{:S(2)}) collective-permute-start(f32[16,1,128]{2,1,0:T(1,128)S(1)} %get-tuple-element.20), channel_id=1, source_target_pairs={{0,1},{1,0},{2,3},{3,2},{4,5},{5,4},{6,7},{7,6},{8,9},{9,8},{10,11... | collective-permute-start | bytes 24584 | tf_op jit(solution)/shard_map/ppermute | solution.py:48
  76.2 0.3 collective-permute-start.5
  76.5 12.4 %coarse.2 = (f32[16,128,128]{2,1,0:T(8,128)S(1)}, f32[16,1,128]{2,1,0:T(1,128)S(1)}) custom-call(s32[3]{0:T(128)S(1)} %get-tuple-element.29.info_ref, bf16[8,168,128]{2,1,0:T(8,128)(2,1)} %all-to-all-done.rest_0_, bf16[8,168,128]{2,1,0:T(8,128)(2,1)} %collective-permute-done.1.rest_1_, bf16[8,168,128]{2,1,0:T(8,128)(2,1)} %collective-permute-done.2.rest_2_, ...), custom_call_target="tpu_custom_call" | custom-call | flops 42949672960 | bytes 3145728 | tf_op jit(solution)/shard_map/coarse/pallas_call | solution.py:161
  88.8 1.0 copy-done.1
  89.8 19.7 %all-to-all-done.2.incoming = bf16[64,160,128]{2,1,0:T(8,128)(2,1)S(1)} async-done(((bf16[64,160,128]{2,1,0:T(8,128)(2,1)}), bf16[64,160,128]{2,1,0:T(8,128)(2,1)S(1)}, u32[]{:S(2)}, u32[]{:S(2)}) %all-to-all-start.2) | async-done | bytes 2621472 | tf_op jit(solution)/shard_map/all_to_all | solution.py:364
  109.5 8.4 %tail.1 = (f32[128,640]{1,0:T(8,128)S(1)}, bf16[128,640]{1,0:T(8,128)(2,1)S(1)}, bf16[128,640]{1,0:T(8,128)(2,1)S(1)}, bf16[128,640]{1,0:T(8,128)(2,1)S(1)}) custom-call(s32[19]{0:T(128)S(1)} %pad_add_fusion.info_ref, bf16[64,160,128]{2,1,0:T(8,128)(2,1)S(1)} %all-to-all-done.2.incoming, bf16[16,192,128]{2,1,0:T(8,128)(2,1)} %bitcast.21, ...), custom_call_target="tpu_custom_call" | custom-call | flops 2684354560 | bytes 10485760 | tf_op jit(solution)/shard_map/tail/pallas_call | solution.py:278
  117.9 2.8 %collective-permute-start.8 = (bf16[128,640]{1,0:T(8,128)(2,1)S(1)}, bf16[128,640]{1,0:T(8,128)(2,1)S(1)}, u32[]{:S(2)}, u32[]{:S(2)}) collective-permute-start(bf16[128,640]{1,0:T(8,128)(2,1)S(1)} %get-tuple-element.26), channel_id=1, source_target_pairs={{0,192},{64,0},{128,64},{192,128},{1,193},{65,1},{129,65},{193,129... | collective-permute-start | bytes 491528 | tf_op jit(solution)/shard_map/ppermute | solution.py:383
  120.7 0.3 collective-permute-start.7
  121.1 0.7 collective-permute-start.6
  121.8 2.1 %collective-permute-done.8 = bf16[128,640]{1,0:T(8,128)(2,1)S(1)} collective-permute-done((bf16[128,640]{1,0:T(8,128)(2,1)S(1)}, bf16[128,640]{1,0:T(8,128)(2,1)S(1)}, u32[]{:S(2)}, u32[]{:S(2)}) %collective-permute-start.8) | collective-permute-done | bytes 163872 | tf_op jit(solution)/shard_map/ppermute | solution.py:383
  123.9 2.7 %collective-permute-done.7 = bf16[128,640]{1,0:T(8,128)(2,1)S(1)} collective-permute-done((bf16[128,640]{1,0:T(8,128)(2,1)S(1)}, bf16[128,640]{1,0:T(8,128)(2,1)S(1)}, u32[]{:S(2)}, u32[]{:S(2)}) %collective-permute-start.7) | collective-permute-done | bytes 163872 | tf_op jit(solution)/shard_map/ppermute | solution.py:383
  126.5 4.4 %collective-permute-done.6 = bf16[128,640]{1,0:T(8,128)(2,1)S(1)} collective-permute-done((bf16[128,640]{1,0:T(8,128)(2,1)S(1)}, bf16[128,640]{1,0:T(8,128)(2,1)S(1)}, u32[]{:S(2)}, u32[]{:S(2)}) %collective-permute-start.6) | collective-permute-done | bytes 163872 | tf_op jit(solution)/shard_map/ppermute | solution.py:383
  130.9 0.8 add_convert_fusion
  (25 shorter events, 0.4 us)
Async XLA Ops:
  0.0 39.4 %copy-start = (bf16[128,2560]{1,0:T(8,128)(2,1)S(1)}, bf16[128,2560]{1,0:T(8,128)(2,1)}, u32[]{:S(2)}) copy-start(bf16[128,2560]{1,0:T(8,128)(2,1)} %param.14) | copy-start | bytes 1966084
  0.0 12.5 %copy-start.5 = (bf16[1,1024,192]{1,2,0:T(8,128)(2,1)S(1)}, bf16[1,1024,192]{1,2,0:T(8,128)(2,1)}, u32[]{:S(2)}) copy-start(bf16[1,1024,192]{1,2,0:T(8,128)(2,1)} %param.10) | copy-start | bytes 1179652
  2.4 10.6 %copy-start.6 = (bf16[1,1024,128]{2,1,0:T(8,128)(2,1)S(1)}, bf16[1,1024,128]{2,1,0:T(8,128)(2,1)}, u32[]{:S(2)}) copy-start(bf16[1,1024,128]{2,1,0:T(8,128)(2,1)} %param.11) | copy-start | bytes 786436
  2.4 21.6 %all-to-all-start = ((bf16[8,168,128]{2,1,0:T(8,128)(2,1)}), bf16[8,168,128]{2,1,0:T(8,128)(2,1)}, u32[]{:S(2)}, u32[]{:S(2)}) async-start(bf16[8,168,128]{2,1,0:T(8,128)(2,1)} %letters.1), calls=%async_computation | async-start | bytes 688128 | tf_op jit(solution)/shard_map/all_to_all | solution.py:352
  11.5 24.9 %collective-permute-start = (bf16[16,192,128]{2,1,0:T(8,128)(2,1)}, bf16[16,192,128]{2,1,0:T(8,128)(2,1)S(1)}, u32[]{:S(2)}, u32[]{:S(2)}) collective-permute-start(bf16[16,192,128]{2,1,0:T(8,128)(2,1)} %bitcast.20), channel_id=1, source_target_pairs={{0,1},{1,0},{2,3},{3,2},{4,5},{5,4},{6,7},{7,6},{8,9},{9,8},{10,11... | collective-permute-start | bytes 2359304 | tf_op jit(solution)/shard_map/ppermute | solution.py:48
  12.7 26.7 %copy-start.8 = (s32[1,1,16]{2,1,0:T(1,128)S(1)}, s32[1,1,16]{2,1,0:T(1,128)}, u32[]{:S(2)}) copy-start(s32[1,1,16]{2,1,0:T(1,128)} %param.17) | copy-start | bytes 196
  12.7 26.7 %copy-start.7 = (bf16[1,2560,32]{1,2,0:T(8,128)(2,1)S(1)}, bf16[1,2560,32]{1,2,0:T(8,128)(2,1)}, u32[]{:S(2)}) copy-start(bf16[1,2560,32]{1,2,0:T(8,128)(2,1)} %param.15) | copy-start | bytes 491524
  25.4 11.0 %all-to-all-start.1 = ((s32[8,1,8]{2,1,0:T(1,128)}), s32[8,1,8]{2,1,0:T(1,128)S(1)}, u32[]{:S(2)}, u32[]{:S(2)}) async-start(s32[8,1,8]{2,1,0:T(1,128)} %copy.11), calls=%async_computation.1 | async-start | bytes 8192 | tf_op jit(solution)/shard_map/all_to_all | solution.py:356
  36.4 6.0 %copy-start.3 = (bf16[16,192,128]{2,1,0:T(8,128)(2,1)}, bf16[16,192,128]{2,1,0:T(8,128)(2,1)S(1)}, u32[]{:S(2)}) copy-start(bf16[16,192,128]{2,1,0:T(8,128)(2,1)S(1)} %collective-permute-done.rest_4_) | copy-start | bytes 2359300
  36.4 11.8 %collective-permute-start.1 = (bf16[8,168,128]{2,1,0:T(8,128)(2,1)}, bf16[8,168,128]{2,1,0:T(8,128)(2,1)}, u32[]{:S(2)}, u32[]{:S(2)}) collective-permute-start(bf16[8,168,128]{2,1,0:T(8,128)(2,1)} %all-to-all-done.rest_0_), channel_id=1, source_target_pairs={{0,2},{1,3},{2,4},{3,5},{4,6},{5,7},{6,0},{7,1},{8,10},{9,11},{10,... | collective-permute-start | bytes 1032200 | tf_op jit(solution)/shard_map/ppermute | solution.py:48
  36.7 17.0 %collective-permute-start.2 = (bf16[8,168,128]{2,1,0:T(8,128)(2,1)}, bf16[8,168,128]{2,1,0:T(8,128)(2,1)}, u32[]{:S(2)}, u32[]{:S(2)}) collective-permute-start(bf16[8,168,128]{2,1,0:T(8,128)(2,1)} %all-to-all-done.rest_0_), channel_id=1, source_target_pairs={{0,4},{1,5},{2,6},{3,7},{4,0},{5,1},{6,2},{7,3},{8,12},{9,13},{10,... | collective-permute-start | bytes 1032200 | tf_op jit(solution)/shard_map/ppermute | solution.py:48
  38.5 19.7 %collective-permute-start.3 = (bf16[8,168,128]{2,1,0:T(8,128)(2,1)}, bf16[8,168,128]{2,1,0:T(8,128)(2,1)}, u32[]{:S(2)}, u32[]{:S(2)}) collective-permute-start(bf16[8,168,128]{2,1,0:T(8,128)(2,1)} %all-to-all-done.rest_0_), channel_id=1, source_target_pairs={{0,6},{1,7},{2,0},{3,1},{4,2},{5,3},{6,4},{7,5},{8,14},{9,15},{10,... | collective-permute-start | bytes 1032200 | tf_op jit(solution)/shard_map/ppermute | solution.py:48
  42.4 67.1 %all-to-all-start.2 = ((bf16[64,160,128]{2,1,0:T(8,128)(2,1)}), bf16[64,160,128]{2,1,0:T(8,128)(2,1)S(1)}, u32[]{:S(2)}, u32[]{:S(2)}) async-start(bf16[64,160,128]{2,1,0:T(8,128)(2,1)} %payload.1), calls=%async_computation.2 | async-start | bytes 5242880 | tf_op jit(solution)/shard_map/all_to_all | solution.py:364
  58.2 1.1 copy-start.4
  59.3 17.2 %copy-start.2 = (bf16[128,16,192]{0,2,1:T(8,128)(2,1)S(1)}, bf16[128,16,192]{0,2,1:T(8,128)(2,1)}, u32[]{:S(2)}) copy-start(bf16[128,16,192]{0,2,1:T(8,128)(2,1)} %param.9) | copy-start | bytes 2359300
  71.7 18.2 %collective-permute-start.4 = (f32[16,1,128]{2,1,0:T(1,128)S(1)}, f32[16,1,128]{2,1,0:T(1,128)S(1)}, u32[]{:S(2)}, u32[]{:S(2)}) collective-permute-start(f32[16,1,128]{2,1,0:T(1,128)S(1)} %get-tuple-element.20), channel_id=1, source_target_pairs={{0,1},{1,0},{2,3},{3,2},{4,5},{5,4},{6,7},{7,6},{8,9},{9,8},{10,11... | collective-permute-start | bytes 24584 | tf_op jit(solution)/shard_map/ppermute | solution.py:48
  76.2 13.7 %collective-permute-start.5 = (bf16[16,128,128]{2,1,0:T(8,128)(2,1)S(1)}, bf16[16,128,128]{2,1,0:T(8,128)(2,1)}, u32[]{:S(2)}, u32[]{:S(2)}) collective-permute-start(bf16[16,128,128]{2,1,0:T(8,128)(2,1)S(1)} %get-tuple-element.22), channel_id=1, source_target_pairs={{0,1},{1,0},{2,3},{3,2},{4,5},{5,4},{6,7},{7,6},{8,9},{9,8},{10,11... | collective-permute-start | bytes 1572872 | tf_op jit(solution)/shard_map/ppermute | solution.py:48
  88.8 1.0 copy-start.1
  117.9 5.9 %collective-permute-start.8 = (bf16[128,640]{1,0:T(8,128)(2,1)S(1)}, bf16[128,640]{1,0:T(8,128)(2,1)S(1)}, u32[]{:S(2)}, u32[]{:S(2)}) collective-permute-start(bf16[128,640]{1,0:T(8,128)(2,1)S(1)} %get-tuple-element.26), channel_id=1, source_target_pairs={{0,192},{64,0},{128,64},{192,128},{1,193},{65,1},{129,65},{193,129... | collective-permute-start | bytes 491528 | tf_op jit(solution)/shard_map/ppermute | solution.py:383
  120.7 5.8 %collective-permute-start.7 = (bf16[128,640]{1,0:T(8,128)(2,1)S(1)}, bf16[128,640]{1,0:T(8,128)(2,1)S(1)}, u32[]{:S(2)}, u32[]{:S(2)}) collective-permute-start(bf16[128,640]{1,0:T(8,128)(2,1)S(1)} %get-tuple-element.25), channel_id=1, source_target_pairs={{0,128},{64,192},{128,0},{192,64},{1,129},{65,193},{129,1},{193,65... | collective-permute-start | bytes 491528 | tf_op jit(solution)/shard_map/ppermute | solution.py:383
  121.1 9.8 %collective-permute-start.6 = (bf16[128,640]{1,0:T(8,128)(2,1)S(1)}, bf16[128,640]{1,0:T(8,128)(2,1)S(1)}, u32[]{:S(2)}, u32[]{:S(2)}) collective-permute-start(bf16[128,640]{1,0:T(8,128)(2,1)S(1)} %get-tuple-element.24), channel_id=1, source_target_pairs={{0,64},{64,128},{128,192},{192,0},{1,65},{65,129},{129,193},{193,1... | collective-permute-start | bytes 491528 | tf_op jit(solution)/shard_map/ppermute | solution.py:383

commit v6 on v5

--- a/solution.py
+++ b/solution.py
@@ -19,7 +19,7 @@
 LETTER = PACK + 8
 OWNED_BITS = 4
 OWNED = 1 << OWNED_BITS
-EARLY = 16
+EARLY = 9.62
 NEGATIVE = -1e30
 EXP_SCALE = DQK**-0.5 * math.log2(math.e)
 Z, X, C = 8, 4, 2
@@ -179,9 +179,9 @@
             jax.ShapeDtypeStruct((heads, 1, TILE), jnp.float32),
         ],
         cost_estimate=pl.CostEstimate(
-            flops=EARLY * 2 * heads * TILE * tokens * (DQK + DV),
+            flops=int(EARLY * 2 * heads * TILE) * tokens * (DQK + DV),
             bytes_accessed=tokens * (DQK + DV) * 2 + heads * TILE * (DQK * 2 + DV * 4),
-            transcendentals=EARLY * heads * TILE * tokens,
+            transcendentals=int(EARLY * heads * TILE * tokens),
         ),
         compiler_params=pltpu.CompilerParams(vmem_limit_bytes=20 << 20),
         name="coarse",
@@ -353,9 +353,8 @@
         letters(own_list, coarse_keys, coarse_values), "seq", 0, 0, axis_index_groups=ALONG_Z, tiled=True
     )
     wanted = jnp.transpose(came[:, PACK, : X * C])[:, None, :].astype(jnp.int32)
+    column, wanted, other_q = lax.optimization_barrier((came, wanted, other_q))
     wanted = lax.all_to_all(wanted, "seq", 0, 0, axis_index_groups=IN_PLANE, tiled=True)
-
-    column, wanted, other_q = lax.optimization_barrier((came, wanted, other_q))
     coarse = [column] + [shifted(column, k, 0) for k in range(1, X)]
 
     blocks = packed_blocks(

time: 132 us -> 130 us (0.985)
  waiting for transfers between devices: 54.2 us -> 50.9 us
    all_to_all x1, waiting for transfers between devices: 4.5 us -> 0.01 us  [shards(): lax.all_to_all(wanted, 'seq', 0, 0, axis_index_groups=IN_PLANE, tiled=True)]
    all_to_all x1, waiting for transfers between devices: 19.7 us -> 23 us  [shards(): incoming = lax.all_to_all(payload(wanted, blocks), 'seq', 0, 0, tiled=True)]
    ppermute x6, waiting for transfers between devices: 10 us -> 7.68 us  [shifted(): lax.ppermute(x, 'seq', [(index(*s), index(s[0], s[1] + dx, s[2] + dc)) fo...]
  transfers between devices with their start and end apart: 12 -> 12, of which waited for: 8 -> 7; matrix products, arithmetic and copies ran while one was open for 2% -> 2% of each run, Pallas kernels for 21% -> 21%
where the time goes in v6:
time: 130 us
  waiting for transfers between devices  50.9 us (39%)
  Pallas kernels  38.2 us (29%)
  starting transfers between devices  34.5 us (27%)
  local copies, waits for them, and re-layouts  3.99 us (3%)
  other arithmetic  1.74 us (1%)
    pallas_call x2, Pallas kernels, coarse_half(): pl.pallas_call(coarse_kernel, grid_spec=pltpu.PrefetchScalarGridSpec(num_...  24.7 us
    all_to_all x1, waiting for transfers between devices, shards(): incoming = lax.all_to_all(payload(wanted, blocks), 'seq', 0, 0, tiled=True)  23 us
    all_to_all x1, waiting for transfers between devices, shards(): lax.all_to_all(letters(own_list, coarse_keys, coarse_values), 'seq', 0, 0...  11 us
    ppermute x6, starting transfers between devices, shifted(): lax.ppermute(x, 'seq', [(index(*s), index(s[0], s[1] + dx, s[2] + dc)) fo...  9.47 us
    ppermute x3, waiting for transfers between devices, shards(): own = own + lax.ppermute(part, 'grp', perm).astype(jnp.float32)  9.28 us
    all_to_all x1, starting transfers between devices, shards(): lax.all_to_all(letters(own_list, coarse_keys, coarse_values), 'seq', 0, 0...  9.15 us
    pallas_call x1, Pallas kernels, tail(): pl.pallas_call(functools.partial(tail_kernel, n_grp), grid_spec=pltpu.Pre...  8.43 us
    ppermute x6, waiting for transfers between devices, shifted(): lax.ppermute(x, 'seq', [(index(*s), index(s[0], s[1] + dx, s[2] + dc)) fo...  7.68 us
  transfers between devices with their start and end apart: 12, of which 7 were waited for; matrix products, arithmetic and copies ran while one was open for 2% of the time, Pallas kernels for 21%

profile of v6, /device:TPU:1, one launch (start us, length us, event | category | flops | bytes accessed | tf_op | source)
XLA Modules:
  0.0 129.7 jit_solution(15918659648017057198)
XLA Ops:
  0.0 2.4 %letters.1 = bf16[8,168,128]{2,1,0:T(8,128)(2,1)} custom-call(s32[16]{0:T(128)} %bitcast.28, bf16[1,64,192]{2,1,0:T(8,128)(2,1)} %keys_ref.1, bf16[1,64,128]{2,1,0:T(8,128)(2,1)} %values_ref.1), custom_call_target="tpu_custom_call" | custom-call | bytes 344064 | tf_op jit(solution)/shard_map/letters/pallas_call | solution.py:67
  2.4 9.1 %all-to-all-start = ((bf16[8,168,128]{2,1,0:T(8,128)(2,1)}), bf16[8,168,128]{2,1,0:T(8,128)(2,1)}, u32[]{:S(2)}, u32[]{:S(2)}) async-start(bf16[8,168,128]{2,1,0:T(8,128)(2,1)} %letters.1), calls=%async_computation | async-start | bytes 688128 | tf_op jit(solution)/shard_map/all_to_all | solution.py:352
  11.5 1.0 collective-permute-start
  12.5 0.2 copy.12
  13.0 11.0 %all-to-all-done.rest_0_ = bf16[8,168,128]{2,1,0:T(8,128)(2,1)} async-done(((bf16[8,168,128]{2,1,0:T(8,128)(2,1)}), bf16[8,168,128]{2,1,0:T(8,128)(2,1)}, u32[]{:S(2)}, u32[]{:S(2)}) %all-to-all-start) | async-done | bytes 344096 | tf_op jit(solution)/shard_map/all_to_all | solution.py:352
  24.0 0.7 slice_convert_fusion
  24.7 0.7 copy.10
  25.4 0.9 copy-done.3
  26.3 6.5 %all-to-all-start.1 = ((s32[8,1,8]{2,1,0:T(1,128)}), s32[8,1,8]{2,1,0:T(1,128)S(1)}, u32[]{:S(2)}, u32[]{:S(2)}) async-start(s32[8,1,8]{2,1,0:T(1,128)} %bitcast.8), calls=%async_computation.1 | async-start | bytes 8192 | tf_op jit(solution)/shard_map/all_to_all | solution.py:357
  32.8 1.4 %collective-permute-start.1 = (bf16[8,168,128]{2,1,0:T(8,128)(2,1)}, bf16[8,168,128]{2,1,0:T(8,128)(2,1)}, u32[]{:S(2)}, u32[]{:S(2)}) collective-permute-start(bf16[8,168,128]{2,1,0:T(8,128)(2,1)} %all-to-all-done.rest_0_), channel_id=1, source_target_pairs={{0,2},{1,3},{2,4},{3,5},{4,6},{5,7},{6,0},{7,1},{8,10},{9,11},{10,... | collective-permute-start | bytes 1032200 | tf_op jit(solution)/shard_map/ppermute | solution.py:48
  34.2 2.4 %collective-permute-start.2 = (bf16[8,168,128]{2,1,0:T(8,128)(2,1)}, bf16[8,168,128]{2,1,0:T(8,128)(2,1)}, u32[]{:S(2)}, u32[]{:S(2)}) collective-permute-start(bf16[8,168,128]{2,1,0:T(8,128)(2,1)} %all-to-all-done.rest_0_), channel_id=1, source_target_pairs={{0,4},{1,5},{2,6},{3,7},{4,0},{5,1},{6,2},{7,3},{8,12},{9,13},{10,... | collective-permute-start | bytes 1032200 | tf_op jit(solution)/shard_map/ppermute | solution.py:48
  36.6 1.2 collective-permute-start.3
  37.8 2.6 %payload.1 = bf16[64,160,128]{2,1,0:T(8,128)(2,1)} custom-call(s32[8,1,8]{2,1,0:T(1,128)S(1)} %all-to-all-done.1.wanted_ref, bf16[16,160,128]{2,1,0:T(8,128)(2,1)S(1)} %maximum_maximum_fusion.blocks_ref), custom_call_target="tpu_custom_call" | custom-call | bytes 5242880 | tf_op jit(solution)/shard_map/payload/pallas_call | solution.py:91
  40.4 5.5 %all-to-all-start.2 = ((bf16[64,160,128]{2,1,0:T(8,128)(2,1)}), bf16[64,160,128]{2,1,0:T(8,128)(2,1)S(1)}, u32[]{:S(2)}, u32[]{:S(2)}) async-start(bf16[64,160,128]{2,1,0:T(8,128)(2,1)} %payload.1), calls=%async_computation.2 | async-start | bytes 5242880 | tf_op jit(solution)/shard_map/all_to_all | solution.py:363
  46.0 0.3 fusion.2
  46.3 6.1 %collective-permute-done.2.rest_2_ = bf16[8,168,128]{2,1,0:T(8,128)(2,1)} collective-permute-done((bf16[8,168,128]{2,1,0:T(8,128)(2,1)}, bf16[8,168,128]{2,1,0:T(8,128)(2,1)}, u32[]{:S(2)}, u32[]{:S(2)}) %collective-permute-start.2) | collective-permute-done | bytes 344096 | tf_op jit(solution)/shard_map/ppermute | solution.py:48
  52.4 1.6 %collective-permute-done.3.rest_3_ = bf16[8,168,128]{2,1,0:T(8,128)(2,1)} collective-permute-done((bf16[8,168,128]{2,1,0:T(8,128)(2,1)}, bf16[8,168,128]{2,1,0:T(8,128)(2,1)}, u32[]{:S(2)}, u32[]{:S(2)}) %collective-permute-start.3) | collective-permute-done | bytes 344096 | tf_op jit(solution)/shard_map/ppermute | solution.py:48
  54.0 1.1 copy-done.4
  55.1 12.4 %coarse.3 = (bf16[16,128,128]{2,1,0:T(8,128)(2,1)S(1)}, f32[16,1,128]{2,1,0:T(1,128)S(1)}) custom-call(s32[3]{0:T(128)S(1)} %get-tuple-element.30.info_ref, bf16[8,168,128]{2,1,0:T(8,128)(2,1)} %all-to-all-done.rest_0_, bf16[8,168,128]{2,1,0:T(8,128)(2,1)} %collective-permute-done.1.rest_1_, bf16[8,168,128]{2,1,0:T(8,128)(2,1)} %collective-permute-done.2.rest_2_, ...), custom_call_target="tpu_custom_call" | custom-call | flops 25823150080 | bytes 3145728 | tf_op jit(solution)/shard_map/coarse/pallas_call | solution.py:161
  67.5 3.3 %collective-permute-start.4 = (f32[16,1,128]{2,1,0:T(1,128)S(1)}, f32[16,1,128]{2,1,0:T(1,128)S(1)}, u32[]{:S(2)}, u32[]{:S(2)}) collective-permute-start(f32[16,1,128]{2,1,0:T(1,128)S(1)} %get-tuple-element.20), channel_id=1, source_target_pairs={{0,1},{1,0},{2,3},{3,2},{4,5},{5,4},{6,7},{7,6},{8,9},{9,8},{10,11... | collective-permute-start | bytes 24584 | tf_op jit(solution)/shard_map/ppermute | solution.py:48
  70.8 0.3 collective-permute-start.5
  71.1 12.4 %coarse.2 = (f32[16,128,128]{2,1,0:T(8,128)S(1)}, f32[16,1,128]{2,1,0:T(1,128)S(1)}) custom-call(s32[3]{0:T(128)S(1)} %get-tuple-element.29.info_ref, bf16[8,168,128]{2,1,0:T(8,128)(2,1)} %all-to-all-done.rest_0_, bf16[8,168,128]{2,1,0:T(8,128)(2,1)} %collective-permute-done.1.rest_1_, bf16[8,168,128]{2,1,0:T(8,128)(2,1)} %collective-permute-done.2.rest_2_, ...), custom_call_target="tpu_custom_call" | custom-call | flops 25823150080 | bytes 3145728 | tf_op jit(solution)/shard_map/coarse/pallas_call | solution.py:161
  83.4 1.0 copy-done.1
  84.4 23.0 %all-to-all-done.2.incoming = bf16[64,160,128]{2,1,0:T(8,128)(2,1)S(1)} async-done(((bf16[64,160,128]{2,1,0:T(8,128)(2,1)}), bf16[64,160,128]{2,1,0:T(8,128)(2,1)S(1)}, u32[]{:S(2)}, u32[]{:S(2)}) %all-to-all-start.2) | async-done | bytes 2621472 | tf_op jit(solution)/shard_map/all_to_all | solution.py:363
  107.4 8.4 %tail.1 = (f32[128,640]{1,0:T(8,128)S(1)}, bf16[128,640]{1,0:T(8,128)(2,1)S(1)}, bf16[128,640]{1,0:T(8,128)(2,1)S(1)}, bf16[128,640]{1,0:T(8,128)(2,1)S(1)}) custom-call(s32[19]{0:T(128)S(1)} %pad_add_fusion.info_ref, bf16[64,160,128]{2,1,0:T(8,128)(2,1)S(1)} %all-to-all-done.2.incoming, bf16[16,192,128]{2,1,0:T(8,128)(2,1)} %bitcast.21, ...), custom_call_target="tpu_custom_call" | custom-call | flops 2684354560 | bytes 10485760 | tf_op jit(solution)/shard_map/tail/pallas_call | solution.py:278
  115.8 2.8 %collective-permute-start.8 = (bf16[128,640]{1,0:T(8,128)(2,1)S(1)}, bf16[128,640]{1,0:T(8,128)(2,1)S(1)}, u32[]{:S(2)}, u32[]{:S(2)}) collective-permute-start(bf16[128,640]{1,0:T(8,128)(2,1)S(1)} %get-tuple-element.26), channel_id=1, source_target_pairs={{0,192},{64,0},{128,64},{192,128},{1,193},{65,1},{129,65},{193,129... | collective-permute-start | bytes 491528 | tf_op jit(solution)/shard_map/ppermute | solution.py:382
  118.7 0.3 collective-permute-start.7
  119.0 0.7 collective-permute-start.6
  119.7 2.2 %collective-permute-done.8 = bf16[128,640]{1,0:T(8,128)(2,1)S(1)} collective-permute-done((bf16[128,640]{1,0:T(8,128)(2,1)S(1)}, bf16[128,640]{1,0:T(8,128)(2,1)S(1)}, u32[]{:S(2)}, u32[]{:S(2)}) %collective-permute-start.8) | collective-permute-done | bytes 163872 | tf_op jit(solution)/shard_map/ppermute | solution.py:382
  121.9 2.5 %collective-permute-done.7 = bf16[128,640]{1,0:T(8,128)(2,1)S(1)} collective-permute-done((bf16[128,640]{1,0:T(8,128)(2,1)S(1)}, bf16[128,640]{1,0:T(8,128)(2,1)S(1)}, u32[]{:S(2)}, u32[]{:S(2)}) %collective-permute-start.7) | collective-permute-done | bytes 163872 | tf_op jit(solution)/shard_map/ppermute | solution.py:382
  124.4 4.5 %collective-permute-done.6 = bf16[128,640]{1,0:T(8,128)(2,1)S(1)} collective-permute-done((bf16[128,640]{1,0:T(8,128)(2,1)S(1)}, bf16[128,640]{1,0:T(8,128)(2,1)S(1)}, u32[]{:S(2)}, u32[]{:S(2)}) %collective-permute-start.6) | collective-permute-done | bytes 163872 | tf_op jit(solution)/shard_map/ppermute | solution.py:382
  129.0 0.8 add_convert_fusion
  (25 shorter events, 0.4 us)
Async XLA Ops:
  0.0 46.0 %copy-start = (bf16[128,2560]{1,0:T(8,128)(2,1)S(1)}, bf16[128,2560]{1,0:T(8,128)(2,1)}, u32[]{:S(2)}) copy-start(bf16[128,2560]{1,0:T(8,128)(2,1)} %param.14) | copy-start | bytes 1966084
  0.0 12.5 %copy-start.5 = (bf16[1,1024,192]{1,2,0:T(8,128)(2,1)S(1)}, bf16[1,1024,192]{1,2,0:T(8,128)(2,1)}, u32[]{:S(2)}) copy-start(bf16[1,1024,192]{1,2,0:T(8,128)(2,1)} %param.10) | copy-start | bytes 1179652
  2.4 10.5 %copy-start.6 = (bf16[1,1024,128]{2,1,0:T(8,128)(2,1)S(1)}, bf16[1,1024,128]{2,1,0:T(8,128)(2,1)}, u32[]{:S(2)}) copy-start(bf16[1,1024,128]{2,1,0:T(8,128)(2,1)} %param.11) | copy-start | bytes 786436
  2.4 21.6 %all-to-all-start = ((bf16[8,168,128]{2,1,0:T(8,128)(2,1)}), bf16[8,168,128]{2,1,0:T(8,128)(2,1)}, u32[]{:S(2)}, u32[]{:S(2)}) async-start(bf16[8,168,128]{2,1,0:T(8,128)(2,1)} %letters.1), calls=%async_computation | async-start | bytes 688128 | tf_op jit(solution)/shard_map/all_to_all | solution.py:352
  11.5 13.9 %collective-permute-start = (bf16[16,192,128]{2,1,0:T(8,128)(2,1)}, bf16[16,192,128]{2,1,0:T(8,128)(2,1)S(1)}, u32[]{:S(2)}, u32[]{:S(2)}) collective-permute-start(bf16[16,192,128]{2,1,0:T(8,128)(2,1)} %bitcast.20), channel_id=1, source_target_pairs={{0,1},{1,0},{2,3},{3,2},{4,5},{5,4},{6,7},{7,6},{8,9},{9,8},{10,11... | collective-permute-start | bytes 2359304 | tf_op jit(solution)/shard_map/ppermute | solution.py:48
  25.4 0.9 copy-start.3
  26.3 11.5 %all-to-all-start.1 = ((s32[8,1,8]{2,1,0:T(1,128)}), s32[8,1,8]{2,1,0:T(1,128)S(1)}, u32[]{:S(2)}, u32[]{:S(2)}) async-start(s32[8,1,8]{2,1,0:T(1,128)} %bitcast.8), calls=%async_computation.1 | async-start | bytes 8192 | tf_op jit(solution)/shard_map/all_to_all | solution.py:357
  32.8 13.5 %collective-permute-start.1 = (bf16[8,168,128]{2,1,0:T(8,128)(2,1)}, bf16[8,168,128]{2,1,0:T(8,128)(2,1)}, u32[]{:S(2)}, u32[]{:S(2)}) collective-permute-start(bf16[8,168,128]{2,1,0:T(8,128)(2,1)} %all-to-all-done.rest_0_), channel_id=1, source_target_pairs={{0,2},{1,3},{2,4},{3,5},{4,6},{5,7},{6,0},{7,1},{8,10},{9,11},{10,... | collective-permute-start | bytes 1032200 | tf_op jit(solution)/shard_map/ppermute | solution.py:48
  34.2 18.2 %collective-permute-start.2 = (bf16[8,168,128]{2,1,0:T(8,128)(2,1)}, bf16[8,168,128]{2,1,0:T(8,128)(2,1)}, u32[]{:S(2)}, u32[]{:S(2)}) collective-permute-start(bf16[8,168,128]{2,1,0:T(8,128)(2,1)} %all-to-all-done.rest_0_), channel_id=1, source_target_pairs={{0,4},{1,5},{2,6},{3,7},{4,0},{5,1},{6,2},{7,3},{8,12},{9,13},{10,... | collective-permute-start | bytes 1032200 | tf_op jit(solution)/shard_map/ppermute | solution.py:48
  36.6 17.4 %collective-permute-start.3 = (bf16[8,168,128]{2,1,0:T(8,128)(2,1)}, bf16[8,168,128]{2,1,0:T(8,128)(2,1)}, u32[]{:S(2)}, u32[]{:S(2)}) collective-permute-start(bf16[8,168,128]{2,1,0:T(8,128)(2,1)} %all-to-all-done.rest_0_), channel_id=1, source_target_pairs={{0,6},{1,7},{2,0},{3,1},{4,2},{5,3},{6,4},{7,5},{8,14},{9,15},{10,... | collective-permute-start | bytes 1032200 | tf_op jit(solution)/shard_map/ppermute | solution.py:48
  40.4 5.5 %copy-start.8 = (s32[1,1,16]{2,1,0:T(1,128)S(1)}, s32[1,1,16]{2,1,0:T(1,128)}, u32[]{:S(2)}) copy-start(s32[1,1,16]{2,1,0:T(1,128)} %param.17) | copy-start | bytes 196
  40.4 5.6 %copy-start.7 = (bf16[1,2560,32]{1,2,0:T(8,128)(2,1)S(1)}, bf16[1,2560,32]{1,2,0:T(8,128)(2,1)}, u32[]{:S(2)}) copy-start(bf16[1,2560,32]{1,2,0:T(8,128)(2,1)} %param.15) | copy-start | bytes 491524
  40.4 67.0 %all-to-all-start.2 = ((bf16[64,160,128]{2,1,0:T(8,128)(2,1)}), bf16[64,160,128]{2,1,0:T(8,128)(2,1)S(1)}, u32[]{:S(2)}, u32[]{:S(2)}) async-start(bf16[64,160,128]{2,1,0:T(8,128)(2,1)} %payload.1), calls=%async_computation.2 | async-start | bytes 5242880 | tf_op jit(solution)/shard_map/all_to_all | solution.py:363
  54.0 1.1 copy-start.4
  55.1 15.9 %copy-start.2 = (bf16[128,16,192]{0,2,1:T(8,128)(2,1)S(1)}, bf16[128,16,192]{0,2,1:T(8,128)(2,1)}, u32[]{:S(2)}) copy-start(bf16[128,16,192]{0,2,1:T(8,128)(2,1)} %param.9) | copy-start | bytes 2359300
  67.5 16.9 %collective-permute-start.4 = (f32[16,1,128]{2,1,0:T(1,128)S(1)}, f32[16,1,128]{2,1,0:T(1,128)S(1)}, u32[]{:S(2)}, u32[]{:S(2)}) collective-permute-start(f32[16,1,128]{2,1,0:T(1,128)S(1)} %get-tuple-element.20), channel_id=1, source_target_pairs={{0,1},{1,0},{2,3},{3,2},{4,5},{5,4},{6,7},{7,6},{8,9},{9,8},{10,11... | collective-permute-start | bytes 24584 | tf_op jit(solution)/shard_map/ppermute | solution.py:48
  70.8 13.6 %collective-permute-start.5 = (bf16[16,128,128]{2,1,0:T(8,128)(2,1)S(1)}, bf16[16,128,128]{2,1,0:T(8,128)(2,1)}, u32[]{:S(2)}, u32[]{:S(2)}) collective-permute-start(bf16[16,128,128]{2,1,0:T(8,128)(2,1)S(1)} %get-tuple-element.22), channel_id=1, source_target_pairs={{0,1},{1,0},{2,3},{3,2},{4,5},{5,4},{6,7},{7,6},{8,9},{9,8},{10,11... | collective-permute-start | bytes 1572872 | tf_op jit(solution)/shard_map/ppermute | solution.py:48
  83.4 1.0 copy-start.1
  115.8 6.1 %collective-permute-start.8 = (bf16[128,640]{1,0:T(8,128)(2,1)S(1)}, bf16[128,640]{1,0:T(8,128)(2,1)S(1)}, u32[]{:S(2)}, u32[]{:S(2)}) collective-permute-start(bf16[128,640]{1,0:T(8,128)(2,1)S(1)} %get-tuple-element.26), channel_id=1, source_target_pairs={{0,192},{64,0},{128,64},{192,128},{1,193},{65,1},{129,65},{193,129... | collective-permute-start | bytes 491528 | tf_op jit(solution)/shard_map/ppermute | solution.py:382
  118.7 5.8 %collective-permute-start.7 = (bf16[128,640]{1,0:T(8,128)(2,1)S(1)}, bf16[128,640]{1,0:T(8,128)(2,1)S(1)}, u32[]{:S(2)}, u32[]{:S(2)}) collective-permute-start(bf16[128,640]{1,0:T(8,128)(2,1)S(1)} %get-tuple-element.25), channel_id=1, source_target_pairs={{0,128},{64,192},{128,0},{192,64},{1,129},{65,193},{129,1},{193,65... | collective-permute-start | bytes 491528 | tf_op jit(solution)/shard_map/ppermute | solution.py:382
  119.0 10.0 %collective-permute-start.6 = (bf16[128,640]{1,0:T(8,128)(2,1)S(1)}, bf16[128,640]{1,0:T(8,128)(2,1)S(1)}, u32[]{:S(2)}, u32[]{:S(2)}) collective-permute-start(bf16[128,640]{1,0:T(8,128)(2,1)S(1)} %get-tuple-element.24), channel_id=1, source_target_pairs={{0,64},{64,128},{128,192},{192,0},{1,65},{65,129},{129,193},{193,1... | collective-permute-start | bytes 491528 | tf_op jit(solution)/shard_map/ppermute | solution.py:382

commit v7 on v6

--- a/solution.py
+++ b/solution.py
@@ -353,7 +353,7 @@
         letters(own_list, coarse_keys, coarse_values), "seq", 0, 0, axis_index_groups=ALONG_Z, tiled=True
     )
     wanted = jnp.transpose(came[:, PACK, : X * C])[:, None, :].astype(jnp.int32)
-    column, wanted, other_q = lax.optimization_barrier((came, wanted, other_q))
+    column, wanted = lax.optimization_barrier((came, wanted))
     wanted = lax.all_to_all(wanted, "seq", 0, 0, axis_index_groups=IN_PLANE, tiled=True)
     coarse = [column] + [shifted(column, k, 0) for k in range(1, X)]
 

time: 130 us -> 129 us (level)
  local copies, waits for them, and re-layouts: 3.99 us -> 1.95 us
    unnamed x19 -> x15, local copies, waits for them, and re-layouts: 3.23 us -> 1.18 us
where the time goes in v7:
time: 129 us
  waiting for transfers between devices  51.8 us (40%)
  Pallas kernels  38.3 us (30%)
  starting transfers between devices  34.4 us (27%)
  local copies, waits for them, and re-layouts  1.95 us (2%)
  other arithmetic  1.82 us (1%)
    pallas_call x2, Pallas kernels, coarse_half(): pl.pallas_call(coarse_kernel, grid_spec=pltpu.PrefetchScalarGridSpec(num_...  24.8 us
    all_to_all x1, waiting for transfers between devices, shards(): incoming = lax.all_to_all(payload(wanted, blocks), 'seq', 0, 0, tiled=True)  24 us
    all_to_all x1, waiting for transfers between devices, shards(): lax.all_to_all(letters(own_list, coarse_keys, coarse_values), 'seq', 0, 0...  10.9 us
    ppermute x6, starting transfers between devices, shifted(): lax.ppermute(x, 'seq', [(index(*s), index(s[0], s[1] + dx, s[2] + dc)) fo...  9.46 us
    ppermute x3, waiting for transfers between devices, shards(): own = own + lax.ppermute(part, 'grp', perm).astype(jnp.float32)  9.28 us
    all_to_all x1, starting transfers between devices, shards(): lax.all_to_all(letters(own_list, coarse_keys, coarse_values), 'seq', 0, 0...  9.15 us
    pallas_call x1, Pallas kernels, tail(): pl.pallas_call(functools.partial(tail_kernel, n_grp), grid_spec=pltpu.Pre...  8.43 us
    ppermute x6, waiting for transfers between devices, shifted(): lax.ppermute(x, 'seq', [(index(*s), index(s[0], s[1] + dx, s[2] + dc)) fo...  7.67 us
  transfers between devices with their start and end apart: 12, of which 7 were waited for; matrix products, arithmetic and copies ran while one was open for 2% of the time, Pallas kernels for 21%

profile of v7, /device:TPU:1, one launch (start us, length us, event | category | flops | bytes accessed | tf_op | source)
XLA Modules:
  0.0 128.8 jit_solution(16705628943617904448)
XLA Ops:
  0.0 2.4 %letters.1 = bf16[8,168,128]{2,1,0:T(8,128)(2,1)} custom-call(s32[16]{0:T(128)} %bitcast.28, bf16[1,64,192]{2,1,0:T(8,128)(2,1)} %keys_ref.1, bf16[1,64,128]{2,1,0:T(8,128)(2,1)} %values_ref.1), custom_call_target="tpu_custom_call" | custom-call | bytes 344064 | tf_op jit(solution)/shard_map/letters/pallas_call | solution.py:67
  2.4 9.1 %all-to-all-start = ((bf16[8,168,128]{2,1,0:T(8,128)(2,1)}), bf16[8,168,128]{2,1,0:T(8,128)(2,1)}, u32[]{:S(2)}, u32[]{:S(2)}) async-start(bf16[8,168,128]{2,1,0:T(8,128)(2,1)} %letters.1), calls=%async_computation | async-start | bytes 688128 | tf_op jit(solution)/shard_map/all_to_all | solution.py:352
  11.5 1.0 collective-permute-start.3
  12.5 0.2 copy.12
  13.0 0.1 maximum_maximum_fusion.blocks_ref
  13.1 10.9 %all-to-all-done.rest_0_ = bf16[8,168,128]{2,1,0:T(8,128)(2,1)} async-done(((bf16[8,168,128]{2,1,0:T(8,128)(2,1)}), bf16[8,168,128]{2,1,0:T(8,128)(2,1)}, u32[]{:S(2)}, u32[]{:S(2)}) %all-to-all-start) | async-done | bytes 344096 | tf_op jit(solution)/shard_map/all_to_all | solution.py:352
  24.0 0.7 slice_convert_fusion
  24.7 0.7 copy.10
  25.4 6.5 %all-to-all-start.1 = ((s32[8,1,8]{2,1,0:T(1,128)}), s32[8,1,8]{2,1,0:T(1,128)S(1)}, u32[]{:S(2)}, u32[]{:S(2)}) async-start(s32[8,1,8]{2,1,0:T(1,128)} %bitcast.7), calls=%async_computation.1 | async-start | bytes 8192 | tf_op jit(solution)/shard_map/all_to_all | solution.py:357
  31.9 1.4 %collective-permute-start = (bf16[8,168,128]{2,1,0:T(8,128)(2,1)}, bf16[8,168,128]{2,1,0:T(8,128)(2,1)}, u32[]{:S(2)}, u32[]{:S(2)}) collective-permute-start(bf16[8,168,128]{2,1,0:T(8,128)(2,1)} %all-to-all-done.rest_0_), channel_id=1, source_target_pairs={{0,2},{1,3},{2,4},{3,5},{4,6},{5,7},{6,0},{7,1},{8,10},{9,11},{10,... | collective-permute-start | bytes 1032200 | tf_op jit(solution)/shard_map/ppermute | solution.py:48
  33.3 2.4 %collective-permute-start.1 = (bf16[8,168,128]{2,1,0:T(8,128)(2,1)}, bf16[8,168,128]{2,1,0:T(8,128)(2,1)}, u32[]{:S(2)}, u32[]{:S(2)}) collective-permute-start(bf16[8,168,128]{2,1,0:T(8,128)(2,1)} %all-to-all-done.rest_0_), channel_id=1, source_target_pairs={{0,4},{1,5},{2,6},{3,7},{4,0},{5,1},{6,2},{7,3},{8,12},{9,13},{10,... | collective-permute-start | bytes 1032200 | tf_op jit(solution)/shard_map/ppermute | solution.py:48
  35.7 1.2 collective-permute-start.2
  36.9 2.6 %payload.1 = bf16[64,160,128]{2,1,0:T(8,128)(2,1)} custom-call(s32[8,1,8]{2,1,0:T(1,128)S(1)} %all-to-all-done.1.wanted_ref, bf16[16,160,128]{2,1,0:T(8,128)(2,1)S(1)} %maximum_maximum_fusion.blocks_ref), custom_call_target="tpu_custom_call" | custom-call | bytes 5242880 | tf_op jit(solution)/shard_map/payload/pallas_call | solution.py:91
  39.5 5.5 %all-to-all-start.2 = ((bf16[64,160,128]{2,1,0:T(8,128)(2,1)}), bf16[64,160,128]{2,1,0:T(8,128)(2,1)S(1)}, u32[]{:S(2)}, u32[]{:S(2)}) async-start(bf16[64,160,128]{2,1,0:T(8,128)(2,1)} %payload.1), calls=%async_computation.2 | async-start | bytes 5242880 | tf_op jit(solution)/shard_map/all_to_all | solution.py:363
  45.0 0.1 pad_add_fusion.info_ref
  45.1 0.3 fusion.2
  45.4 6.1 %collective-permute-done.1.rest_2_ = bf16[8,168,128]{2,1,0:T(8,128)(2,1)} collective-permute-done((bf16[8,168,128]{2,1,0:T(8,128)(2,1)}, bf16[8,168,128]{2,1,0:T(8,128)(2,1)}, u32[]{:S(2)}, u32[]{:S(2)}) %collective-permute-start.1) | collective-permute-done | bytes 344096 | tf_op jit(solution)/shard_map/ppermute | solution.py:48
  51.5 1.6 %collective-permute-done.2.rest_3_ = bf16[8,168,128]{2,1,0:T(8,128)(2,1)} collective-permute-done((bf16[8,168,128]{2,1,0:T(8,128)(2,1)}, bf16[8,168,128]{2,1,0:T(8,128)(2,1)}, u32[]{:S(2)}, u32[]{:S(2)}) %collective-permute-start.2) | collective-permute-done | bytes 344096 | tf_op jit(solution)/shard_map/ppermute | solution.py:48
  53.1 12.5 %coarse.3 = (bf16[16,128,128]{2,1,0:T(8,128)(2,1)S(1)}, f32[16,1,128]{2,1,0:T(1,128)S(1)}) custom-call(s32[3]{0:T(128)S(1)} %add_add_fusion.1.info_ref, bf16[8,168,128]{2,1,0:T(8,128)(2,1)} %all-to-all-done.rest_0_, bf16[8,168,128]{2,1,0:T(8,128)(2,1)} %collective-permute-done.rest_1_, bf16[8,168,128]{2,1,0:T(8,128)(2,1)} %collective-permute-done.1.rest_2_, ...), custom_call_target="tpu_custom_call" | custom-call | flops 25823150080 | bytes 3145728 | tf_op jit(solution)/shard_map/coarse/pallas_call | solution.py:161
  65.6 3.3 %collective-permute-start.4 = (f32[16,1,128]{2,1,0:T(1,128)S(1)}, f32[16,1,128]{2,1,0:T(1,128)S(1)}, u32[]{:S(2)}, u32[]{:S(2)}) collective-permute-start(f32[16,1,128]{2,1,0:T(1,128)S(1)} %get-tuple-element.18), channel_id=1, source_target_pairs={{0,1},{1,0},{2,3},{3,2},{4,5},{5,4},{6,7},{7,6},{8,9},{9,8},{10,11... | collective-permute-start | bytes 24584 | tf_op jit(solution)/shard_map/ppermute | solution.py:48
  68.9 0.3 collective-permute-start.5
  69.1 12.4 %coarse.2 = (f32[16,128,128]{2,1,0:T(8,128)S(1)}, f32[16,1,128]{2,1,0:T(1,128)S(1)}) custom-call(s32[3]{0:T(128)S(1)} %add_add_fusion.info_ref, bf16[8,168,128]{2,1,0:T(8,128)(2,1)} %all-to-all-done.rest_0_, bf16[8,168,128]{2,1,0:T(8,128)(2,1)} %collective-permute-done.rest_1_, bf16[8,168,128]{2,1,0:T(8,128)(2,1)} %collective-permute-done.1.rest_2_, ...), custom_call_target="tpu_custom_call" | custom-call | flops 25823150080 | bytes 3145728 | tf_op jit(solution)/shard_map/coarse/pallas_call | solution.py:161
  81.5 1.0 copy-done.1
  82.5 24.0 %all-to-all-done.2.incoming = bf16[64,160,128]{2,1,0:T(8,128)(2,1)S(1)} async-done(((bf16[64,160,128]{2,1,0:T(8,128)(2,1)}), bf16[64,160,128]{2,1,0:T(8,128)(2,1)S(1)}, u32[]{:S(2)}, u32[]{:S(2)}) %all-to-all-start.2) | async-done | bytes 2621472 | tf_op jit(solution)/shard_map/all_to_all | solution.py:363
  106.5 8.4 %tail.1 = (f32[128,640]{1,0:T(8,128)S(1)}, bf16[128,640]{1,0:T(8,128)(2,1)S(1)}, bf16[128,640]{1,0:T(8,128)(2,1)S(1)}, bf16[128,640]{1,0:T(8,128)(2,1)S(1)}) custom-call(s32[19]{0:T(128)S(1)} %pad_add_fusion.info_ref, bf16[64,160,128]{2,1,0:T(8,128)(2,1)S(1)} %all-to-all-done.2.incoming, bf16[16,192,128]{2,1,0:T(8,128)(2,1)} %bitcast.21, ...), custom_call_target="tpu_custom_call" | custom-call | flops 2684354560 | bytes 10485760 | tf_op jit(solution)/shard_map/tail/pallas_call | solution.py:278
  114.9 2.8 %collective-permute-start.8 = (bf16[128,640]{1,0:T(8,128)(2,1)S(1)}, bf16[128,640]{1,0:T(8,128)(2,1)S(1)}, u32[]{:S(2)}, u32[]{:S(2)}) collective-permute-start(bf16[128,640]{1,0:T(8,128)(2,1)S(1)} %get-tuple-element.24), channel_id=1, source_target_pairs={{0,192},{64,0},{128,64},{192,128},{1,193},{65,1},{129,65},{193,129... | collective-permute-start | bytes 491528 | tf_op jit(solution)/shard_map/ppermute | solution.py:382
  117.7 0.3 collective-permute-start.7
  118.1 0.7 collective-permute-start.6
  118.8 2.2 %collective-permute-done.8 = bf16[128,640]{1,0:T(8,128)(2,1)S(1)} collective-permute-done((bf16[128,640]{1,0:T(8,128)(2,1)S(1)}, bf16[128,640]{1,0:T(8,128)(2,1)S(1)}, u32[]{:S(2)}, u32[]{:S(2)}) %collective-permute-start.8) | collective-permute-done | bytes 163872 | tf_op jit(solution)/shard_map/ppermute | solution.py:382
  121.0 2.5 %collective-permute-done.7 = bf16[128,640]{1,0:T(8,128)(2,1)S(1)} collective-permute-done((bf16[128,640]{1,0:T(8,128)(2,1)S(1)}, bf16[128,640]{1,0:T(8,128)(2,1)S(1)}, u32[]{:S(2)}, u32[]{:S(2)}) %collective-permute-start.7) | collective-permute-done | bytes 163872 | tf_op jit(solution)/shard_map/ppermute | solution.py:382
  123.5 4.5 %collective-permute-done.6 = bf16[128,640]{1,0:T(8,128)(2,1)S(1)} collective-permute-done((bf16[128,640]{1,0:T(8,128)(2,1)S(1)}, bf16[128,640]{1,0:T(8,128)(2,1)S(1)}, u32[]{:S(2)}, u32[]{:S(2)}) %collective-permute-start.6) | collective-permute-done | bytes 163872 | tf_op jit(solution)/shard_map/ppermute | solution.py:382
  128.0 0.8 add_convert_fusion
  (22 shorter events, 0.3 us)
Async XLA Ops:
  0.0 45.1 %copy-start = (bf16[128,2560]{1,0:T(8,128)(2,1)S(1)}, bf16[128,2560]{1,0:T(8,128)(2,1)}, u32[]{:S(2)}) copy-start(bf16[128,2560]{1,0:T(8,128)(2,1)} %param.14) | copy-start | bytes 1966084
  0.0 12.5 %copy-start.3 = (bf16[1,1024,192]{1,2,0:T(8,128)(2,1)S(1)}, bf16[1,1024,192]{1,2,0:T(8,128)(2,1)}, u32[]{:S(2)}) copy-start(bf16[1,1024,192]{1,2,0:T(8,128)(2,1)} %param.10) | copy-start | bytes 1179652
  2.4 10.6 %copy-start.4 = (bf16[1,1024,128]{2,1,0:T(8,128)(2,1)S(1)}, bf16[1,1024,128]{2,1,0:T(8,128)(2,1)}, u32[]{:S(2)}) copy-start(bf16[1,1024,128]{2,1,0:T(8,128)(2,1)} %param.11) | copy-start | bytes 786436
  2.4 21.6 %all-to-all-start = ((bf16[8,168,128]{2,1,0:T(8,128)(2,1)}), bf16[8,168,128]{2,1,0:T(8,128)(2,1)}, u32[]{:S(2)}, u32[]{:S(2)}) async-start(bf16[8,168,128]{2,1,0:T(8,128)(2,1)} %letters.1), calls=%async_computation | async-start | bytes 688128 | tf_op jit(solution)/shard_map/all_to_all | solution.py:352
  11.5 33.9 %collective-permute-start.3 = (bf16[16,192,128]{2,1,0:T(8,128)(2,1)}, bf16[16,192,128]{2,1,0:T(8,128)(2,1)}, u32[]{:S(2)}, u32[]{:S(2)}) collective-permute-start(bf16[16,192,128]{2,1,0:T(8,128)(2,1)} %bitcast.20), channel_id=1, source_target_pairs={{0,1},{1,0},{2,3},{3,2},{4,5},{5,4},{6,7},{7,6},{8,9},{9,8},{10,11... | collective-permute-start | bytes 2359304 | tf_op jit(solution)/shard_map/ppermute | solution.py:48
  25.4 11.5 %all-to-all-start.1 = ((s32[8,1,8]{2,1,0:T(1,128)}), s32[8,1,8]{2,1,0:T(1,128)S(1)}, u32[]{:S(2)}, u32[]{:S(2)}) async-start(s32[8,1,8]{2,1,0:T(1,128)} %bitcast.7), calls=%async_computation.1 | async-start | bytes 8192 | tf_op jit(solution)/shard_map/all_to_all | solution.py:357
  31.9 13.5 %collective-permute-start = (bf16[8,168,128]{2,1,0:T(8,128)(2,1)}, bf16[8,168,128]{2,1,0:T(8,128)(2,1)}, u32[]{:S(2)}, u32[]{:S(2)}) collective-permute-start(bf16[8,168,128]{2,1,0:T(8,128)(2,1)} %all-to-all-done.rest_0_), channel_id=1, source_target_pairs={{0,2},{1,3},{2,4},{3,5},{4,6},{5,7},{6,0},{7,1},{8,10},{9,11},{10,... | collective-permute-start | bytes 1032200 | tf_op jit(solution)/shard_map/ppermute | solution.py:48
  33.3 18.2 %collective-permute-start.1 = (bf16[8,168,128]{2,1,0:T(8,128)(2,1)}, bf16[8,168,128]{2,1,0:T(8,128)(2,1)}, u32[]{:S(2)}, u32[]{:S(2)}) collective-permute-start(bf16[8,168,128]{2,1,0:T(8,128)(2,1)} %all-to-all-done.rest_0_), channel_id=1, source_target_pairs={{0,4},{1,5},{2,6},{3,7},{4,0},{5,1},{6,2},{7,3},{8,12},{9,13},{10,... | collective-permute-start | bytes 1032200 | tf_op jit(solution)/shard_map/ppermute | solution.py:48
  35.7 17.4 %collective-permute-start.2 = (bf16[8,168,128]{2,1,0:T(8,128)(2,1)}, bf16[8,168,128]{2,1,0:T(8,128)(2,1)}, u32[]{:S(2)}, u32[]{:S(2)}) collective-permute-start(bf16[8,168,128]{2,1,0:T(8,128)(2,1)} %all-to-all-done.rest_0_), channel_id=1, source_target_pairs={{0,6},{1,7},{2,0},{3,1},{4,2},{5,3},{6,4},{7,5},{8,14},{9,15},{10,... | collective-permute-start | bytes 1032200 | tf_op jit(solution)/shard_map/ppermute | solution.py:48
  39.5 5.5 %copy-start.6 = (s32[1,1,16]{2,1,0:T(1,128)S(1)}, s32[1,1,16]{2,1,0:T(1,128)}, u32[]{:S(2)}) copy-start(s32[1,1,16]{2,1,0:T(1,128)} %param.17) | copy-start | bytes 196
  39.5 5.6 %copy-start.5 = (bf16[1,2560,32]{1,2,0:T(8,128)(2,1)S(1)}, bf16[1,2560,32]{1,2,0:T(8,128)(2,1)}, u32[]{:S(2)}) copy-start(bf16[1,2560,32]{1,2,0:T(8,128)(2,1)} %param.15) | copy-start | bytes 491524
  39.5 67.0 %all-to-all-start.2 = ((bf16[64,160,128]{2,1,0:T(8,128)(2,1)}), bf16[64,160,128]{2,1,0:T(8,128)(2,1)S(1)}, u32[]{:S(2)}, u32[]{:S(2)}) async-start(bf16[64,160,128]{2,1,0:T(8,128)(2,1)} %payload.1), calls=%async_computation.2 | async-start | bytes 5242880 | tf_op jit(solution)/shard_map/all_to_all | solution.py:363
  45.4 23.7 %copy-start.2 = (bf16[128,16,192]{0,2,1:T(8,128)(2,1)S(1)}, bf16[128,16,192]{0,2,1:T(8,128)(2,1)}, u32[]{:S(2)}) copy-start(bf16[128,16,192]{0,2,1:T(8,128)(2,1)} %param.9) | copy-start | bytes 2359300
  65.6 16.9 %collective-permute-start.4 = (f32[16,1,128]{2,1,0:T(1,128)S(1)}, f32[16,1,128]{2,1,0:T(1,128)S(1)}, u32[]{:S(2)}, u32[]{:S(2)}) collective-permute-start(f32[16,1,128]{2,1,0:T(1,128)S(1)} %get-tuple-element.18), channel_id=1, source_target_pairs={{0,1},{1,0},{2,3},{3,2},{4,5},{5,4},{6,7},{7,6},{8,9},{9,8},{10,11... | collective-permute-start | bytes 24584 | tf_op jit(solution)/shard_map/ppermute | solution.py:48
  68.9 13.6 %collective-permute-start.5 = (bf16[16,128,128]{2,1,0:T(8,128)(2,1)S(1)}, bf16[16,128,128]{2,1,0:T(8,128)(2,1)}, u32[]{:S(2)}, u32[]{:S(2)}) collective-permute-start(bf16[16,128,128]{2,1,0:T(8,128)(2,1)S(1)} %get-tuple-element.20), channel_id=1, source_target_pairs={{0,1},{1,0},{2,3},{3,2},{4,5},{5,4},{6,7},{7,6},{8,9},{9,8},{10,11... | collective-permute-start | bytes 1572872 | tf_op jit(solution)/shard_map/ppermute | solution.py:48
  81.5 1.0 copy-start.1
  114.9 6.1 %collective-permute-start.8 = (bf16[128,640]{1,0:T(8,128)(2,1)S(1)}, bf16[128,640]{1,0:T(8,128)(2,1)S(1)}, u32[]{:S(2)}, u32[]{:S(2)}) collective-permute-start(bf16[128,640]{1,0:T(8,128)(2,1)S(1)} %get-tuple-element.24), channel_id=1, source_target_pairs={{0,192},{64,0},{128,64},{192,128},{1,193},{65,1},{129,65},{193,129... | collective-permute-start | bytes 491528 | tf_op jit(solution)/shard_map/ppermute | solution.py:382
  117.7 5.8 %collective-permute-start.7 = (bf16[128,640]{1,0:T(8,128)(2,1)S(1)}, bf16[128,640]{1,0:T(8,128)(2,1)S(1)}, u32[]{:S(2)}, u32[]{:S(2)}) collective-permute-start(bf16[128,640]{1,0:T(8,128)(2,1)S(1)} %get-tuple-element.23), channel_id=1, source_target_pairs={{0,128},{64,192},{128,0},{192,64},{1,129},{65,193},{129,1},{193,65... | collective-permute-start | bytes 491528 | tf_op jit(solution)/shard_map/ppermute | solution.py:382
  118.1 10.0 %collective-permute-start.6 = (bf16[128,640]{1,0:T(8,128)(2,1)S(1)}, bf16[128,640]{1,0:T(8,128)(2,1)S(1)}, u32[]{:S(2)}, u32[]{:S(2)}) collective-permute-start(bf16[128,640]{1,0:T(8,128)(2,1)S(1)} %get-tuple-element.22), channel_id=1, source_target_pairs={{0,64},{64,128},{128,192},{192,0},{1,65},{65,129},{129,193},{193,1... | collective-permute-start | bytes 491528 | tf_op jit(solution)/shard_map/ppermute | solution.py:382

commit v8 on v7

--- a/solution.py
+++ b/solution.py
@@ -66,12 +66,12 @@
 def letters(own_list, keys, values):
     return pl.pallas_call(
         letter_kernel,
-        grid_spec=pltpu.PrefetchScalarGridSpec(
-            num_scalar_prefetch=1,
-            grid=(1,),
-            in_specs=[pl.BlockSpec(a.shape, lambda i, s: (0, 0, 0)) for a in (keys, values)],
-            out_specs=pl.BlockSpec((Z, LETTER, DV), lambda i, s: (0, 0, 0)),
-        ),
+        in_specs=[
+            pl.BlockSpec(memory_space=pltpu.SMEM),
+            pl.BlockSpec(memory_space=pltpu.VMEM),
+            pl.BlockSpec(memory_space=pltpu.VMEM),
+        ],
+        out_specs=pl.BlockSpec(memory_space=pltpu.VMEM),
         out_shape=jax.ShapeDtypeStruct((Z, LETTER, DV), keys.dtype),
         cost_estimate=pl.CostEstimate(flops=0, bytes_accessed=Z * LETTER * DV * 2, transcendentals=0),
         name="letters",
@@ -352,7 +352,13 @@
     came = lax.all_to_all(
         letters(own_list, coarse_keys, coarse_values), "seq", 0, 0, axis_index_groups=ALONG_Z, tiled=True
     )
-    wanted = jnp.transpose(came[:, PACK, : X * C])[:, None, :].astype(jnp.int32)
+    wanted = lax.dot_general(
+        jnp.eye(X * C, DV, dtype=came.dtype),
+        came[:, PACK],
+        (((1,), (1,)), ((), ())),
+        preferred_element_type=jnp.float32,
+    )
+    wanted = wanted.astype(jnp.int32)[:, None, :]
     column, wanted = lax.optimization_barrier((came, wanted))
     wanted = lax.all_to_all(wanted, "seq", 0, 0, axis_index_groups=IN_PLANE, tiled=True)
     coarse = [column] + [shifted(column, k, 0) for k in range(1, X)]

time: 129 us -> 129 us (level)
  no operation moved by 1% of the time
where the time goes in v8:
time: 129 us; the launch traced here: 128 us
  waiting for transfers between devices  51.8 us (40%)
  Pallas kernels  37.6 us (29%)
  starting transfers between devices  34.4 us (27%)
  local copies, waits for them, and re-layouts  2 us (2%)
    pallas_call x2, Pallas kernels, coarse_half(): pl.pallas_call(coarse_kernel, grid_spec=pltpu.PrefetchScalarGridSpec(num_...  24.8 us
    all_to_all x1, waiting for transfers between devices, shards(): incoming = lax.all_to_all(payload(wanted, blocks), 'seq', 0, 0, tiled=True)  24 us
    all_to_all x1, waiting for transfers between devices, shards(): lax.all_to_all(letters(own_list, coarse_keys, coarse_values), 'seq', 0, 0...  10.9 us
    ppermute x6, starting transfers between devices, shifted(): lax.ppermute(x, 'seq', [(index(*s), index(s[0], s[1] + dx, s[2] + dc)) fo...  9.46 us
    ppermute x3, waiting for transfers between devices, shards(): own = own + lax.ppermute(part, 'grp', perm).astype(jnp.float32)  9.26 us
    all_to_all x1, starting transfers between devices, shards(): lax.all_to_all(letters(own_list, coarse_keys, coarse_values), 'seq', 0, 0...  9.15 us
    pallas_call x1, Pallas kernels, tail(): pl.pallas_call(functools.partial(tail_kernel, n_grp), grid_spec=pltpu.Pre...  8.43 us
    ppermute x6, waiting for transfers between devices, shifted(): lax.ppermute(x, 'seq', [(index(*s), index(s[0], s[1] + dx, s[2] + dc)) fo...  7.67 us
  transfers between devices with their start and end apart: 12, of which 7 were waited for; matrix products, arithmetic and copies ran while one was open for 2% of the time, Pallas kernels for 21%

profile of v8, /device:TPU:1, one launch (start us, length us, event | category | flops | bytes accessed | tf_op | source)
XLA Modules:
  0.0 128.1 jit_solution(2315499421928552727)
XLA Ops:
  0.0 1.7 %letters.1 = bf16[8,168,128]{2,1,0:T(8,128)(2,1)} custom-call(s32[16]{0:T(128)} %bitcast.28, bf16[1,64,192]{2,1,0:T(8,128)(2,1)} %keys_ref.1, bf16[1,64,128]{2,1,0:T(8,128)(2,1)} %values_ref.1), custom_call_target="tpu_custom_call" | custom-call | bytes 344064 | tf_op jit(solution)/shard_map/letters/pallas_call | solution.py:67
  1.7 9.1 %all-to-all-start = ((bf16[8,168,128]{2,1,0:T(8,128)(2,1)}), bf16[8,168,128]{2,1,0:T(8,128)(2,1)}, u32[]{:S(2)}, u32[]{:S(2)}) async-start(bf16[8,168,128]{2,1,0:T(8,128)(2,1)} %letters.1), calls=%async_computation | async-start | bytes 688128 | tf_op jit(solution)/shard_map/all_to_all | solution.py:352
  10.8 1.0 collective-permute-start.3
  11.8 0.2 copy.13
  12.3 0.1 maximum_maximum_fusion.blocks_ref
  12.4 10.9 %all-to-all-done.rest_0_ = bf16[8,168,128]{2,1,0:T(8,128)(2,1)} async-done(((bf16[8,168,128]{2,1,0:T(8,128)(2,1)}), bf16[8,168,128]{2,1,0:T(8,128)(2,1)}, u32[]{:S(2)}, u32[]{:S(2)}) %all-to-all-start) | async-done | bytes 344096 | tf_op jit(solution)/shard_map/all_to_all | solution.py:352
  23.3 0.7 slice.16
  24.0 0.7 fusion.3
  24.7 6.5 %all-to-all-start.1 = ((s32[8,1,8]{2,1,0:T(1,128)}), s32[8,1,8]{2,1,0:T(1,128)S(1)}, u32[]{:S(2)}, u32[]{:S(2)}) async-start(s32[8,1,8]{2,1,0:T(1,128)} %bitcast.5), calls=%async_computation.1 | async-start | bytes 8192 | tf_op jit(solution)/shard_map/all_to_all | solution.py:363
  31.2 1.4 %collective-permute-start = (bf16[8,168,128]{2,1,0:T(8,128)(2,1)}, bf16[8,168,128]{2,1,0:T(8,128)(2,1)}, u32[]{:S(2)}, u32[]{:S(2)}) collective-permute-start(bf16[8,168,128]{2,1,0:T(8,128)(2,1)} %all-to-all-done.rest_0_), channel_id=1, source_target_pairs={{0,2},{1,3},{2,4},{3,5},{4,6},{5,7},{6,0},{7,1},{8,10},{9,11},{10,... | collective-permute-start | bytes 1032200 | tf_op jit(solution)/shard_map/ppermute | solution.py:48
  32.6 2.4 %collective-permute-start.1 = (bf16[8,168,128]{2,1,0:T(8,128)(2,1)}, bf16[8,168,128]{2,1,0:T(8,128)(2,1)}, u32[]{:S(2)}, u32[]{:S(2)}) collective-permute-start(bf16[8,168,128]{2,1,0:T(8,128)(2,1)} %all-to-all-done.rest_0_), channel_id=1, source_target_pairs={{0,4},{1,5},{2,6},{3,7},{4,0},{5,1},{6,2},{7,3},{8,12},{9,13},{10,... | collective-permute-start | bytes 1032200 | tf_op jit(solution)/shard_map/ppermute | solution.py:48
  35.0 1.2 collective-permute-start.2
  36.2 2.6 %payload.1 = bf16[64,160,128]{2,1,0:T(8,128)(2,1)} custom-call(s32[8,1,8]{2,1,0:T(1,128)S(1)} %all-to-all-done.1.wanted_ref, bf16[16,160,128]{2,1,0:T(8,128)(2,1)S(1)} %maximum_maximum_fusion.blocks_ref), custom_call_target="tpu_custom_call" | custom-call | bytes 5242880 | tf_op jit(solution)/shard_map/payload/pallas_call | solution.py:91
  38.8 5.5 %all-to-all-start.2 = ((bf16[64,160,128]{2,1,0:T(8,128)(2,1)}), bf16[64,160,128]{2,1,0:T(8,128)(2,1)S(1)}, u32[]{:S(2)}, u32[]{:S(2)}) async-start(bf16[64,160,128]{2,1,0:T(8,128)(2,1)} %payload.1), calls=%async_computation.2 | async-start | bytes 5242880 | tf_op jit(solution)/shard_map/all_to_all | solution.py:369
  44.3 0.1 pad_add_fusion.info_ref
  44.4 0.3 fusion.2
  44.8 6.1 %collective-permute-done.1.rest_2_ = bf16[8,168,128]{2,1,0:T(8,128)(2,1)} collective-permute-done((bf16[8,168,128]{2,1,0:T(8,128)(2,1)}, bf16[8,168,128]{2,1,0:T(8,128)(2,1)}, u32[]{:S(2)}, u32[]{:S(2)}) %collective-permute-start.1) | collective-permute-done | bytes 344096 | tf_op jit(solution)/shard_map/ppermute | solution.py:48
  50.9 1.6 %collective-permute-done.2.rest_3_ = bf16[8,168,128]{2,1,0:T(8,128)(2,1)} collective-permute-done((bf16[8,168,128]{2,1,0:T(8,128)(2,1)}, bf16[8,168,128]{2,1,0:T(8,128)(2,1)}, u32[]{:S(2)}, u32[]{:S(2)}) %collective-permute-start.2) | collective-permute-done | bytes 344096 | tf_op jit(solution)/shard_map/ppermute | solution.py:48
  52.5 12.5 %coarse.3 = (bf16[16,128,128]{2,1,0:T(8,128)(2,1)S(1)}, f32[16,1,128]{2,1,0:T(1,128)S(1)}) custom-call(s32[3]{0:T(128)S(1)} %add_add_fusion.1.info_ref, bf16[8,168,128]{2,1,0:T(8,128)(2,1)} %all-to-all-done.rest_0_, bf16[8,168,128]{2,1,0:T(8,128)(2,1)} %collective-permute-done.rest_1_, bf16[8,168,128]{2,1,0:T(8,128)(2,1)} %collective-permute-done.1.rest_2_, ...), custom_call_target="tpu_custom_call" | custom-call | flops 25823150080 | bytes 3145728 | tf_op jit(solution)/shard_map/coarse/pallas_call | solution.py:161
  65.0 3.3 %collective-permute-start.4 = (f32[16,1,128]{2,1,0:T(1,128)S(1)}, f32[16,1,128]{2,1,0:T(1,128)S(1)}, u32[]{:S(2)}, u32[]{:S(2)}) collective-permute-start(f32[16,1,128]{2,1,0:T(1,128)S(1)} %get-tuple-element.18), channel_id=1, source_target_pairs={{0,1},{1,0},{2,3},{3,2},{4,5},{5,4},{6,7},{7,6},{8,9},{9,8},{10,11... | collective-permute-start | bytes 24584 | tf_op jit(solution)/shard_map/ppermute | solution.py:48
  68.2 0.3 collective-permute-start.5
  68.5 12.4 %coarse.2 = (f32[16,128,128]{2,1,0:T(8,128)S(1)}, f32[16,1,128]{2,1,0:T(1,128)S(1)}) custom-call(s32[3]{0:T(128)S(1)} %add_add_fusion.info_ref, bf16[8,168,128]{2,1,0:T(8,128)(2,1)} %all-to-all-done.rest_0_, bf16[8,168,128]{2,1,0:T(8,128)(2,1)} %collective-permute-done.rest_1_, bf16[8,168,128]{2,1,0:T(8,128)(2,1)} %collective-permute-done.1.rest_2_, ...), custom_call_target="tpu_custom_call" | custom-call | flops 25823150080 | bytes 3145728 | tf_op jit(solution)/shard_map/coarse/pallas_call | solution.py:161
  80.9 1.0 copy-done.1
  81.8 24.0 %all-to-all-done.2.incoming = bf16[64,160,128]{2,1,0:T(8,128)(2,1)S(1)} async-done(((bf16[64,160,128]{2,1,0:T(8,128)(2,1)}), bf16[64,160,128]{2,1,0:T(8,128)(2,1)S(1)}, u32[]{:S(2)}, u32[]{:S(2)}) %all-to-all-start.2) | async-done | bytes 2621472 | tf_op jit(solution)/shard_map/all_to_all | solution.py:369
  105.8 8.4 %tail.1 = (f32[128,640]{1,0:T(8,128)S(1)}, bf16[128,640]{1,0:T(8,128)(2,1)S(1)}, bf16[128,640]{1,0:T(8,128)(2,1)S(1)}, bf16[128,640]{1,0:T(8,128)(2,1)S(1)}) custom-call(s32[19]{0:T(128)S(1)} %pad_add_fusion.info_ref, bf16[64,160,128]{2,1,0:T(8,128)(2,1)S(1)} %all-to-all-done.2.incoming, bf16[16,192,128]{2,1,0:T(8,128)(2,1)} %bitcast.22, ...), custom_call_target="tpu_custom_call" | custom-call | flops 2684354560 | bytes 10485760 | tf_op jit(solution)/shard_map/tail/pallas_call | solution.py:278
  114.3 2.8 %collective-permute-start.8 = (bf16[128,640]{1,0:T(8,128)(2,1)S(1)}, bf16[128,640]{1,0:T(8,128)(2,1)S(1)}, u32[]{:S(2)}, u32[]{:S(2)}) collective-permute-start(bf16[128,640]{1,0:T(8,128)(2,1)S(1)} %get-tuple-element.24), channel_id=1, source_target_pairs={{0,192},{64,0},{128,64},{192,128},{1,193},{65,1},{129,65},{193,129... | collective-permute-start | bytes 491528 | tf_op jit(solution)/shard_map/ppermute | solution.py:388
  117.1 0.3 collective-permute-start.7
  117.4 0.7 collective-permute-start.6
  118.1 2.2 %collective-permute-done.8 = bf16[128,640]{1,0:T(8,128)(2,1)S(1)} collective-permute-done((bf16[128,640]{1,0:T(8,128)(2,1)S(1)}, bf16[128,640]{1,0:T(8,128)(2,1)S(1)}, u32[]{:S(2)}, u32[]{:S(2)}) %collective-permute-start.8) | collective-permute-done | bytes 163872 | tf_op jit(solution)/shard_map/ppermute | solution.py:388
  120.3 2.5 %collective-permute-done.7 = bf16[128,640]{1,0:T(8,128)(2,1)S(1)} collective-permute-done((bf16[128,640]{1,0:T(8,128)(2,1)S(1)}, bf16[128,640]{1,0:T(8,128)(2,1)S(1)}, u32[]{:S(2)}, u32[]{:S(2)}) %collective-permute-start.7) | collective-permute-done | bytes 163872 | tf_op jit(solution)/shard_map/ppermute | solution.py:388
  122.9 4.5 %collective-permute-done.6 = bf16[128,640]{1,0:T(8,128)(2,1)S(1)} collective-permute-done((bf16[128,640]{1,0:T(8,128)(2,1)S(1)}, bf16[128,640]{1,0:T(8,128)(2,1)S(1)}, u32[]{:S(2)}, u32[]{:S(2)}) %collective-permute-start.6) | collective-permute-done | bytes 163872 | tf_op jit(solution)/shard_map/ppermute | solution.py:388
  127.4 0.8 add_convert_fusion
  (22 shorter events, 0.3 us)
Async XLA Ops:
  0.0 44.4 %copy-start = (bf16[128,2560]{1,0:T(8,128)(2,1)S(1)}, bf16[128,2560]{1,0:T(8,128)(2,1)}, u32[]{:S(2)}) copy-start(bf16[128,2560]{1,0:T(8,128)(2,1)} %param.14) | copy-start | bytes 1966084
  0.0 11.8 %copy-start.3 = (bf16[1,1024,192]{1,2,0:T(8,128)(2,1)S(1)}, bf16[1,1024,192]{1,2,0:T(8,128)(2,1)}, u32[]{:S(2)}) copy-start(bf16[1,1024,192]{1,2,0:T(8,128)(2,1)} %param.10) | copy-start | bytes 1179652
  1.7 10.6 %copy-start.4 = (bf16[1,1024,128]{2,1,0:T(8,128)(2,1)S(1)}, bf16[1,1024,128]{2,1,0:T(8,128)(2,1)}, u32[]{:S(2)}) copy-start(bf16[1,1024,128]{2,1,0:T(8,128)(2,1)} %param.11) | copy-start | bytes 786436
  1.7 21.6 %all-to-all-start = ((bf16[8,168,128]{2,1,0:T(8,128)(2,1)}), bf16[8,168,128]{2,1,0:T(8,128)(2,1)}, u32[]{:S(2)}, u32[]{:S(2)}) async-start(bf16[8,168,128]{2,1,0:T(8,128)(2,1)} %letters.1), calls=%async_computation | async-start | bytes 688128 | tf_op jit(solution)/shard_map/all_to_all | solution.py:352
  10.8 34.0 %collective-permute-start.3 = (bf16[16,192,128]{2,1,0:T(8,128)(2,1)}, bf16[16,192,128]{2,1,0:T(8,128)(2,1)}, u32[]{:S(2)}, u32[]{:S(2)}) collective-permute-start(bf16[16,192,128]{2,1,0:T(8,128)(2,1)} %bitcast.21), channel_id=1, source_target_pairs={{0,1},{1,0},{2,3},{3,2},{4,5},{5,4},{6,7},{7,6},{8,9},{9,8},{10,11... | collective-permute-start | bytes 2359304 | tf_op jit(solution)/shard_map/ppermute | solution.py:48
  24.7 11.5 %all-to-all-start.1 = ((s32[8,1,8]{2,1,0:T(1,128)}), s32[8,1,8]{2,1,0:T(1,128)S(1)}, u32[]{:S(2)}, u32[]{:S(2)}) async-start(s32[8,1,8]{2,1,0:T(1,128)} %bitcast.5), calls=%async_computation.1 | async-start | bytes 8192 | tf_op jit(solution)/shard_map/all_to_all | solution.py:363
  31.2 13.5 %collective-permute-start = (bf16[8,168,128]{2,1,0:T(8,128)(2,1)}, bf16[8,168,128]{2,1,0:T(8,128)(2,1)}, u32[]{:S(2)}, u32[]{:S(2)}) collective-permute-start(bf16[8,168,128]{2,1,0:T(8,128)(2,1)} %all-to-all-done.rest_0_), channel_id=1, source_target_pairs={{0,2},{1,3},{2,4},{3,5},{4,6},{5,7},{6,0},{7,1},{8,10},{9,11},{10,... | collective-permute-start | bytes 1032200 | tf_op jit(solution)/shard_map/ppermute | solution.py:48
  32.6 18.2 %collective-permute-start.1 = (bf16[8,168,128]{2,1,0:T(8,128)(2,1)}, bf16[8,168,128]{2,1,0:T(8,128)(2,1)}, u32[]{:S(2)}, u32[]{:S(2)}) collective-permute-start(bf16[8,168,128]{2,1,0:T(8,128)(2,1)} %all-to-all-done.rest_0_), channel_id=1, source_target_pairs={{0,4},{1,5},{2,6},{3,7},{4,0},{5,1},{6,2},{7,3},{8,12},{9,13},{10,... | collective-permute-start | bytes 1032200 | tf_op jit(solution)/shard_map/ppermute | solution.py:48
  35.0 17.4 %collective-permute-start.2 = (bf16[8,168,128]{2,1,0:T(8,128)(2,1)}, bf16[8,168,128]{2,1,0:T(8,128)(2,1)}, u32[]{:S(2)}, u32[]{:S(2)}) collective-permute-start(bf16[8,168,128]{2,1,0:T(8,128)(2,1)} %all-to-all-done.rest_0_), channel_id=1, source_target_pairs={{0,6},{1,7},{2,0},{3,1},{4,2},{5,3},{6,4},{7,5},{8,14},{9,15},{10,... | collective-permute-start | bytes 1032200 | tf_op jit(solution)/shard_map/ppermute | solution.py:48
  38.8 5.5 %copy-start.6 = (s32[1,1,16]{2,1,0:T(1,128)S(1)}, s32[1,1,16]{2,1,0:T(1,128)}, u32[]{:S(2)}) copy-start(s32[1,1,16]{2,1,0:T(1,128)} %param.17) | copy-start | bytes 196
  38.8 5.6 %copy-start.5 = (bf16[1,2560,32]{1,2,0:T(8,128)(2,1)S(1)}, bf16[1,2560,32]{1,2,0:T(8,128)(2,1)}, u32[]{:S(2)}) copy-start(bf16[1,2560,32]{1,2,0:T(8,128)(2,1)} %param.15) | copy-start | bytes 491524
  38.8 67.0 %all-to-all-start.2 = ((bf16[64,160,128]{2,1,0:T(8,128)(2,1)}), bf16[64,160,128]{2,1,0:T(8,128)(2,1)S(1)}, u32[]{:S(2)}, u32[]{:S(2)}) async-start(bf16[64,160,128]{2,1,0:T(8,128)(2,1)} %payload.1), calls=%async_computation.2 | async-start | bytes 5242880 | tf_op jit(solution)/shard_map/all_to_all | solution.py:369
  44.8 23.7 %copy-start.2 = (bf16[128,16,192]{0,2,1:T(8,128)(2,1)S(1)}, bf16[128,16,192]{0,2,1:T(8,128)(2,1)}, u32[]{:S(2)}) copy-start(bf16[128,16,192]{0,2,1:T(8,128)(2,1)} %param.9) | copy-start | bytes 2359300
  65.0 16.9 %collective-permute-start.4 = (f32[16,1,128]{2,1,0:T(1,128)S(1)}, f32[16,1,128]{2,1,0:T(1,128)S(1)}, u32[]{:S(2)}, u32[]{:S(2)}) collective-permute-start(f32[16,1,128]{2,1,0:T(1,128)S(1)} %get-tuple-element.18), channel_id=1, source_target_pairs={{0,1},{1,0},{2,3},{3,2},{4,5},{5,4},{6,7},{7,6},{8,9},{9,8},{10,11... | collective-permute-start | bytes 24584 | tf_op jit(solution)/shard_map/ppermute | solution.py:48
  68.2 13.6 %collective-permute-start.5 = (bf16[16,128,128]{2,1,0:T(8,128)(2,1)S(1)}, bf16[16,128,128]{2,1,0:T(8,128)(2,1)}, u32[]{:S(2)}, u32[]{:S(2)}) collective-permute-start(bf16[16,128,128]{2,1,0:T(8,128)(2,1)S(1)} %get-tuple-element.20), channel_id=1, source_target_pairs={{0,1},{1,0},{2,3},{3,2},{4,5},{5,4},{6,7},{7,6},{8,9},{9,8},{10,11... | collective-permute-start | bytes 1572872 | tf_op jit(solution)/shard_map/ppermute | solution.py:48
  80.9 1.0 copy-start.1
  114.3 6.1 %collective-permute-start.8 = (bf16[128,640]{1,0:T(8,128)(2,1)S(1)}, bf16[128,640]{1,0:T(8,128)(2,1)S(1)}, u32[]{:S(2)}, u32[]{:S(2)}) collective-permute-start(bf16[128,640]{1,0:T(8,128)(2,1)S(1)} %get-tuple-element.24), channel_id=1, source_target_pairs={{0,192},{64,0},{128,64},{192,128},{1,193},{65,1},{129,65},{193,129... | collective-permute-start | bytes 491528 | tf_op jit(solution)/shard_map/ppermute | solution.py:388
  117.1 5.8 %collective-permute-start.7 = (bf16[128,640]{1,0:T(8,128)(2,1)S(1)}, bf16[128,640]{1,0:T(8,128)(2,1)S(1)}, u32[]{:S(2)}, u32[]{:S(2)}) collective-permute-start(bf16[128,640]{1,0:T(8,128)(2,1)S(1)} %get-tuple-element.23), channel_id=1, source_target_pairs={{0,128},{64,192},{128,0},{192,64},{1,129},{65,193},{129,1},{193,65... | collective-permute-start | bytes 491528 | tf_op jit(solution)/shard_map/ppermute | solution.py:388
  117.4 10.0 %collective-permute-start.6 = (bf16[128,640]{1,0:T(8,128)(2,1)S(1)}, bf16[128,640]{1,0:T(8,128)(2,1)S(1)}, u32[]{:S(2)}, u32[]{:S(2)}) collective-permute-start(bf16[128,640]{1,0:T(8,128)(2,1)S(1)} %get-tuple-element.22), channel_id=1, source_target_pairs={{0,64},{64,128},{128,192},{192,0},{1,65},{65,129},{129,193},{193,1... | collective-permute-start | bytes 491528 | tf_op jit(solution)/shard_map/ppermute | solution.py:388

commit v9 on v8

--- a/solution.py
+++ b/solution.py
@@ -90,12 +90,9 @@
     steps = 4
     return pl.pallas_call(
         payload_kernel,
-        grid_spec=pltpu.PrefetchScalarGridSpec(
-            num_scalar_prefetch=1,
-            grid=(steps,),
-            in_specs=[pl.BlockSpec(blocks.shape, lambda i, w: (0, 0, 0))],
-            out_specs=pl.BlockSpec((tiles // steps, PACK, DV), lambda i, w: (i, 0, 0)),
-        ),
+        grid=(steps,),
+        in_specs=[pl.BlockSpec(memory_space=pltpu.SMEM), pl.BlockSpec(blocks.shape, lambda i: (0, 0, 0))],
+        out_specs=pl.BlockSpec((tiles // steps, PACK, DV), lambda i: (i, 0, 0)),
         out_shape=jax.ShapeDtypeStruct((tiles, PACK, DV), blocks.dtype),
         cost_estimate=pl.CostEstimate(flops=0, bytes_accessed=2 * tiles * PACK * DV * 2, transcendentals=0),
         compiler_params=pltpu.CompilerParams(vmem_limit_bytes=16 << 20),

time: 129 us -> 129 us (level)
  no operation moved by 1% of the time
where the time goes in v9:
time: 129 us; the launch traced here: 128 us
  waiting for transfers between devices  51.8 us (40%)
  Pallas kernels  37.6 us (29%)
  starting transfers between devices  34.5 us (27%)
  local copies, waits for them, and re-layouts  2 us (2%)
    pallas_call x2, Pallas kernels, coarse_half(): pl.pallas_call(coarse_kernel, grid_spec=pltpu.PrefetchScalarGridSpec(num_...  24.8 us
    all_to_all x1, waiting for transfers between devices, shards(): incoming = lax.all_to_all(payload(wanted, blocks), 'seq', 0, 0, tiled=True)  24 us
    all_to_all x1, waiting for transfers between devices, shards(): lax.all_to_all(letters(own_list, coarse_keys, coarse_values), 'seq', 0, 0...  10.9 us
    ppermute x6, starting transfers between devices, shifted(): lax.ppermute(x, 'seq', [(index(*s), index(s[0], s[1] + dx, s[2] + dc)) fo...  9.47 us
    ppermute x3, waiting for transfers between devices, shards(): own = own + lax.ppermute(part, 'grp', perm).astype(jnp.float32)  9.27 us
    all_to_all x1, starting transfers between devices, shards(): lax.all_to_all(letters(own_list, coarse_keys, coarse_values), 'seq', 0, 0...  9.15 us
    pallas_call x1, Pallas kernels, tail(): pl.pallas_call(functools.partial(tail_kernel, n_grp), grid_spec=pltpu.Pre...  8.43 us
    ppermute x6, waiting for transfers between devices, shifted(): lax.ppermute(x, 'seq', [(index(*s), index(s[0], s[1] + dx, s[2] + dc)) fo...  7.68 us
  transfers between devices with their start and end apart: 12, of which 7 were waited for; matrix products, arithmetic and copies ran while one was open for 2% of the time, Pallas kernels for 21%

profile of v9, /device:TPU:1, one launch (start us, length us, event | category | flops | bytes accessed | tf_op | source)
XLA Modules:
  0.0 128.1 jit_solution(1327550367675479494)
XLA Ops:
  0.0 1.7 %letters.1 = bf16[8,168,128]{2,1,0:T(8,128)(2,1)} custom-call(s32[16]{0:T(128)} %bitcast.28, bf16[1,64,192]{2,1,0:T(8,128)(2,1)} %keys_ref.1, bf16[1,64,128]{2,1,0:T(8,128)(2,1)} %values_ref.1), custom_call_target="tpu_custom_call" | custom-call | bytes 344064 | tf_op jit(solution)/shard_map/letters/pallas_call | solution.py:67
  1.7 9.1 %all-to-all-start = ((bf16[8,168,128]{2,1,0:T(8,128)(2,1)}), bf16[8,168,128]{2,1,0:T(8,128)(2,1)}, u32[]{:S(2)}, u32[]{:S(2)}) async-start(bf16[8,168,128]{2,1,0:T(8,128)(2,1)} %letters.1), calls=%async_computation | async-start | bytes 688128 | tf_op jit(solution)/shard_map/all_to_all | solution.py:349
  10.8 1.0 collective-permute-start.3
  11.8 0.2 copy.13
  12.3 0.1 maximum_maximum_fusion.blocks_ref
  12.4 10.9 %all-to-all-done.rest_0_ = bf16[8,168,128]{2,1,0:T(8,128)(2,1)} async-done(((bf16[8,168,128]{2,1,0:T(8,128)(2,1)}), bf16[8,168,128]{2,1,0:T(8,128)(2,1)}, u32[]{:S(2)}, u32[]{:S(2)}) %all-to-all-start) | async-done | bytes 344096 | tf_op jit(solution)/shard_map/all_to_all | solution.py:349
  23.3 0.7 slice.16
  24.0 0.7 fusion.3
  24.7 6.5 %all-to-all-start.1 = ((s32[8,1,8]{2,1,0:T(1,128)}), s32[8,1,8]{2,1,0:T(1,128)S(1)}, u32[]{:S(2)}, u32[]{:S(2)}) async-start(s32[8,1,8]{2,1,0:T(1,128)} %bitcast.5), calls=%async_computation.1 | async-start | bytes 8192 | tf_op jit(solution)/shard_map/all_to_all | solution.py:360
  31.2 1.4 %collective-permute-start = (bf16[8,168,128]{2,1,0:T(8,128)(2,1)}, bf16[8,168,128]{2,1,0:T(8,128)(2,1)}, u32[]{:S(2)}, u32[]{:S(2)}) collective-permute-start(bf16[8,168,128]{2,1,0:T(8,128)(2,1)} %all-to-all-done.rest_0_), channel_id=1, source_target_pairs={{0,2},{1,3},{2,4},{3,5},{4,6},{5,7},{6,0},{7,1},{8,10},{9,11},{10,... | collective-permute-start | bytes 1032200 | tf_op jit(solution)/shard_map/ppermute | solution.py:48
  32.6 2.4 %collective-permute-start.1 = (bf16[8,168,128]{2,1,0:T(8,128)(2,1)}, bf16[8,168,128]{2,1,0:T(8,128)(2,1)}, u32[]{:S(2)}, u32[]{:S(2)}) collective-permute-start(bf16[8,168,128]{2,1,0:T(8,128)(2,1)} %all-to-all-done.rest_0_), channel_id=1, source_target_pairs={{0,4},{1,5},{2,6},{3,7},{4,0},{5,1},{6,2},{7,3},{8,12},{9,13},{10,... | collective-permute-start | bytes 1032200 | tf_op jit(solution)/shard_map/ppermute | solution.py:48
  35.0 1.2 collective-permute-start.2
  36.2 2.6 %payload.1 = bf16[64,160,128]{2,1,0:T(8,128)(2,1)} custom-call(s32[8,1,8]{2,1,0:T(1,128)S(1)} %all-to-all-done.1.wanted_ref, bf16[16,160,128]{2,1,0:T(8,128)(2,1)S(1)} %maximum_maximum_fusion.blocks_ref), custom_call_target="tpu_custom_call" | custom-call | bytes 5242880 | tf_op jit(solution)/shard_map/payload/pallas_call | solution.py:91
  38.8 5.5 %all-to-all-start.2 = ((bf16[64,160,128]{2,1,0:T(8,128)(2,1)}), bf16[64,160,128]{2,1,0:T(8,128)(2,1)S(1)}, u32[]{:S(2)}, u32[]{:S(2)}) async-start(bf16[64,160,128]{2,1,0:T(8,128)(2,1)} %payload.1), calls=%async_computation.2 | async-start | bytes 5242880 | tf_op jit(solution)/shard_map/all_to_all | solution.py:366
  44.3 0.1 pad_add_fusion.info_ref
  44.4 0.3 fusion.2
  44.8 6.2 %collective-permute-done.1.rest_2_ = bf16[8,168,128]{2,1,0:T(8,128)(2,1)} collective-permute-done((bf16[8,168,128]{2,1,0:T(8,128)(2,1)}, bf16[8,168,128]{2,1,0:T(8,128)(2,1)}, u32[]{:S(2)}, u32[]{:S(2)}) %collective-permute-start.1) | collective-permute-done | bytes 344096 | tf_op jit(solution)/shard_map/ppermute | solution.py:48
  51.0 1.5 %collective-permute-done.2.rest_3_ = bf16[8,168,128]{2,1,0:T(8,128)(2,1)} collective-permute-done((bf16[8,168,128]{2,1,0:T(8,128)(2,1)}, bf16[8,168,128]{2,1,0:T(8,128)(2,1)}, u32[]{:S(2)}, u32[]{:S(2)}) %collective-permute-start.2) | collective-permute-done | bytes 344096 | tf_op jit(solution)/shard_map/ppermute | solution.py:48
  52.5 12.5 %coarse.3 = (bf16[16,128,128]{2,1,0:T(8,128)(2,1)S(1)}, f32[16,1,128]{2,1,0:T(1,128)S(1)}) custom-call(s32[3]{0:T(128)S(1)} %add_add_fusion.1.info_ref, bf16[8,168,128]{2,1,0:T(8,128)(2,1)} %all-to-all-done.rest_0_, bf16[8,168,128]{2,1,0:T(8,128)(2,1)} %collective-permute-done.rest_1_, bf16[8,168,128]{2,1,0:T(8,128)(2,1)} %collective-permute-done.1.rest_2_, ...), custom_call_target="tpu_custom_call" | custom-call | flops 25823150080 | bytes 3145728 | tf_op jit(solution)/shard_map/coarse/pallas_call | solution.py:158
  65.0 3.3 %collective-permute-start.4 = (f32[16,1,128]{2,1,0:T(1,128)S(1)}, f32[16,1,128]{2,1,0:T(1,128)S(1)}, u32[]{:S(2)}, u32[]{:S(2)}) collective-permute-start(f32[16,1,128]{2,1,0:T(1,128)S(1)} %get-tuple-element.18), channel_id=1, source_target_pairs={{0,1},{1,0},{2,3},{3,2},{4,5},{5,4},{6,7},{7,6},{8,9},{9,8},{10,11... | collective-permute-start | bytes 24584 | tf_op jit(solution)/shard_map/ppermute | solution.py:48
  68.2 0.3 collective-permute-start.5
  68.5 12.4 %coarse.2 = (f32[16,128,128]{2,1,0:T(8,128)S(1)}, f32[16,1,128]{2,1,0:T(1,128)S(1)}) custom-call(s32[3]{0:T(128)S(1)} %add_add_fusion.info_ref, bf16[8,168,128]{2,1,0:T(8,128)(2,1)} %all-to-all-done.rest_0_, bf16[8,168,128]{2,1,0:T(8,128)(2,1)} %collective-permute-done.rest_1_, bf16[8,168,128]{2,1,0:T(8,128)(2,1)} %collective-permute-done.1.rest_2_, ...), custom_call_target="tpu_custom_call" | custom-call | flops 25823150080 | bytes 3145728 | tf_op jit(solution)/shard_map/coarse/pallas_call | solution.py:158
  80.9 1.0 copy-done.1
  81.8 24.0 %all-to-all-done.2.incoming = bf16[64,160,128]{2,1,0:T(8,128)(2,1)S(1)} async-done(((bf16[64,160,128]{2,1,0:T(8,128)(2,1)}), bf16[64,160,128]{2,1,0:T(8,128)(2,1)S(1)}, u32[]{:S(2)}, u32[]{:S(2)}) %all-to-all-start.2) | async-done | bytes 2621472 | tf_op jit(solution)/shard_map/all_to_all | solution.py:366
  105.8 8.4 %tail.1 = (f32[128,640]{1,0:T(8,128)S(1)}, bf16[128,640]{1,0:T(8,128)(2,1)S(1)}, bf16[128,640]{1,0:T(8,128)(2,1)S(1)}, bf16[128,640]{1,0:T(8,128)(2,1)S(1)}) custom-call(s32[19]{0:T(128)S(1)} %pad_add_fusion.info_ref, bf16[64,160,128]{2,1,0:T(8,128)(2,1)S(1)} %all-to-all-done.2.incoming, bf16[16,192,128]{2,1,0:T(8,128)(2,1)} %bitcast.22, ...), custom_call_target="tpu_custom_call" | custom-call | flops 2684354560 | bytes 10485760 | tf_op jit(solution)/shard_map/tail/pallas_call | solution.py:275
  114.3 2.8 %collective-permute-start.8 = (bf16[128,640]{1,0:T(8,128)(2,1)S(1)}, bf16[128,640]{1,0:T(8,128)(2,1)S(1)}, u32[]{:S(2)}, u32[]{:S(2)}) collective-permute-start(bf16[128,640]{1,0:T(8,128)(2,1)S(1)} %get-tuple-element.24), channel_id=1, source_target_pairs={{0,192},{64,0},{128,64},{192,128},{1,193},{65,1},{129,65},{193,129... | collective-permute-start | bytes 491528 | tf_op jit(solution)/shard_map/ppermute | solution.py:385
  117.1 0.3 collective-permute-start.7
  117.4 0.7 collective-permute-start.6
  118.1 2.2 %collective-permute-done.8 = bf16[128,640]{1,0:T(8,128)(2,1)S(1)} collective-permute-done((bf16[128,640]{1,0:T(8,128)(2,1)S(1)}, bf16[128,640]{1,0:T(8,128)(2,1)S(1)}, u32[]{:S(2)}, u32[]{:S(2)}) %collective-permute-start.8) | collective-permute-done | bytes 163872 | tf_op jit(solution)/shard_map/ppermute | solution.py:385
  120.3 2.5 %collective-permute-done.7 = bf16[128,640]{1,0:T(8,128)(2,1)S(1)} collective-permute-done((bf16[128,640]{1,0:T(8,128)(2,1)S(1)}, bf16[128,640]{1,0:T(8,128)(2,1)S(1)}, u32[]{:S(2)}, u32[]{:S(2)}) %collective-permute-start.7) | collective-permute-done | bytes 163872 | tf_op jit(solution)/shard_map/ppermute | solution.py:385
  122.9 4.5 %collective-permute-done.6 = bf16[128,640]{1,0:T(8,128)(2,1)S(1)} collective-permute-done((bf16[128,640]{1,0:T(8,128)(2,1)S(1)}, bf16[128,640]{1,0:T(8,128)(2,1)S(1)}, u32[]{:S(2)}, u32[]{:S(2)}) %collective-permute-start.6) | collective-permute-done | bytes 163872 | tf_op jit(solution)/shard_map/ppermute | solution.py:385
  127.4 0.8 add_convert_fusion
  (22 shorter events, 0.3 us)
Async XLA Ops:
  0.0 44.4 %copy-start = (bf16[128,2560]{1,0:T(8,128)(2,1)S(1)}, bf16[128,2560]{1,0:T(8,128)(2,1)}, u32[]{:S(2)}) copy-start(bf16[128,2560]{1,0:T(8,128)(2,1)} %param.14) | copy-start | bytes 1966084
  0.0 11.8 %copy-start.3 = (bf16[1,1024,192]{1,2,0:T(8,128)(2,1)S(1)}, bf16[1,1024,192]{1,2,0:T(8,128)(2,1)}, u32[]{:S(2)}) copy-start(bf16[1,1024,192]{1,2,0:T(8,128)(2,1)} %param.10) | copy-start | bytes 1179652
  1.7 10.6 %copy-start.4 = (bf16[1,1024,128]{2,1,0:T(8,128)(2,1)S(1)}, bf16[1,1024,128]{2,1,0:T(8,128)(2,1)}, u32[]{:S(2)}) copy-start(bf16[1,1024,128]{2,1,0:T(8,128)(2,1)} %param.11) | copy-start | bytes 786436
  1.7 21.6 %all-to-all-start = ((bf16[8,168,128]{2,1,0:T(8,128)(2,1)}), bf16[8,168,128]{2,1,0:T(8,128)(2,1)}, u32[]{:S(2)}, u32[]{:S(2)}) async-start(bf16[8,168,128]{2,1,0:T(8,128)(2,1)} %letters.1), calls=%async_computation | async-start | bytes 688128 | tf_op jit(solution)/shard_map/all_to_all | solution.py:349
  10.8 34.0 %collective-permute-start.3 = (bf16[16,192,128]{2,1,0:T(8,128)(2,1)}, bf16[16,192,128]{2,1,0:T(8,128)(2,1)}, u32[]{:S(2)}, u32[]{:S(2)}) collective-permute-start(bf16[16,192,128]{2,1,0:T(8,128)(2,1)} %bitcast.21), channel_id=1, source_target_pairs={{0,1},{1,0},{2,3},{3,2},{4,5},{5,4},{6,7},{7,6},{8,9},{9,8},{10,11... | collective-permute-start | bytes 2359304 | tf_op jit(solution)/shard_map/ppermute | solution.py:48
  24.7 11.5 %all-to-all-start.1 = ((s32[8,1,8]{2,1,0:T(1,128)}), s32[8,1,8]{2,1,0:T(1,128)S(1)}, u32[]{:S(2)}, u32[]{:S(2)}) async-start(s32[8,1,8]{2,1,0:T(1,128)} %bitcast.5), calls=%async_computation.1 | async-start | bytes 8192 | tf_op jit(solution)/shard_map/all_to_all | solution.py:360
  31.2 13.5 %collective-permute-start = (bf16[8,168,128]{2,1,0:T(8,128)(2,1)}, bf16[8,168,128]{2,1,0:T(8,128)(2,1)}, u32[]{:S(2)}, u32[]{:S(2)}) collective-permute-start(bf16[8,168,128]{2,1,0:T(8,128)(2,1)} %all-to-all-done.rest_0_), channel_id=1, source_target_pairs={{0,2},{1,3},{2,4},{3,5},{4,6},{5,7},{6,0},{7,1},{8,10},{9,11},{10,... | collective-permute-start | bytes 1032200 | tf_op jit(solution)/shard_map/ppermute | solution.py:48
  32.6 18.3 %collective-permute-start.1 = (bf16[8,168,128]{2,1,0:T(8,128)(2,1)}, bf16[8,168,128]{2,1,0:T(8,128)(2,1)}, u32[]{:S(2)}, u32[]{:S(2)}) collective-permute-start(bf16[8,168,128]{2,1,0:T(8,128)(2,1)} %all-to-all-done.rest_0_), channel_id=1, source_target_pairs={{0,4},{1,5},{2,6},{3,7},{4,0},{5,1},{6,2},{7,3},{8,12},{9,13},{10,... | collective-permute-start | bytes 1032200 | tf_op jit(solution)/shard_map/ppermute | solution.py:48
  35.0 17.4 %collective-permute-start.2 = (bf16[8,168,128]{2,1,0:T(8,128)(2,1)}, bf16[8,168,128]{2,1,0:T(8,128)(2,1)}, u32[]{:S(2)}, u32[]{:S(2)}) collective-permute-start(bf16[8,168,128]{2,1,0:T(8,128)(2,1)} %all-to-all-done.rest_0_), channel_id=1, source_target_pairs={{0,6},{1,7},{2,0},{3,1},{4,2},{5,3},{6,4},{7,5},{8,14},{9,15},{10,... | collective-permute-start | bytes 1032200 | tf_op jit(solution)/shard_map/ppermute | solution.py:48
  38.8 5.5 %copy-start.6 = (s32[1,1,16]{2,1,0:T(1,128)S(1)}, s32[1,1,16]{2,1,0:T(1,128)}, u32[]{:S(2)}) copy-start(s32[1,1,16]{2,1,0:T(1,128)} %param.17) | copy-start | bytes 196
  38.8 5.6 %copy-start.5 = (bf16[1,2560,32]{1,2,0:T(8,128)(2,1)S(1)}, bf16[1,2560,32]{1,2,0:T(8,128)(2,1)}, u32[]{:S(2)}) copy-start(bf16[1,2560,32]{1,2,0:T(8,128)(2,1)} %param.15) | copy-start | bytes 491524
  38.8 67.0 %all-to-all-start.2 = ((bf16[64,160,128]{2,1,0:T(8,128)(2,1)}), bf16[64,160,128]{2,1,0:T(8,128)(2,1)S(1)}, u32[]{:S(2)}, u32[]{:S(2)}) async-start(bf16[64,160,128]{2,1,0:T(8,128)(2,1)} %payload.1), calls=%async_computation.2 | async-start | bytes 5242880 | tf_op jit(solution)/shard_map/all_to_all | solution.py:366
  44.8 23.8 %copy-start.2 = (bf16[128,16,192]{0,2,1:T(8,128)(2,1)S(1)}, bf16[128,16,192]{0,2,1:T(8,128)(2,1)}, u32[]{:S(2)}) copy-start(bf16[128,16,192]{0,2,1:T(8,128)(2,1)} %param.9) | copy-start | bytes 2359300
  65.0 16.9 %collective-permute-start.4 = (f32[16,1,128]{2,1,0:T(1,128)S(1)}, f32[16,1,128]{2,1,0:T(1,128)S(1)}, u32[]{:S(2)}, u32[]{:S(2)}) collective-permute-start(f32[16,1,128]{2,1,0:T(1,128)S(1)} %get-tuple-element.18), channel_id=1, source_target_pairs={{0,1},{1,0},{2,3},{3,2},{4,5},{5,4},{6,7},{7,6},{8,9},{9,8},{10,11... | collective-permute-start | bytes 24584 | tf_op jit(solution)/shard_map/ppermute | solution.py:48
  68.2 13.6 %collective-permute-start.5 = (bf16[16,128,128]{2,1,0:T(8,128)(2,1)S(1)}, bf16[16,128,128]{2,1,0:T(8,128)(2,1)}, u32[]{:S(2)}, u32[]{:S(2)}) collective-permute-start(bf16[16,128,128]{2,1,0:T(8,128)(2,1)S(1)} %get-tuple-element.20), channel_id=1, source_target_pairs={{0,1},{1,0},{2,3},{3,2},{4,5},{5,4},{6,7},{7,6},{8,9},{9,8},{10,11... | collective-permute-start | bytes 1572872 | tf_op jit(solution)/shard_map/ppermute | solution.py:48
  80.9 1.0 copy-start.1
  114.3 6.1 %collective-permute-start.8 = (bf16[128,640]{1,0:T(8,128)(2,1)S(1)}, bf16[128,640]{1,0:T(8,128)(2,1)S(1)}, u32[]{:S(2)}, u32[]{:S(2)}) collective-permute-start(bf16[128,640]{1,0:T(8,128)(2,1)S(1)} %get-tuple-element.24), channel_id=1, source_target_pairs={{0,192},{64,0},{128,64},{192,128},{1,193},{65,1},{129,65},{193,129... | collective-permute-start | bytes 491528 | tf_op jit(solution)/shard_map/ppermute | solution.py:385
  117.1 5.8 %collective-permute-start.7 = (bf16[128,640]{1,0:T(8,128)(2,1)S(1)}, bf16[128,640]{1,0:T(8,128)(2,1)S(1)}, u32[]{:S(2)}, u32[]{:S(2)}) collective-permute-start(bf16[128,640]{1,0:T(8,128)(2,1)S(1)} %get-tuple-element.23), channel_id=1, source_target_pairs={{0,128},{64,192},{128,0},{192,64},{1,129},{65,193},{129,1},{193,65... | collective-permute-start | bytes 491528 | tf_op jit(solution)/shard_map/ppermute | solution.py:385
  117.4 10.0 %collective-permute-start.6 = (bf16[128,640]{1,0:T(8,128)(2,1)S(1)}, bf16[128,640]{1,0:T(8,128)(2,1)S(1)}, u32[]{:S(2)}, u32[]{:S(2)}) collective-permute-start(bf16[128,640]{1,0:T(8,128)(2,1)S(1)} %get-tuple-element.22), channel_id=1, source_target_pairs={{0,64},{64,128},{128,192},{192,0},{1,65},{65,129},{129,193},{193,1... | collective-permute-start | bytes 491528 | tf_op jit(solution)/shard_map/ppermute | solution.py:385
